TPU v7x, 128 devices: a whole 4x4x4 slice. The times are simulated.
128 devices in a mesh: mic: 16 (over z, y), mode: 8 (over x, core).
Axes of the slice: x: 4, y: 4, z: 4, core: 2. Of those that a mesh axis runs over, the one named last changes fastest.
Arguments:
- signal: bfloat16 [16, 4096, 4096], P('mic', 'mode'), may hold values from -6 to 6
- mic_axial: int32 [4096], P('mic'), may hold values from 0 to 63
- mic_azimuth: int32 [4096], P('mic'), may hold values from 0 to 511
- mode_m: int32 [8192], P('mode'), may hold values from -128 to 127
- mode_n: int32 [8192], P('mode'), may hold values from 0 to 31
- freq_bins: int32 [16], replicated, may hold values from 1 to 1023
Outputs:
- amplitude: float32 [16, 2, 16, 8192], P(None, None, None, 'mode')
- power: float32 [16, 8192], P(None, 'mode')
- residual: float32 [16, 2, 16, 4096], P('mode', None, None, 'mic')
All inputs are finite; a program needn't handle non-finite values.
Results may differ from a plain program's by a relative error of at most 0.0051.
Values may be sent and summed in bfloat16 or wider, within the bound.
No kernel may reach another device: no remote copies, remote signals or barrier semaphores. Data moves between devices by JAX's collectives and lax.ppermute only.
A program may use at most 64 MiB of HBM per device.

v0:
```python
import math

import jax
import jax.numpy as jnp
from jax import lax
from jax.sharding import PartitionSpec as P

ITERS = 2
AZIM = 512
AXIAL = 64
NRAD = 32


EPS = 1e-06


def analysis_rows(freq_bins, seglen):
    sample_index = jnp.arange(seglen, dtype=jnp.int32)
    phase_turns = jnp.mod(freq_bins[:, None] * sample_index[None, :], seglen)
    phase_angle = phase_turns.astype(jnp.float32) * (2.0 * math.pi / seglen)
    window = 0.5 - 0.5 * jnp.cos(sample_index.astype(jnp.float32) * (2.0 * math.pi / seglen))
    norm_scale = (3.0 * seglen / 8.0) ** (-0.5)
    cosine = window[None, :] * jnp.cos(phase_angle) * norm_scale
    sine = -window[None, :] * jnp.sin(phase_angle) * norm_scale
    stacked = jnp.stack([cosine, sine], axis=1)
    return stacked.reshape(2 * freq_bins.shape[0], seglen).astype(jnp.bfloat16)


def mode_tile(bin_value, mic_axial, mic_azimuth, mode_m, mode_n, norm_scale):
    period = AZIM * AXIAL
    phase_turns = jnp.mod(
        mic_azimuth[:, None] * (mode_m * AXIAL)[None, :]
        + mic_axial[:, None] * (bin_value * (2 * NRAD - mode_n))[None, :],
        period,
    )
    phase_angle = phase_turns.astype(jnp.float32) * (2.0 * math.pi / period)
    weight = norm_scale / jnp.sqrt(1.0 + mode_n.astype(jnp.float32))
    real_part = (weight[None, :] * jnp.cos(phase_angle)).astype(jnp.bfloat16)
    imag_part = (weight[None, :] * jnp.sin(phase_angle)).astype(jnp.bfloat16)
    return (real_part, imag_part)


def forward_product(real_part, imag_part, vector):
    segs = vector.shape[1]
    stacked = vector.reshape(2 * segs, vector.shape[2]).astype(jnp.bfloat16)
    dims = (((1,), (1,)), ((), ()))
    first = lax.dot_general(stacked, real_part, dims, preferred_element_type=jnp.float32)
    second = lax.dot_general(stacked, imag_part, dims, preferred_element_type=jnp.float32)
    return jnp.stack([first[:segs] - second[segs:], first[segs:] + second[:segs]])


def adjoint_product(real_part, imag_part, vector):
    segs = vector.shape[1]
    stacked = vector.reshape(2 * segs, vector.shape[2])
    first = jnp.dot(stacked, real_part, preferred_element_type=jnp.float32)
    second = jnp.dot(stacked, imag_part, preferred_element_type=jnp.float32)
    return jnp.stack([first[:segs] + second[segs:], first[segs:] - second[:segs]])


def on_device(signal, mic_axial, mic_azimuth, mode_m, mode_n, freq_bins):
    seglen = signal.shape[2]
    freqs = freq_bins.shape[0]
    total_mics = mic_axial.shape[0] * lax.axis_size("mic")
    norm_scale = total_mics ** (-0.5)
    analysis = analysis_rows(freq_bins, seglen)
    spectra = lax.dot_general(
        analysis, signal, (((1,), (2,)), ((), ())), preferred_element_type=jnp.float32
    )
    spectra = spectra.reshape(freqs, 2, signal.shape[0], signal.shape[1])
    rhs = lax.all_to_all(
        lax.all_to_all(spectra, "mode", split_axis=0, concat_axis=3, tiled=True),
        "mic",
        split_axis=3,
        concat_axis=2,
        tiled=True,
    )
    freq_rows = rhs.shape[0]
    row_offset = lax.axis_index("mode") * freq_rows

    def tile_for(freq_row):
        bin_value = lax.dynamic_index_in_dim(freq_bins, freq_row, 0, keepdims=False)
        return mode_tile(bin_value, mic_axial, mic_azimuth, mode_m, mode_n, norm_scale)

    def gradients(residual_rows):

        def gradients_single(item):
            freq_row, vector = item
            real_part, imag_part = tile_for(freq_row)
            return adjoint_product(real_part, imag_part, vector)

        row_index = jnp.arange(residual_rows.shape[0], dtype=jnp.int32)
        return lax.map(gradients_single, (row_index, residual_rows))

    def gradient_of(residual):
        rounded = residual.astype(jnp.bfloat16)
        partial_sum = gradients(lax.all_gather(rounded, "mode", axis=0, tiled=True))
        gradient = lax.psum(partial_sum, "mic")
        grad_norm = lax.psum(jnp.sum(gradient * gradient, axis=(1, 3)), "mode")
        return (gradient, grad_norm)

    residual = rhs
    gradient, grad_norm = gradient_of(residual)
    direction = gradient
    amplitude = jnp.zeros_like(direction)
    for sweep in range(ITERS):

        def images_single(freq_row):
            real_part, imag_part = tile_for(freq_row)
            vector = lax.dynamic_index_in_dim(direction, freq_row, 0, keepdims=False)
            return forward_product(real_part, imag_part, vector)

        image = lax.psum_scatter(
            lax.map(images_single, jnp.arange(freq_rows * lax.axis_size("mode"), dtype=jnp.int32)),
            "mode",
            scatter_dimension=0,
            tiled=True,
        )
        local_norm = jnp.sum(image * image, axis=(1, 3))
        padded = lax.dynamic_update_slice(
            jnp.zeros((freqs, local_norm.shape[1]), jnp.float32),
            local_norm,
            (row_offset, jnp.zeros((), jnp.int32)),
        )
        image_norm = lax.psum(padded, ("mic", "mode"))
        step_size = grad_norm / (image_norm + EPS)
        row_steps = lax.dynamic_slice_in_dim(step_size, row_offset, freq_rows, 0)
        residual = residual - row_steps[:, None, :, None] * image
        amplitude = amplitude + step_size[:, None, :, None] * direction
        if sweep + 1 < ITERS:
            gradient, next_norm = gradient_of(residual)
            momentum = next_norm / (grad_norm + EPS)
            direction = gradient + momentum[:, None, :, None] * direction
            grad_norm = next_norm
    power = jnp.mean(jnp.sum(amplitude * amplitude, axis=1), axis=1)
    return (amplitude, power, residual)


def solution(mesh):
    in_specs = (P("mic", "mode", None), P("mic"), P("mic"), P("mode"), P("mode"), P())
    out_specs = (P(None, None, None, "mode"), P(None, "mode"), P("mode", None, None, "mic"))
    return jax.shard_map(
        on_device, mesh=mesh, in_specs=in_specs, out_specs=out_specs, check_vma=False
    )
```

profile of v0, /device:TPU:1, one launch (start us, length us, event | category | flops | bytes accessed | tf_op | source)
XLA Modules:
  0.0 1280.7 jit_solution(2784293578209869933)
XLA Ops:
  12.8 10.4 all_to_all.30
  26.3 8.1 reshape.310
  34.5 7.8 all-to-all-start.1
  42.3 6.4 all-to-all-done.1
  50.1 7.7 reshape.311
  61.4 15.1 %all_gather.6 = bf16[16,2,16,256]{3,2,1,0:T(8,128)(2,1)S(1)} all-gather(bf16[2,2,16,256]{3,2,1,0:T(8,128)(2,1)S(1)} %convert_element_type.147), channel_id=1, replica_groups=mesh['mic'=16,'mode'=8] {'mode'}, dimensions={0}, use_global_device_ids=true | all-gather | bytes 294912 | tf_op jit(solution)/shard_map/all_gather | solution.py:96
  76.8 193.2 %while.48 = (s32[]{:T(128)}, f32[16,2,16,1024]{3,2,1,0:T(8,128)S(1)}, bf16[16,2,16,256]{3,2,1,0:T(8,128)(2,1)S(1)}, f32[1,1024]{1,0:T(1,128)S(1)}, s32[256]{0:T(...) while((s32[]{:T(128)}, ...), condition=%wide.region_1.2_spmd, body=%wide.region_0.1_spmd.sunk | while | flops 43062276 | bytes 1036483 | solution.py:92
  84.7 4.1 fusion.116
  96.8 4.1 fusion.116
  108.8 4.1 fusion.116
  120.9 4.1 fusion.116
  133.0 4.1 fusion.116
  145.1 4.1 fusion.116
  157.2 4.1 fusion.116
  169.2 4.1 fusion.116
  181.3 4.1 fusion.116
  193.4 4.1 fusion.116
  205.5 4.1 fusion.116
  217.5 4.1 fusion.116
  229.6 4.1 fusion.116
  241.7 4.1 fusion.116
  253.8 4.1 fusion.116
  265.9 4.1 fusion.116
  271.7 85.4 %all-reduce.3.cloned.1.call-done = f32[16,2,16,1024]{3,2,1,0:T(8,128)} async-done(((f32[16,2,16,1024]{3,2,1,0:T(8,128)}), f32[16,2,16,1024]{3,2,1,0:T(8,128)}) %all-reduce.3.cloned.1.call-update) | async-done | bytes 2097168 | tf_op jit(solution)/shard_map/psum | solution.py:97
  359.7 193.1 %while.49 = (s32[]{:T(128)}, f32[16,2,16,256]{3,2,1,0:T(8,128)S(1)}, s32[16]{0:T(128)S(1)}, bf16[16,2,16,1024]{3,2,1,0:T(8,128)(2,1)S(1)}, f32[1,1024]{1,0:T(1,1...) while((s32[]{:T(128)}, ...), condition=%wide.region_6.7_spmd, body=%wide.region_5.6_spmd.sunk | while | flops 43013124 | bytes 544963 | solution.py:113
  553.7 14.1 %psum.43 = f32[16,16]{1,0:T(8,128)S(1)} all-reduce(f32[16,16]{1,0:T(8,128)S(1)} %get-tuple-element.587), channel_id=1, replica_groups=mesh['mic'=16,'mode'=8] {'mode'}, use_global_device_ids=true, to_apply=%region_4.5 | all-reduce | flops 256 | bytes 2048 | tf_op jit(solution)/shard_map/psum | solution.py:98
  567.8 15.4 %reduce-scatter.3.cloned.1.call-done = f32[2,2,16,256]{3,2,1,0:T(8,128)} async-done(((f32[16,2,16,256]{3,2,1,0:T(8,128)}), f32[2,2,16,256]{3,2,1,0:T(8,128)}) %reduce-scatter.3.cloned.1.call-update) | async-done | bytes 65552 | tf_op jit(solution)/shard_map/reduce_scatter | solution.py:112
  584.2 67.6 %psum.44 = f32[16,16]{1,0:T(8,128)S(1)} all-reduce(f32[16,16]{1,0:T(8,128)S(1)} %constant_dynamic-update-slice_fusion.1), channel_id=1, replica_groups=mesh['mic'=16,'mode'=8] {'mic','mode'}, use_global_device_ids=true, to_apply=%region_9.10 | all-reduce | flops 256 | bytes 2048 | tf_op jit(solution)/shard_map/psum | solution.py:124
  652.7 14.0 %all_gather.7 = bf16[16,2,16,256]{3,2,1,0:T(8,128)(2,1)S(1)} all-gather(bf16[2,2,16,256]{3,2,1,0:T(8,128)(2,1)S(1)} %fusion.78), channel_id=1, replica_groups=mesh['mic'=16,'mode'=8] {'mode'}, dimensions={0}, use_global_device_ids=true | all-gather | bytes 294912 | tf_op jit(solution)/shard_map/all_gather | solution.py:96
  667.0 193.2 %while.50 = (s32[]{:T(128)}, f32[16,2,16,1024]{3,2,1,0:T(8,128)S(1)}, bf16[16,2,16,256]{3,2,1,0:T(8,128)(2,1)S(1)}, f32[1,1024]{1,0:T(1,128)S(1)}, s32[256]{0:T(...) while((s32[]{:T(128)}, ...), condition=%wide.region_11.12_spmd, body=%wide.region_10.11_spmd.sunk | while | flops 43062276 | bytes 1036483 | solution.py:92
  674.9 4.1 fusion.128
  686.9 4.1 fusion.128
  699.0 4.1 fusion.128
  711.1 4.1 fusion.128
  723.2 4.1 fusion.128
  735.3 4.1 fusion.128
  747.3 4.1 fusion.128
  759.4 4.1 fusion.128
  771.5 4.1 fusion.128
  783.6 4.1 fusion.128
  795.6 4.1 fusion.128
  807.7 4.1 fusion.128
  819.8 4.1 fusion.128
  831.9 4.1 fusion.128
  844.0 4.1 fusion.128
  856.0 4.1 fusion.128
  861.6 86.1 %all-reduce.5.cloned.1.call-done = f32[16,2,16,1024]{3,2,1,0:T(8,128)} async-done(((f32[16,2,16,1024]{3,2,1,0:T(8,128)}), f32[16,2,16,1024]{3,2,1,0:T(8,128)}) %all-reduce.5.cloned.1.call-update) | async-done | bytes 2097168 | tf_op jit(solution)/shard_map/psum | solution.py:97
  949.5 14.2 %psum.46 = f32[16,16]{1,0:T(8,128)S(1)} all-reduce(f32[16,16]{1,0:T(8,128)S(1)} %multiply_reduce_fusion.1), channel_id=1, replica_groups=mesh['mic'=16,'mode'=8] {'mode'}, use_global_device_ids=true, to_apply=%region_14.15 | all-reduce | flops 256 | bytes 2048 | tf_op jit(solution)/shard_map/psum | solution.py:98
  967.4 206.3 %while.51 = (s32[]{:T(128)}, f32[16,2,16,256]{3,2,1,0:T(8,128)S(1)}, s32[16]{0:T(128)S(1)}, bf16[16,2,16,1024]{3,2,1,0:T(8,128)(2,1)}, f32[1,1024]{1,0:T(1,128)S...) while((s32[]{:T(128)}, ...), condition=%wide.region_16.17_spmd, body=%wide.region_15.16_spmd.sunk | while | flops 43013124 | bytes 544963 | solution.py:113
  976.1 4.1 fusion.134
  989.0 4.1 fusion.134
  1001.9 4.1 fusion.134
  1014.8 4.1 fusion.134
  1027.7 4.1 fusion.134
  1040.6 4.1 fusion.134
  1053.5 4.1 fusion.134
  1066.4 4.1 fusion.134
  1079.3 4.1 fusion.134
  1092.2 4.1 fusion.134
  1105.1 4.1 fusion.134
  1118.0 4.1 fusion.134
  1156.7 4.1 fusion.134
  1174.5 26.1 %reduce-scatter.5.cloned.1.call-done = f32[2,2,16,256]{3,2,1,0:T(8,128)} async-done(((f32[16,2,16,256]{3,2,1,0:T(8,128)}), f32[2,2,16,256]{3,2,1,0:T(8,128)}) %reduce-scatter.5.cloned.1.call-update) | async-done | bytes 65552 | tf_op jit(solution)/shard_map/reduce_scatter | solution.py:112
  1201.6 67.6 %psum.47 = f32[16,16]{1,0:T(8,128)S(1)} all-reduce(f32[16,16]{1,0:T(8,128)S(1)} %constant_dynamic-update-slice_fusion), channel_id=1, replica_groups=mesh['mic'=16,'mode'=8] {'mic','mode'}, use_global_device_ids=true, to_apply=%region_19.20 | all-reduce | flops 256 | bytes 2048 | tf_op jit(solution)/shard_map/psum | solution.py:124
  (600 shorter events, 506.8 us)
Async XLA Ops:
  26.3 16.0 %copy-start.5 = (s32[1024]{0:T(1024)S(1)}, s32[1024]{0:T(1024)}, u32[]{:S(2)}) copy-start(s32[1024]{0:T(1024)} %param.18) | copy-start | bytes 12292
  34.5 14.3 %all-to-all-start.1 = ((f32[16,1,1024]{2,1,0:T(1,128)}), f32[16,1,1024]{2,1,0:T(1,128)S(1)}, u32[]{:S(2)}, u32[]{:S(2)}) async-start(f32[16,1,1024]{2,1,0:T(1,128)} %reshape.310), calls=%async_computation.1 | async-start | bytes 131072 | tf_op jit(solution)/shard_map/all_to_all | solution.py:70
  42.2 314.9 %all-reduce.3.cloned.1.call-start = ((), (), s32[]{:S(2)}) async-start(), calls=%async_computation.4 | async-start | bytes 4194304 | tf_op jit(solution)/shard_map/psum | solution.py:97
  61.3 15.4 %copy-start.6 = (s32[1024]{0:T(1024)S(1)}, s32[1024]{0:T(1024)}, u32[]{:S(2)}) copy-start(s32[1024]{0:T(1024)} %param.17) | copy-start | bytes 12292
  61.4 15.4 %copy-start.9 = (s32[16]{0:T(128)S(1)}, s32[16]{0:T(128)}, u32[]{:S(2)}) copy-start(s32[16]{0:T(128)} %param.19) | copy-start | bytes 196
  61.4 15.4 %copy-start.10 = (s32[256]{0:T(256)S(1)}, s32[256]{0:T(256)}, u32[]{:S(2)}) copy-start(s32[256]{0:T(256)} %param.16) | copy-start | bytes 3076
  61.4 15.4 %copy-start.11 = (s32[256]{0:T(256)S(1)}, s32[256]{0:T(256)}, u32[]{:S(2)}) copy-start(s32[256]{0:T(256)} %param.15) | copy-start | bytes 3076
  270.0 1.3 copy-start.1
  271.4 311.8 %reduce-scatter.3.cloned.1.call-start = ((), (), s32[]{:S(2)}) async-start(), calls=%async_computation.5 | async-start | bytes 589824 | tf_op jit(solution)/shard_map/reduce_scatter | solution.py:112
  552.8 0.8 copy-start.3
  553.6 394.1 %all-reduce.5.cloned.1.call-start = ((), (), s32[]{:S(2)}) async-start(), calls=%async_computation.6 | async-start | bytes 4194304 | tf_op jit(solution)/shard_map/psum | solution.py:97
  860.2 1.3 copy-start.2
  861.5 102.2 %copy-start = (f32[16,2,16,1024]{3,2,1,0:T(8,128)S(1)}, f32[16,2,16,1024]{3,2,1,0:T(8,128)}, u32[]{:S(2)}) copy-start(f32[16,2,16,1024]{3,2,1,0:T(8,128)} %all-reduce.3.cloned.1.call-done) | copy-start | bytes 6291460
  861.6 339.1 %reduce-scatter.5.cloned.1.call-start = ((), (), s32[]{:S(2)}) async-start(), calls=%async_computation.7 | async-start | bytes 589824 | tf_op jit(solution)/shard_map/reduce_scatter | solution.py:112
  1173.7 0.8 copy-start.4
  1269.1 4.2 copy-start.7
  1269.1 4.2 copy-start.8
Sparse Core Ops, SparseCore 0:
  271.5 85.5 all-reduce.2
  553.8 29.4 reduce-scatter.2
  861.7 85.9 all-reduce.4
  1174.7 25.9 reduce-scatter.4
where the time goes:
time: 1290 us; the launch traced here: 1280 us
  matrix products  528 us (41%)
  waiting for transfers between devices  219 us (17%)
  blocking collectives  203 us (16%)
  loops' own time  128 us (10%)
  local copies, waits for them, and re-layouts  117 us (9%)
  other arithmetic  62.5 us (5%)
  between operations  14.3 us (1%)
    psum x2, waiting for transfers between devices, gradient_of(): gradient = lax.psum(partial_sum, 'mic')  171 us
    psum x2, blocking collectives, on_device(): image_norm = lax.psum(padded, ('mic', 'mode'))  135 us
    dot_general x32, matrix products, adjoint_product(): second = jnp.dot(stacked, imag_part, preferred_element_type=jnp.float32)  132 us
    dot_general x32, matrix products, forward_product(): lax.dot_general(stacked, imag_part, dims, preferred_element_type=jnp.floa...  132 us
    dot_general x32, matrix products, adjoint_product(): first = jnp.dot(stacked, real_part, preferred_element_type=jnp.float32)  130 us
    dot_general x32, matrix products, forward_product(): lax.dot_general(stacked, real_part, dims, preferred_element_type=jnp.floa...  130 us
    another operation x2, loops' own time, on_device(): lax.map(images_single, jnp.arange(freq_rows * lax.axis_size('mode'), dtyp...  64.3 us
    another operation x2, loops' own time, gradients(): return lax.map(gradients_single, (row_index, residual_rows))  64 us
  transfers between devices with their start and end apart: 5, of which 5 were waited for; matrix products, arithmetic and copies ran while one was open for 0% of the time, Pallas kernels for 0%

commit v1 on v0

v1 whole, which is shorter than its diff:
```python
import math

import jax
import jax.numpy as jnp
from jax import lax
from jax.experimental import pallas as pl
from jax.experimental.pallas import tpu as pltpu
from jax.sharding import PartitionSpec as P

ITERS = 2
AZIM = 512
AXIAL = 64
NRAD = 32
ORDERS = 256
EPS = 1e-06
SIN_COEFS = (1.5707963200919937, -0.6459637612912833, 0.07968992686556589, -0.0046741574942986315, 0.0001516785309118288)
BF16 = jnp.bfloat16
F32 = jnp.float32


def cos_turns(phase, bits):
    half = 1 << (bits - 1)
    quarter = 1 << (bits - 2)
    centred = ((phase + half) & (2 * half - 1)) - half
    y = (quarter - jnp.abs(centred)).astype(F32) * (1.0 / quarter)
    square = y * y
    total = jnp.full_like(y, SIN_COEFS[-1])
    for coef in SIN_COEFS[-2::-1]:
        total = total * square + coef
    return total * y


def sin_turns(phase, bits):
    return cos_turns(phase - (1 << (bits - 2)), bits)


def iota(shape, axis):
    return lax.broadcasted_iota(jnp.int32, shape, axis)


def nt_dot(a, b):
    return lax.dot_general(a, b, (((1,), (1,)), ((), ())), preferred_element_type=F32)


def spectra_kernel(freq_ref, m_lo_ref, m_hi_ref, n_lo_ref, n_hi_ref, signal_ref, out_ref, analysis_ref):
    rows, seglen = analysis_ref.shape
    freqs = rows // 2

    @pl.when(pl.program_id(0) == 0)
    def _():
        row = iota((rows, 128), 0)
        column = jnp.zeros((rows, 128), jnp.int32)
        for f in range(freqs):
            column = jnp.where((row >> 1) == f, freq_ref[f], column)
        quarter = (row & 1) * (seglen // 4)
        bits = seglen.bit_length() - 1
        scale = (3.0 * seglen / 8.0) ** (-0.5)
        for block in range(seglen // 128):
            sample = iota((rows, 128), 1) + block * 128
            wave = cos_turns(column * sample + quarter, bits)
            window = 0.5 - 0.5 * cos_turns(iota((8, 128), 1) + block * 128, bits)[:1]
            analysis_ref[:, block * 128 : (block + 1) * 128] = (window * wave * scale).astype(BF16)

    spectra = nt_dot(analysis_ref[...], signal_ref[...])
    per = rows // out_ref.shape[0]
    for d in range(out_ref.shape[0]):
        out_ref[d, 0:per, :] = spectra[d * per : (d + 1) * per]
    codes = []
    for m_ref, n_ref in ((m_lo_ref, n_lo_ref), (m_hi_ref, n_hi_ref)):
        m = m_ref[...]
        codes.append((jnp.where(m >= 0, m, ORDERS // 2 - 1 - m) * NRAD + n_ref[...]).astype(F32))
    for d in range(out_ref.shape[0]):
        out_ref[d, per : per + 1, :] = codes[0]
        out_ref[d, per + 1 : per + 2, :] = codes[1]
        out_ref[d, per + 2 :, :] = jnp.zeros((out_ref.shape[1] - per - 2, 128), F32)


def spectra_call(freq_bins, mode_m, mode_n, signal, dests):
    mics, seglen = signal.shape
    rows = 2 * freq_bins.shape[0]
    steps = mics // 128
    lo = pl.BlockSpec((1, 128), lambda i: (0, i))
    hi = pl.BlockSpec((1, 128), lambda i: (0, steps + i))
    m_row, n_row = mode_m.reshape(1, -1), mode_n.reshape(1, -1)
    return pl.pallas_call(
        spectra_kernel,
        grid=(steps,),
        in_specs=[
            pl.BlockSpec(memory_space=pltpu.SMEM),
            lo,
            hi,
            lo,
            hi,
            pl.BlockSpec((128, seglen), lambda i: (i, 0)),
        ],
        out_specs=pl.BlockSpec((dests, 8, 128), lambda i: (0, 0, i)),
        out_shape=jax.ShapeDtypeStruct((dests, 8, mics), F32),
        scratch_shapes=[pltpu.VMEM((rows, seglen), BF16)],
        name="spectra",
        cost_estimate=pl.CostEstimate(flops=2 * rows * mics * seglen, bytes_accessed=mics * seglen * 2, transcendentals=0),
    )(freq_bins, m_row, m_row, n_row, n_row, signal)


def basis_kernel(freq_ref, code_ref, azim_ref, radial_ref):
    half = ORDERS // 2
    for b in range(code_ref.shape[0]):
        lanes = code_ref.shape[2]
        at = pl.ds(b * lanes, lanes)
        code = code_ref[b]
        azimuth = code >> 6
        axial = code & 63
        fine_phase = azimuth * (2 * iota((8, lanes), 0) + 1)
        fine_cos, fine_sin = cos_turns(fine_phase, 10), sin_turns(fine_phase, 10)
        coarse_phase = azimuth * (8 * iota((half // 8, lanes), 0))
        coarse_cos, coarse_sin = cos_turns(coarse_phase, 9), sin_turns(coarse_phase, 9)
        cos_rows, sin_rows = [], []
        for a in range(half // 8):
            cc, cs = coarse_cos[a : a + 1], coarse_sin[a : a + 1]
            cos_rows.append(cc * fine_cos - cs * fine_sin)
            sin_rows.append(cs * fine_cos + cc * fine_sin)
        azim_ref[0, 0:half, at] = jnp.concatenate(cos_rows, axis=0).astype(BF16)
        azim_ref[0, half:, at] = jnp.concatenate(sin_rows, axis=0).astype(BF16)
        for fl in range(radial_ref.shape[1]):
            turns = axial * freq_ref[fl]
            phase = turns * (2 * NRAD - iota((NRAD, lanes), 0)) - azimuth * 32
            radial_ref[0, fl, 0, :, at] = cos_turns(phase, 15)
            radial_ref[0, fl, 1, :, at] = sin_turns(phase, 15)


def basis_call(own_bins, codes, chunks):
    blocks, _, lanes = codes.shape
    mics = blocks * lanes
    per = mics // chunks
    own = own_bins.shape[0]
    return pl.pallas_call(
        basis_kernel,
        grid=(chunks,),
        in_specs=[
            pl.BlockSpec(memory_space=pltpu.SMEM),
            pl.BlockSpec((blocks // chunks, 1, lanes), lambda i: (i, 0, 0)),
        ],
        out_specs=[
            pl.BlockSpec((1, ORDERS, per), lambda i: (i, 0, 0)),
            pl.BlockSpec((1, own, 2, NRAD, per), lambda i: (i, 0, 0, 0, 0)),
        ],
        out_shape=[
            jax.ShapeDtypeStruct((chunks, ORDERS, per), BF16),
            jax.ShapeDtypeStruct((chunks, own, 2, NRAD, per), F32),
        ],
        name="basis",
        cost_estimate=pl.CostEstimate(flops=40 * ORDERS * mics, bytes_accessed=6 * ORDERS * mics, transcendentals=0),
    )(own_bins, codes)


def solve_kernel(recv_ref, azim_ref, radial_ref, amp_ref, res_out_ref, onehot_ref, radmask_ref, res_ref, image_ref, acc_ref, rows_ref):
    chunks, _, per = azim_ref.shape
    own = radial_ref.shape[1]
    half = ORDERS // 2
    group = 2 * NRAD
    mics = chunks * per

    acc_ref[0:NRAD, :] = jnp.zeros((NRAD, ORDERS), F32)

    @pl.loop(0, chunks)
    def _(ch):
        for part in range(2):
            code = recv_ref[ch, 2 * own + part : 2 * own + part + 1, :].astype(jnp.int32)
            at = pl.ds(part * per, per)
            onehot_ref[ch, :, at] = jnp.where(iota((ORDERS, per), 0) == (code >> 5), 1.0, 0.0).astype(BF16)
            radmask_ref[ch, :, at] = jnp.where(iota((NRAD, per), 0) == (code & 31), 1.0, 0.0)
        acc_ref[0:NRAD, :] += nt_dot(radmask_ref[ch].astype(BF16), onehot_ref[ch])

    counts = acc_ref[0:NRAD, :]
    n_column = iota((NRAD, ORDERS), 0).astype(F32)
    weight = (mics ** (-0.5)) * lax.rsqrt(1.0 + n_column)
    counts_weight = counts * weight

    def adjoint(update):
        acc_ref[...] = jnp.zeros(acc_ref.shape, F32)

        @pl.loop(0, chunks)
        def _(ch):
            rows = []
            for fl in range(own):
                re = update(ch, 2 * fl)
                im = update(ch, 2 * fl + 1)
                ec, es = radial_ref[ch, fl, 0], radial_ref[ch, fl, 1]
                rows.append((re * ec + im * es).astype(BF16))
                rows.append((im * ec - re * es).astype(BF16))
            acc_ref[...] += nt_dot(jnp.concatenate(rows, axis=0), azim_ref[ch])

        gradients = []
        for fl in range(own):
            re = acc_ref[fl * group : fl * group + NRAD, :]
            im = acc_ref[fl * group + NRAD : (fl + 1) * group, :]
            rc, rs, ic, isn = re[:, :half], re[:, half:], im[:, :half], im[:, half:]
            g_re = jnp.concatenate([rc + isn, rc - isn], axis=1) * weight
            g_im = jnp.concatenate([ic - rs, ic + rs], axis=1) * weight
            gradients.append((g_re, g_im))
        norms = [total(counts * (g[0] * g[0] + g[1] * g[1])) for g in gradients]
        return gradients, norms

    def total(x):
        return jnp.sum(jnp.sum(x, axis=0, keepdims=True), axis=1, keepdims=True)

    def forward(directions):
        stacked = []
        for d_re, d_im in directions:
            x_re, x_im = d_re * counts_weight, d_im * counts_weight
            p_re, m_re, p_im, m_im = x_re[:, :half], x_re[:, half:], x_im[:, :half], x_im[:, half:]
            stacked.append(jnp.concatenate([p_re + m_re, m_im - p_im], axis=1))
            stacked.append(jnp.concatenate([p_im + m_im, p_re - m_re], axis=1))
        rows_ref[...] = jnp.concatenate(stacked, axis=0).astype(BF16)

        def step(ch, norms):
            fields = jnp.dot(rows_ref[...], azim_ref[ch], preferred_element_type=F32)
            out = []
            for fl in range(own):
                t_re = fields[fl * group : fl * group + NRAD]
                t_im = fields[fl * group + NRAD : (fl + 1) * group]
                ec, es = radial_ref[ch, fl, 0], radial_ref[ch, fl, 1]
                i_re = jnp.sum(ec * t_re - es * t_im, axis=0, keepdims=True)
                i_im = jnp.sum(ec * t_im + es * t_re, axis=0, keepdims=True)
                image_ref[ch, 2 * fl : 2 * fl + 1, :] = i_re
                image_ref[ch, 2 * fl + 1 : 2 * fl + 2, :] = i_im
                out.append(norms[fl] + i_re * i_re + i_im * i_im)
            return tuple(out)

        sums = lax.fori_loop(0, chunks, step, tuple(jnp.zeros((1, per), F32) for _ in range(own)))
        return [jnp.sum(s, axis=1, keepdims=True) for s in sums]

    def first(ch, row):
        value = recv_ref[ch, row : row + 1, :]
        res_ref[ch, row : row + 1, :] = value
        return value

    gradients, norms = adjoint(first)
    directions = gradients
    amplitude = None
    for sweep in range(ITERS):
        image_norms = forward(directions)
        steps = [g / (i + EPS) for g, i in zip(norms, image_norms)]
        grown = [(s * d[0], s * d[1]) for s, d in zip(steps, directions)]
        if amplitude is None:
            amplitude = grown
        else:
            amplitude = [(a[0] + g[0], a[1] + g[1]) for a, g in zip(amplitude, grown)]

        def advance(ch, row, steps=steps):
            value = res_ref[ch, row : row + 1, :] - steps[row // 2] * image_ref[ch, row : row + 1, :]
            res_ref[ch, row : row + 1, :] = value
            return value

        if sweep + 1 < ITERS:
            gradients, next_norms = adjoint(advance)
            momenta = [a / (b + EPS) for a, b in zip(next_norms, norms)]
            directions = [(g[0] + q * d[0], g[1] + q * d[1]) for g, q, d in zip(gradients, momenta, directions)]
            norms = next_norms

    blocks, _, width = res_out_ref.shape
    pieces = blocks // chunks
    for ch in range(chunks):
        for row in range(2 * own):
            value = advance(ch, row)
            for piece in range(pieces):
                res_out_ref[ch * pieces + piece, row : row + 1, :] = value[:, piece * width : (piece + 1) * width]

    rows_ref[...] = jnp.concatenate([part for a in amplitude for part in a], axis=0).astype(BF16)
    copies = amp_ref.shape[0]

    @pl.loop(0, chunks)
    def _(ch):
        for part in range(2):
            at = pl.ds(part * per, per)
            picked = jnp.dot(rows_ref[...], onehot_ref[ch, :, at], preferred_element_type=F32)
            mask = radmask_ref[ch, :, at]
            for row in range(2 * own):
                value = jnp.sum(picked[row * NRAD : (row + 1) * NRAD] * mask, axis=0, keepdims=True)
                for q in range(per // 128):
                    kc = part * (per // 128) + q
                    acc_ref[kc * 2 * own + row : kc * 2 * own + row + 1, 0:128] = value[:, q * 128 : (q + 1) * 128]
        packed = acc_ref[0 : amp_ref.shape[2], 0:128].astype(BF16)
        for copy in range(copies):
            amp_ref[copy, ch] = packed


def solve_call(recv, azim, radial, copies, own):
    chunks, _, per = azim.shape
    modes = 2 * per * chunks
    vmem = pl.BlockSpec(memory_space=pltpu.VMEM)
    return pl.pallas_call(
        solve_kernel,
        in_specs=[vmem] * 3,
        out_specs=[vmem] * 2,
        out_shape=[
            jax.ShapeDtypeStruct((copies, chunks, 2 * own * modes // chunks // 128, 128), BF16),
            jax.ShapeDtypeStruct((copies, 2 * own, chunks * per // copies), F32),
        ],
        scratch_shapes=[
            pltpu.VMEM((chunks, ORDERS, 2 * per), BF16),
            pltpu.VMEM((chunks, NRAD, 2 * per), F32),
            pltpu.VMEM((chunks, 2 * own, per), F32),
            pltpu.VMEM((chunks, 2 * own, per), F32),
            pltpu.VMEM((2 * own * NRAD, ORDERS), F32),
            pltpu.VMEM((2 * own * NRAD, ORDERS), BF16),
        ],
        compiler_params=pltpu.CompilerParams(vmem_limit_bytes=40 << 20),
        name="solve",
        cost_estimate=pl.CostEstimate(flops=10 * 256 * 4096 * 128, bytes_accessed=8 << 20, transcendentals=0),
    )(recv, azim, radial)


def expand_kernel(in_ref, amp_ref, pow_ref, wide_ref):
    segs, dests, lines, _ = in_ref.shape
    rows = amp_ref.shape[0] // dests
    wide_ref[...] = in_ref[...].astype(F32).reshape(wide_ref.shape)
    for d in range(dests):
        for kc in range(lines // rows):
            power = []
            for row in range(rows):
                value = wide_ref[pl.ds(d * lines + kc * rows + row, segs, stride=dests * lines), :]
                amp_ref[d * rows + row, :, kc * 128 : (kc + 1) * 128] = value
                power.append(jnp.sum(value * value, axis=0, keepdims=True))
            for fl in range(rows // 2):
                at = d * (rows // 2) + fl
                pow_ref[at : at + 1, kc * 128 : (kc + 1) * 128] = (power[2 * fl] + power[2 * fl + 1]) * (1.0 / segs)


def expand_call(recv, rows, splits):
    segs, dests, lines, _ = recv.shape
    modes = lines // rows * 128
    here = dests // splits
    return pl.pallas_call(
        expand_kernel,
        grid=(splits,),
        in_specs=[pl.BlockSpec((segs, here, lines, 128), lambda i: (0, i, 0, 0))],
        out_specs=[
            pl.BlockSpec((here * rows, segs, modes), lambda i: (i, 0, 0)),
            pl.BlockSpec((here * rows // 2, modes), lambda i: (i, 0)),
        ],
        out_shape=[
            jax.ShapeDtypeStruct((dests * rows, segs, modes), F32),
            jax.ShapeDtypeStruct((dests * rows // 2, modes), F32),
        ],
        scratch_shapes=[pltpu.VMEM((segs * here * lines, 128), F32)],
        name="expand",
        cost_estimate=pl.CostEstimate(flops=1 << 21, bytes_accessed=3 << 20, transcendentals=0),
    )(recv)


def turn_kernel(in_ref, out_ref):
    for row in range(out_ref.shape[0]):
        out_ref[row] = in_ref[:, row, :]


def turn_call(recv):
    segs, rows, width = recv.shape
    vmem = pl.BlockSpec(memory_space=pltpu.VMEM)
    return pl.pallas_call(
        turn_kernel,
        in_specs=[vmem],
        out_specs=vmem,
        out_shape=jax.ShapeDtypeStruct((rows, segs, width), F32),
        name="turn",
        cost_estimate=pl.CostEstimate(flops=0, bytes_accessed=1 << 17, transcendentals=0),
    )(recv)


def on_device(signal, mic_axial, mic_azimuth, mode_m, mode_n, freq_bins):
    segs = lax.axis_size("mic")
    owners = lax.axis_size("mode")
    freqs = freq_bins.shape[0]
    own = freqs // owners
    code = mic_azimuth * AXIAL + mic_axial
    codes = lax.all_to_all(jnp.broadcast_to(code[None, None, :], (segs, 1, code.shape[0])), "mic", 0, 0, tiled=True)
    spectra = spectra_call(freq_bins, mode_m, mode_n, signal[0], owners)
    recv = lax.all_to_all(spectra, "mode", 0, 0, tiled=True)
    own_bins = lax.dynamic_slice_in_dim(freq_bins, lax.axis_index("mode") * own, own, 0)
    azim, radial = basis_call(own_bins, codes, owners)
    amp, res = solve_call(recv, azim, radial, segs, own)
    residual = turn_call(lax.all_to_all(res, "mic", 0, 0, tiled=True))
    shape = amp.shape
    amp = lax.all_to_all(amp.reshape(segs * owners, *shape[2:]), ("mic", "mode"), 0, 0, tiled=True)
    amplitude, power = expand_call(amp.reshape(shape), 2 * own, 2)
    modes = mode_m.shape[0]
    return (
        amplitude.reshape(freqs, 2, segs, modes),
        power,
        residual.reshape(own, 2, segs, residual.shape[2]),
    )


def solution(mesh):
    in_specs = (P("mic", "mode", None), P("mic"), P("mic"), P("mode"), P("mode"), P())
    out_specs = (P(None, None, None, "mode"), P(None, "mode"), P("mode", None, None, "mic"))
    return jax.shard_map(
        on_device, mesh=mesh, in_specs=in_specs, out_specs=out_specs, check_vma=False
    )
```

time: 1290 us -> 88.9 us (0.07)
  matrix products: 528 us -> 0 us
  waiting for transfers between devices: 219 us -> 18.8 us
  blocking collectives: 203 us -> 11.1 us
  loops' own time: 128 us -> 0 us
  local copies, waits for them, and re-layouts: 117 us -> 5.36 us
  other arithmetic: 62.5 us -> 0.7 us
  Pallas kernels: 0 us -> 29.3 us
  starting transfers between devices: 8.19 us -> 22.2 us
  between operations: 14.3 us -> 0.67 us
    dot_general x129 -> x0, matrix products: 528 us -> none  [the longest x32 132 us: adjoint_product(): second = jnp.dot(stacked, imag_part, preferred_element_type=jnp.float32)]
    psum x2 -> x0, waiting for transfers between devices: 171 us -> none  [gradient_of(): gradient = lax.psum(partial_sum, 'mic')]
    psum x4 -> x0, blocking collectives: 163 us -> none  [the longest x2 135 us: on_device(): image_norm = lax.psum(padded, ('mic', 'mode'))]
    another operation x4 -> x0, loops' own time: 128 us -> none  [the longest x2 64.3 us: on_device(): lax.map(images_single, jnp.arange(freq_rows * lax.axis_size('mode'), dtyp...]
    dynamic_slice x162 -> x1, local copies, waits for them, and re-layouts: 75.4 us -> 0.58 us  [on_device(): lax.dynamic_slice_in_dim(freq_bins, lax.axis_index('mode') * own, own, 0)]
    reduce_scatter x2 -> x0, waiting for transfers between devices: 41.5 us -> none  [on_device(): lax.psum_scatter(lax.map(images_single, jnp.arange(freq_rows * lax.axis_s...]
    mul x64 -> x0, other arithmetic: 41.5 us -> none  [mode_tile(): bin_value * (2 * NRAD - mode_n)]
    pallas_call x0 -> x5, Pallas kernels: none -> 29.3 us  [the longest x1 13.2 us: solve_call(): pl.pallas_call(solve_kernel, in_specs=[vmem] * 3, out_specs=[vmem] * 2, o...]
  transfers between devices with their start and end apart: 5 -> 3, of which waited for: 5 -> 2; matrix products, arithmetic and copies ran while one was open for 0% -> 1% of each run, Pallas kernels for 0% -> 14%
where the time goes in v1:
time: 88.9 us; the launch traced here: 88.1 us
  Pallas kernels  29.3 us (33%)
  starting transfers between devices  22.2 us (25%)
  waiting for transfers between devices  18.8 us (21%)
  blocking collectives  11.1 us (12%)
  local copies, waits for them, and re-layouts  5.36 us (6%)
    all_to_all x1, waiting for transfers between devices, on_device(): lax.all_to_all(amp.reshape(segs * owners, *shape[2:]), ('mic', 'mode'), 0...  17.7 us
    pallas_call x1, Pallas kernels, solve_call(): pl.pallas_call(solve_kernel, in_specs=[vmem] * 3, out_specs=[vmem] * 2, o...  13.2 us
    all_to_all x1, blocking collectives, on_device(): residual = turn_call(lax.all_to_all(res, 'mic', 0, 0, tiled=True))  11.1 us
    all_to_all x1, starting transfers between devices, on_device(): lax.all_to_all(jnp.broadcast_to(code[None, None, :], (segs, 1, code.shape...  8.59 us
    all_to_all x1, starting transfers between devices, on_device(): lax.all_to_all(amp.reshape(segs * owners, *shape[2:]), ('mic', 'mode'), 0...  7.22 us
    all_to_all x1, starting transfers between devices, on_device(): recv = lax.all_to_all(spectra, 'mode', 0, 0, tiled=True)  6.4 us
    pallas_call x1, Pallas kernels, basis_call(): pl.pallas_call(basis_kernel, grid=(chunks,), in_specs=[pl.BlockSpec(memor...  5.72 us
    pallas_call x1, Pallas kernels, spectra_call(): pl.pallas_call(spectra_kernel, grid=(steps,), in_specs=[pl.BlockSpec(memo...  5.36 us
  transfers between devices with their start and end apart: 3, of which 2 were waited for; matrix products, arithmetic and copies ran while one was open for 1% of the time, Pallas kernels for 14%

profile of v1, /device:TPU:1, one launch (start us, length us, event | category | flops | bytes accessed | tf_op | source)
XLA Modules:
  0.0 88.1 jit_solution(9512602681546761337)
XLA Ops:
  0.6 0.7 multiply_add_fusion
  1.3 0.6 broadcast_in_dim.2
  1.9 8.6 %all-to-all-start.1 = ((s32[16,1,256]{2,1,0:T(1,128)}), s32[16,1,256]{2,1,0:T(1,128)S(1)}, u32[]{:S(2)}, u32[]{:S(2)}) async-start(s32[16,1,256]{2,1,0:T(1,128)} %broadcast_in_dim.2), calls=%async_computation.1 | async-start | bytes 32768 | tf_op jit(solution)/shard_map/all_to_all | solution.py:375
  10.5 0.0 copy-start.4
  10.6 5.4 %spectra.1 = f32[8,8,512]{2,1,0:T(8,128)} custom-call(s32[16]{0:T(128)} %freq_ref.1, s32[1,1024]{1,0:T(1,128)} %bitcast.10, s32[1,1024]{1,0:T(1,128)} %bitcast.11, s32[1,1024]{1,0:T(1,128)} %bitcast.12, s32[1,1024]{1,0:T(1,128)} %bitcast.13, bf16[512,4096]{1,0:T(8,128)(2,1)} %bitcast.7), custom_call_target="tpu_custom_call" | custom-call | flops 134217728 | bytes 4194304 | tf_op jit(solution)/shard_map/spectra/pallas_call | solution.py:85
  15.9 1.1 %all-to-all-done.1.code_ref = s32[16,1,256]{2,1,0:T(1,128)S(1)} async-done(((s32[16,1,256]{2,1,0:T(1,128)}), s32[16,1,256]{2,1,0:T(1,128)S(1)}, u32[]{:S(2)}, u32[]{:S(2)}) %all-to-all-start.1) | async-done | bytes 16416 | tf_op jit(solution)/shard_map/all_to_all | solution.py:375
  17.0 0.0 copy-start.3
  17.0 6.4 %all-to-all-start = ((f32[8,8,512]{2,1,0:T(8,128)}), f32[8,8,512]{2,1,0:T(8,128)S(1)}, u32[]{:S(2)}, u32[]{:S(2)}) async-start(f32[8,8,512]{2,1,0:T(8,128)} %spectra.1), calls=%async_computation | async-start | bytes 262144 | tf_op jit(solution)/shard_map/all_to_all | solution.py:377
  23.4 0.0 copy-done.4
  23.4 0.6 dynamic_slice.3.freq_ref
  24.0 0.0 copy-done.3
  24.0 5.7 %basis.1 = (bf16[8,256,512]{2,1,0:T(8,128)(2,1)}, f32[8,2,2,32,512]{4,3,2,1,0:T(8,128)}) custom-call(s32[2]{0:T(128)} %dynamic_slice.3.freq_ref, s32[16,1,256]{2,1,0:T(1,128)} %copy-done.3), custom_call_target="tpu_custom_call" | custom-call | flops 41943040 | bytes 6291456 | tf_op jit(solution)/shard_map/basis/pallas_call | solution.py:135
  29.7 0.0 all-to-all-done.recv_ref
  29.7 0.0 copy-start
  29.7 1.6 %copy-done = bf16[8,256,512]{2,1,0:T(8,128)(2,1)S(1)} copy-done((bf16[8,256,512]{2,1,0:T(8,128)(2,1)S(1)}, bf16[8,256,512]{2,1,0:T(8,128)(2,1)}, u32[]{:S(2)}) %copy-start) | copy-done | bytes 2097176
  31.3 0.0 copy-start.1
  31.3 1.6 %copy-done.1 = f32[8,2,2,32,512]{4,3,2,1,0:T(8,128)S(1)} copy-done((f32[8,2,2,32,512]{4,3,2,1,0:T(8,128)S(1)}, f32[8,2,2,32,512]{4,3,2,1,0:T(8,128)}, u32[]{:S(2)}) %copy-start.1) | copy-done | bytes 2097176
  32.9 13.2 %solve.1 = (bf16[16,8,32,128]{3,2,1,0:T(8,128)(2,1)}, f32[16,4,256]{2,1,0:T(4,128)S(1)}) custom-call(f32[8,8,512]{2,1,0:T(8,128)S(1)} %all-to-all-done.recv_ref, bf16[8,256,512]{2,1,0:T(8,128)(2,1)S(1)} %copy-done, f32[8,2,2,32,512]{4,3,2,1,0:T(8,128)S(1)} %copy-done.1), custom_call_target="tpu_custom_call" | custom-call | flops 1342177280 | bytes 8388608 | tf_op jit(solution)/shard_map/solve/pallas_call | solution.py:291
  46.1 11.1 %all_to_all.20.in_ref = f32[16,4,256]{2,1,0:T(4,128)} all-to-all(f32[16,4,256]{2,1,0:T(4,128)S(1)} %get-tuple-element.14), channel_id=1, replica_groups=mesh['mic'=16,'mode'=8] {'mic'}, dimensions={0} | all-to-all | bytes 131072 | tf_op jit(solution)/shard_map/all_to_all | solution.py:381
  57.2 7.2 %all-to-all-start.2 = ((bf16[128,32,128]{2,1,0:T(8,128)(2,1)}), bf16[128,32,128]{2,1,0:T(8,128)(2,1)S(1)}, u32[]{:S(2)}, u32[]{:S(2)}) async-start(bf16[128,32,128]{2,1,0:T(8,128)(2,1)} %bitcast.3), calls=%async_computation.2 | async-start | bytes 2097152 | tf_op jit(solution)/shard_map/all_to_all | solution.py:383
  64.4 1.5 %turn.1 = f32[4,16,256]{2,1,0:T(8,128)} custom-call(f32[16,4,256]{2,1,0:T(4,128)} %all_to_all.20.in_ref), custom_call_target="tpu_custom_call" | custom-call | bytes 131072 | tf_op jit(solution)/shard_map/turn/pallas_call | solution.py:359
  65.9 17.7 %all-to-all-done.2 = bf16[128,32,128]{2,1,0:T(8,128)(2,1)S(1)} async-done(((bf16[128,32,128]{2,1,0:T(8,128)(2,1)}), bf16[128,32,128]{2,1,0:T(8,128)(2,1)S(1)}, u32[]{:S(2)}, u32[]{:S(2)}) %all-to-all-start.2) | async-done | bytes 1048608 | tf_op jit(solution)/shard_map/all_to_all | solution.py:383
  83.7 0.0 copy-start.2
  83.7 1.0 %copy-done.2 = bf16[128,32,128]{2,1,0:T(8,128)(2,1)} copy-done((bf16[128,32,128]{2,1,0:T(8,128)(2,1)}, bf16[128,32,128]{2,1,0:T(8,128)(2,1)S(1)}, u32[]{:S(2)}) %copy-start.2) | copy-done | bytes 1048600
  84.6 3.5 %expand.1 = (f32[32,16,1024]{2,1,0:T(8,128)}, f32[16,1024]{1,0:T(8,128)}) custom-call(bf16[16,8,32,128]{3,2,1,0:T(8,128)(2,1)} %bitcast.8), custom_call_target="tpu_custom_call" | custom-call | flops 2097152 | bytes 3145728 | tf_op jit(solution)/shard_map/expand/pallas_call | solution.py:333
Async XLA Ops:
  1.9 15.0 %all-to-all-start.1 = ((s32[16,1,256]{2,1,0:T(1,128)}), s32[16,1,256]{2,1,0:T(1,128)S(1)}, u32[]{:S(2)}, u32[]{:S(2)}) async-start(s32[16,1,256]{2,1,0:T(1,128)} %broadcast_in_dim.2), calls=%async_computation.1 | async-start | bytes 32768 | tf_op jit(solution)/shard_map/all_to_all | solution.py:375
  10.5 12.8 %copy-start.4 = (s32[16]{0:T(128)S(1)}, s32[16]{0:T(128)}, u32[]{:S(2)}) copy-start(s32[16]{0:T(128)} %freq_ref.1) | copy-start | bytes 196
  17.0 7.0 %copy-start.3 = (s32[16,1,256]{2,1,0:T(1,128)}, s32[16,1,256]{2,1,0:T(1,128)S(1)}, u32[]{:S(2)}) copy-start(s32[16,1,256]{2,1,0:T(1,128)S(1)} %all-to-all-done.1.code_ref) | copy-start | bytes 49156
  17.0 12.7 %all-to-all-start = ((f32[8,8,512]{2,1,0:T(8,128)}), f32[8,8,512]{2,1,0:T(8,128)S(1)}, u32[]{:S(2)}, u32[]{:S(2)}) async-start(f32[8,8,512]{2,1,0:T(8,128)} %spectra.1), calls=%async_computation | async-start | bytes 262144 | tf_op jit(solution)/shard_map/all_to_all | solution.py:377
  29.7 1.6 %copy-start = (bf16[8,256,512]{2,1,0:T(8,128)(2,1)S(1)}, bf16[8,256,512]{2,1,0:T(8,128)(2,1)}, u32[]{:S(2)}) copy-start(bf16[8,256,512]{2,1,0:T(8,128)(2,1)} %get-tuple-element.9.azim_ref) | copy-start | bytes 6291460
  31.3 1.6 %copy-start.1 = (f32[8,2,2,32,512]{4,3,2,1,0:T(8,128)S(1)}, f32[8,2,2,32,512]{4,3,2,1,0:T(8,128)}, u32[]{:S(2)}) copy-start(f32[8,2,2,32,512]{4,3,2,1,0:T(8,128)} %get-tuple-element.10.radial_ref) | copy-start | bytes 6291460
  57.2 26.4 %all-to-all-start.2 = ((bf16[128,32,128]{2,1,0:T(8,128)(2,1)}), bf16[128,32,128]{2,1,0:T(8,128)(2,1)S(1)}, u32[]{:S(2)}, u32[]{:S(2)}) async-start(bf16[128,32,128]{2,1,0:T(8,128)(2,1)} %bitcast.3), calls=%async_computation.2 | async-start | bytes 2097152 | tf_op jit(solution)/shard_map/all_to_all | solution.py:383
  83.7 1.0 %copy-start.2 = (bf16[128,32,128]{2,1,0:T(8,128)(2,1)}, bf16[128,32,128]{2,1,0:T(8,128)(2,1)S(1)}, u32[]{:S(2)}) copy-start(bf16[128,32,128]{2,1,0:T(8,128)(2,1)S(1)} %all-to-all-done.2) | copy-start | bytes 3145732

commit v2 on v0

v2 whole, which is shorter than its diff:
```python
import jax
import jax.numpy as jnp
from jax import lax
from jax.experimental import pallas as pl
from jax.experimental.pallas import tpu as pltpu
from jax.sharding import PartitionSpec as P

ITERS = 2
AXIAL = 64
NRAD = 32
ORDERS = 256
HALF = ORDERS // 2
EPS = 1e-06
SIN_COEFS = (1.5707963200919937, -0.6459637612912833, 0.07968992686556589, -0.0046741574942986315, 0.0001516785309118288)
BF16 = jnp.bfloat16
F32 = jnp.float32
VMEM = pl.BlockSpec(memory_space=pltpu.VMEM)
SMEM = pl.BlockSpec(memory_space=pltpu.SMEM)


def cos_turns(turns):
    z = 1.0 - 4.0 * jnp.abs(turns - jnp.round(turns))
    square = z * z
    total = SIN_COEFS[-1] * square + SIN_COEFS[-2]
    for coef in SIN_COEFS[-3::-1]:
        total = total * square + coef
    return total * z


def sin_turns(turns):
    return cos_turns(turns - 0.25)


def turn_by(re, im, step_re, step_im):
    return re * step_re - im * step_im, re * step_im + im * step_re


def iota(shape, axis):
    return lax.broadcasted_iota(jnp.int32, shape, axis)


def nt_dot(a, b):
    return lax.dot_general(a, b, (((1,), (1,)), ((), ())), preferred_element_type=F32)


def groups(x):
    return x.reshape(x.shape[0] // 8, 8, x.shape[1])


def periodic(x):
    x = x + pltpu.roll(x, 4, 0)
    return x + pltpu.roll(x, 2, 0)


def analysis_kernel(freq_ref, out_ref):
    rows, seglen = out_ref.shape
    freqs = rows // 2
    row = iota((freqs, 128), 0)
    freq = jnp.zeros((freqs, 128), jnp.int32)
    for f in range(freqs):
        freq = jnp.where(row == f, freq_ref[f], freq)
    freq = freq.astype(F32)
    lane = iota((freqs, 128), 1).astype(F32)
    start = freq * lane * (1.0 / seglen)
    step = freq * (128.0 / seglen)
    re, im = cos_turns(start), -sin_turns(start)
    step_re, step_im = cos_turns(step), -sin_turns(step)
    scale = (3.0 * seglen / 8.0) ** (-0.5)
    for block in range(seglen // 128):
        sample = iota((8, 128), 1).astype(F32) + block * 128.0
        window = (0.5 - 0.5 * cos_turns(sample * (1.0 / seglen)))[None] * scale
        at = slice(block * 128, (block + 1) * 128)
        out_ref[0:freqs, at] = (groups(re) * window).reshape(freqs, 128).astype(BF16)
        out_ref[freqs:, at] = (groups(im) * window).reshape(freqs, 128).astype(BF16)
        re, im = turn_by(re, im, step_re, step_im)


def analysis_call(freq_bins, seglen):
    return pl.pallas_call(
        analysis_kernel,
        in_specs=[SMEM],
        out_specs=VMEM,
        out_shape=jax.ShapeDtypeStruct((2 * freq_bins.shape[0], seglen), BF16),
        name="analysis",
        cost_estimate=pl.CostEstimate(flops=1 << 21, bytes_accessed=1 << 18, transcendentals=0),
    )(freq_bins)


def spectra_kernel(analysis_ref, m_lo_ref, m_hi_ref, n_lo_ref, n_hi_ref, first_ref, second_ref, signal_ref, out_ref):
    dests = out_ref.shape[0]
    freqs = analysis_ref.shape[0] // 2
    own = freqs // dests
    step = pl.program_id(0)
    spectra = nt_dot(analysis_ref[...], signal_ref[...])
    codes = []
    for m_ref, n_ref in ((m_lo_ref, n_lo_ref), (m_hi_ref, n_hi_ref)):
        m = m_ref[...]
        codes.append((jnp.where(m >= 0, m, HALF - 1 - m) * NRAD + n_ref[...]).astype(F32))
    straight = (lax.axis_index("mic") < dests) == (step < pl.num_programs(0) // 2)
    codes.append(jnp.where(straight, first_ref[...], second_ref[...]).astype(F32))
    codes.append(jnp.zeros_like(codes[0]))
    tail = jnp.concatenate(codes, axis=0)
    for d in range(dests):
        out_ref[d, 0:own, :] = spectra[d * own : (d + 1) * own]
        out_ref[d, own : 2 * own, :] = spectra[freqs + d * own : freqs + (d + 1) * own]
        out_ref[d, 2 * own :, :] = tail


def spectra_call(analysis, mode_m, mode_n, first, second, signal, dests):
    mics, seglen = signal.shape
    rows = analysis.shape[0]
    steps = mics // 128
    lo = pl.BlockSpec((1, 128), lambda i: (0, i))
    hi = pl.BlockSpec((1, 128), lambda i: (0, steps + i))
    code = pl.BlockSpec((1, 128), lambda i: (0, i % (steps // 2)))
    m_row, n_row = mode_m.reshape(1, -1), mode_n.reshape(1, -1)
    return pl.pallas_call(
        spectra_kernel,
        grid=(steps,),
        in_specs=[VMEM, lo, hi, lo, hi, code, code, pl.BlockSpec((128, seglen), lambda i: (i, 0))],
        out_specs=pl.BlockSpec((dests, 8, 128), lambda i: (0, 0, i)),
        out_shape=jax.ShapeDtypeStruct((dests, 8, mics), F32),
        name="spectra",
        cost_estimate=pl.CostEstimate(flops=2 * rows * mics * seglen, bytes_accessed=mics * seglen * 2, transcendentals=0),
    )(analysis, m_row, m_row, n_row, n_row, first.reshape(1, -1), second.reshape(1, -1), signal)


def solve_kernel(
    freq_ref, recv_ref, out_ref, azim_ref, rad_ref, res_ref, image_ref, field_ref, onehot_ref, radhot_ref, dir_ref, grown_ref, rows_ref
):
    chunks, _, per = recv_ref.shape
    mics = chunks * per
    stack = 2 * NRAD
    base = 2 * lax.axis_index("mode")
    odd = (iota((8, per), 0) & 1) == 1
    freq = jnp.where(odd, freq_ref[base + 1], freq_ref[base]).astype(F32)
    row = iota((8, per), 0).astype(F32)
    radial = (iota((8, per), 0) >> 1).astype(F32)

    @pl.loop(0, chunks)
    def _(ch):
        at = pl.ds(pl.multiple_of(ch * per, per), per)
        code = jnp.broadcast_to(recv_ref[ch, 6:7, :], (8, per))
        azimuth = jnp.floor(code * (1.0 / AXIAL))
        axial = code - azimuth * AXIAL
        turns = azimuth * (row + 0.5) * (1.0 / 512)
        re, im = cos_turns(turns), sin_turns(turns)
        turns = azimuth * (8.0 / 512)
        step_re, step_im = cos_turns(turns), sin_turns(turns)
        next_re, next_im = turn_by(re, im, step_re, step_im)
        step_re, step_im = turn_by(step_re, step_im, step_re, step_im)
        re = jnp.stack([re, next_re])
        im = jnp.stack([im, next_im])
        for a in range(HALF // 16):
            azim_ref[16 * a : 16 * a + 16, at] = re.reshape(16, per).astype(BF16)
            azim_ref[HALF + 16 * a : HALF + 16 * a + 16, at] = im.reshape(16, per).astype(BF16)
            if a + 1 < HALF // 16:
                re, im = turn_by(re, im, step_re[None], step_im[None])
        turns = (axial * freq * (2.0 * NRAD - radial) - azimuth * 32.0) * (1.0 / 32768)
        re, im = cos_turns(turns), sin_turns(turns)
        turns = axial * freq * (-4.0 / 32768)
        step_re, step_im = cos_turns(turns), sin_turns(turns)
        for a in range(stack // 8):
            rad_ref[0, 8 * a : 8 * a + 8, at] = re
            rad_ref[1, 8 * a : 8 * a + 8, at] = im
            if a + 1 < stack // 8:
                re, im = turn_by(re, im, step_re, step_im)
        for c in range(2):
            res_ref[c, :, at] = jnp.where(odd, recv_ref[ch, 2 * c + 1 : 2 * c + 2, :], recv_ref[ch, 2 * c : 2 * c + 1, :])

    order_rows = iota((ORDERS, 128), 0).astype(F32).astype(BF16)
    radial_rows = (iota((stack, 128), 0) >> 1).astype(F32).astype(BF16)
    one, zero = jnp.ones((), BF16), jnp.zeros((), BF16)

    @pl.loop(0, chunks)
    def _(ch):
        for part in range(2):
            code = recv_ref[ch, 4 + part : 5 + part, :]
            order = jnp.floor(code * (1.0 / NRAD))
            radius = (code - order * NRAD).astype(BF16)
            order = order.astype(BF16)
            for q in range(per // 128):
                at = pl.ds(pl.multiple_of(ch * 2 * per + part * per + q * 128, 128), 128)
                lanes = slice(q * 128, (q + 1) * 128)
                onehot_ref[:, at] = jnp.where(order_rows == order[:, lanes], one, zero)
                radhot_ref[:, at] = jnp.where(radial_rows == radius[:, lanes], one, zero)

    counts = nt_dot(radhot_ref[...], onehot_ref[...])
    weight = (mics ** (-0.5)) * lax.rsqrt(1.0 + (iota((stack, ORDERS), 0) >> 1).astype(F32))
    counts_weight = counts * weight

    def scaled(column, x):
        return (column[None] * groups(x)).reshape(x.shape)

    def row_sums(x):
        return periodic(jnp.sum(jnp.sum(groups(x), axis=0), axis=1, keepdims=True))

    def adjoint(advance):
        for ch in range(chunks):
            at = slice(ch * per, (ch + 1) * per)
            re, im = advance(0, at)[None], advance(1, at)[None]
            ec, es = groups(rad_ref[0, :, at]), groups(rad_ref[1, :, at])
            field_ref[0:stack, at] = (re * ec + im * es).reshape(stack, per).astype(BF16)
            field_ref[stack:, at] = (im * ec - re * es).reshape(stack, per).astype(BF16)
        out = nt_dot(field_ref[...], azim_ref[...])
        re, im = out[:stack], out[stack:]
        rc, rs, ic, ics = re[:, :HALF], re[:, HALF:], im[:, :HALF], im[:, HALF:]
        g_re = jnp.concatenate([rc + ics, rc - ics], axis=1) * weight
        g_im = jnp.concatenate([ic - rs, ic + rs], axis=1) * weight
        return g_re, g_im, row_sums(counts * (g_re * g_re + g_im * g_im))

    def forward():
        x_re, x_im = dir_ref[0] * counts_weight, dir_ref[1] * counts_weight
        p_re, m_re, p_im, m_im = x_re[:, :HALF], x_re[:, HALF:], x_im[:, :HALF], x_im[:, HALF:]
        rows_ref[0:stack] = jnp.concatenate([p_re + m_re, m_im - p_im], axis=1).astype(BF16)
        rows_ref[stack:] = jnp.concatenate([p_im + m_im, p_re - m_re], axis=1).astype(BF16)
        norm = jnp.zeros((8, per), F32)
        for ch in range(chunks):
            at = slice(ch * per, (ch + 1) * per)
            out = jnp.dot(rows_ref[...], azim_ref[:, at], preferred_element_type=F32)
            t_re, t_im = out[:stack], out[stack:]
            ec, es = rad_ref[0, :, at], rad_ref[1, :, at]
            i_re = periodic(jnp.sum(groups(ec * t_re - es * t_im), axis=0))
            i_im = periodic(jnp.sum(groups(ec * t_im + es * t_re), axis=0))
            image_ref[0, :, at] = i_re
            image_ref[1, :, at] = i_im
            norm = norm + (i_re * i_re + i_im * i_im)
        return jnp.sum(norm, axis=1, keepdims=True)

    g_re, g_im, norm = adjoint(lambda c, at: res_ref[c, :, at])
    dir_ref[0] = g_re
    dir_ref[1] = g_im
    for sweep in range(ITERS):
        step = norm / (forward() + EPS)

        def advance(c, at, step=step):
            value = res_ref[c, :, at] - step * image_ref[c, :, at]
            res_ref[c, :, at] = value
            return value

        for c in range(2):
            grown = scaled(step, dir_ref[c])
            grown_ref[c] = grown if sweep == 0 else grown_ref[c] + grown
        if sweep + 1 < ITERS:
            g_re, g_im, next_norm = adjoint(advance)
            momentum = next_norm / (norm + EPS)
            dir_ref[0] = g_re + scaled(momentum, dir_ref[0])
            dir_ref[1] = g_im + scaled(momentum, dir_ref[1])
            norm = next_norm

    copies, _, lines, _ = out_ref.shape
    width = mics // copies
    upper = (iota((8, width), 0) & 2) == 0
    first = iota((8, 128), 0) < 4
    for copy in range(copies):
        at = slice(copy * width, (copy + 1) * width)
        value = jnp.where(upper, advance(0, at), advance(1, at))
        packed = jnp.where(first, value[:, :128], value[:, 128:]).astype(BF16)
        for ch in range(chunks):
            out_ref[copy, ch, lines - 8 :, :] = packed

    rows_ref[0:stack] = grown_ref[0].astype(BF16)
    rows_ref[stack:] = grown_ref[1].astype(BF16)
    upper = (iota((8, per), 0) & 2) == 0
    radial_rows = (iota((stack, per), 0) >> 1).astype(F32)
    for ch in range(chunks):
        tiles = []
        for part in range(2):
            code = recv_ref[ch, 4 + part : 5 + part, :]
            radius = code - jnp.floor(code * (1.0 / NRAD)) * NRAD
            begin = ch * 2 * per + part * per
            picked = jnp.dot(rows_ref[...], onehot_ref[:, begin : begin + per], preferred_element_type=F32)
            mask = radial_rows == radius
            re = periodic(jnp.sum(groups(jnp.where(mask, picked[:stack], 0.0)), axis=0))
            im = periodic(jnp.sum(groups(jnp.where(mask, picked[stack:], 0.0)), axis=0))
            value = jnp.where(upper, re, im)
            for q in range(0, per // 128, 2):
                tiles.append(jnp.where(first, value[:, q * 128 : (q + 1) * 128], value[:, (q + 1) * 128 : (q + 2) * 128]))
        packed = jnp.concatenate(tiles, axis=0).astype(BF16)
        for copy in range(copies):
            out_ref[copy, ch, 0 : lines - 8, :] = packed


def solve_call(freq_bins, recv, copies):
    chunks, _, per = recv.shape
    mics, modes, stack = chunks * per, 2 * chunks * per, 2 * NRAD
    return pl.pallas_call(
        solve_kernel,
        in_specs=[SMEM, VMEM],
        out_specs=VMEM,
        out_shape=jax.ShapeDtypeStruct((copies, chunks, 4 * modes // chunks // 128 + 8, 128), BF16),
        scratch_shapes=[
            pltpu.VMEM((ORDERS, mics), BF16),
            pltpu.VMEM((2, stack, mics), F32),
            pltpu.VMEM((2, 8, mics), F32),
            pltpu.VMEM((2, 8, mics), F32),
            pltpu.VMEM((2 * stack, mics), BF16),
            pltpu.VMEM((ORDERS, modes), BF16),
            pltpu.VMEM((stack, modes), BF16),
            pltpu.VMEM((2, stack, ORDERS), F32),
            pltpu.VMEM((2, stack, ORDERS), F32),
            pltpu.VMEM((2 * stack, ORDERS), BF16),
        ],
        compiler_params=pltpu.CompilerParams(vmem_limit_bytes=40 << 20),
        name="solve",
        cost_estimate=pl.CostEstimate(flops=10 * 256 * 4096 * 128, bytes_accessed=8 << 20, transcendentals=0),
    )(freq_bins, recv)


def expand_kernel(in_ref, amp_ref, pow_ref, res_ref, wide_ref):
    segs, _, lines, _ = in_ref.shape
    lines = lines - 8
    rows = 4
    dests = amp_ref.shape[0] // rows
    step = pl.program_id(0)
    for d in range(dests):
        for s in range(segs):
            wide_ref[d, pl.ds(s, lines, stride=segs), :] = in_ref[s, step * dests + d, 0:lines, :].astype(F32)
        for kc in range(lines // rows):
            at = slice(kc * 128, (kc + 1) * 128)
            for fl in range(rows // 2):
                power = jnp.zeros((1, 128), F32)
                for c in range(2):
                    line = kc * rows + 2 * c + fl
                    value = wide_ref[d, line * segs : (line + 1) * segs, :]
                    amp_ref[d * rows + 2 * fl + c, :, at] = value
                    power = power + jnp.sum(value * value, axis=0, keepdims=True)
                pow_ref[2 * d + fl : 2 * d + fl + 1, at] = power * (1.0 / segs)

    @pl.when(step == 0)
    def _():
        owner = lax.axis_index("mode")
        for s in range(segs):
            wide_ref[0, pl.ds(s, 8, stride=segs), :] = in_ref[s, owner, lines:, :].astype(F32)
        for half in range(2):
            for fl in range(2):
                for c in range(2):
                    line = half * rows + 2 * c + fl
                    res_ref[2 * fl + c, :, half * 128 : (half + 1) * 128] = wide_ref[0, line * segs : (line + 1) * segs, :]


def expand_call(recv, splits):
    segs, dests, lines, _ = recv.shape
    lines = lines - 8
    rows = 4
    modes = lines // rows * 128
    here = dests // splits
    return pl.pallas_call(
        expand_kernel,
        grid=(splits,),
        in_specs=[VMEM],
        out_specs=[
            pl.BlockSpec((here * rows, segs, modes), lambda i: (i, 0, 0)),
            pl.BlockSpec((here * rows // 2, modes), lambda i: (i, 0)),
            pl.BlockSpec((rows, segs, 256), lambda i: (0, 0, 0)),
        ],
        out_shape=[
            jax.ShapeDtypeStruct((dests * rows, segs, modes), F32),
            jax.ShapeDtypeStruct((dests * rows // 2, modes), F32),
            jax.ShapeDtypeStruct((rows, segs, 256), F32),
        ],
        scratch_shapes=[pltpu.VMEM((here, segs * lines, 128), F32)],
        name="expand",
        cost_estimate=pl.CostEstimate(flops=1 << 21, bytes_accessed=3 << 20, transcendentals=0),
    )(recv)


def on_device(signal, mic_axial, mic_azimuth, mode_m, mode_n, freq_bins):
    segs = lax.axis_size("mic")
    owners = lax.axis_size("mode")
    freqs = freq_bins.shape[0]
    own = freqs // owners
    code = mic_azimuth * AXIAL + mic_axial
    pairs = ([], [])
    for block in range(segs):
        for j in range(owners):
            source = block * owners + j
            pairs[0].append((source, (j + owners * (block % 2)) * owners + block // 2))
            pairs[1].append((source, (j + owners * (1 - block % 2)) * owners + block // 2))
    first = lax.ppermute(code, ("mic", "mode"), pairs[0])
    second = lax.ppermute(code, ("mic", "mode"), pairs[1])
    analysis = analysis_call(freq_bins, signal.shape[2])
    spectra = spectra_call(analysis, mode_m, mode_n, first, second, signal[0], owners)
    recv = lax.all_to_all(spectra, "mode", 0, 0, tiled=True)
    slots = solve_call(freq_bins, recv, segs)
    shape = slots.shape
    slots = lax.all_to_all(slots.reshape(segs * owners, *shape[2:]), ("mic", "mode"), 0, 0, tiled=True)
    amplitude, power, residual = expand_call(slots.reshape(shape), 2)
    modes = mode_m.shape[0]
    return (
        amplitude.reshape(freqs, 2, segs, modes),
        power,
        residual.reshape(own, 2, segs, residual.shape[2]),
    )


def solution(mesh):
    in_specs = (P("mic", "mode", None), P("mic"), P("mic"), P("mode"), P("mode"), P())
    out_specs = (P(None, None, None, "mode"), P(None, "mode"), P("mode", None, None, "mic"))
    return jax.shard_map(
        on_device, mesh=mesh, in_specs=in_specs, out_specs=out_specs, check_vma=False
    )
```

time: 1290 us -> 74.6 us (0.06)
  matrix products: 528 us -> 0 us
  waiting for transfers between devices: 219 us -> 2.9 us
  blocking collectives: 203 us -> 41.6 us
  loops' own time: 128 us -> 0 us
  local copies, waits for them, and re-layouts: 117 us -> 0.57 us
  other arithmetic: 62.5 us -> 0.7 us
  Pallas kernels: 0 us -> 19.9 us
  between operations: 14.3 us -> 0.65 us
    dot_general x129 -> x0, matrix products: 528 us -> none  [the longest x32 132 us: adjoint_product(): second = jnp.dot(stacked, imag_part, preferred_element_type=jnp.float32)]
    psum x2 -> x0, waiting for transfers between devices: 171 us -> none  [gradient_of(): gradient = lax.psum(partial_sum, 'mic')]
    psum x4 -> x0, blocking collectives: 163 us -> none  [the longest x2 135 us: on_device(): image_norm = lax.psum(padded, ('mic', 'mode'))]
    another operation x4 -> x0, loops' own time: 128 us -> none  [the longest x2 64.3 us: on_device(): lax.map(images_single, jnp.arange(freq_rows * lax.axis_size('mode'), dtyp...]
    dynamic_slice x162 -> x0, local copies, waits for them, and re-layouts: 75.4 us -> none  [the longest x96 37.9 us: gradients(): return lax.map(gradients_single, (row_index, residual_rows))]
    reduce_scatter x2 -> x0, waiting for transfers between devices: 41.5 us -> none  [on_device(): lax.psum_scatter(lax.map(images_single, jnp.arange(freq_rows * lax.axis_s...]
    mul x64 -> x0, other arithmetic: 41.5 us -> none  [mode_tile(): bin_value * (2 * NRAD - mode_n)]
    all_to_all x1 -> x2, blocking collectives: 10.4 us -> 41.6 us  [the longest x1 26.5 us: on_device(): lax.all_to_all(slots.reshape(segs * owners, *shape[2:]), ('mic', 'mode'),...]
  transfers between devices with their start and end apart: 5 -> 2, of which waited for: 5 -> 1; matrix products, arithmetic and copies ran while one was open for 0% -> 0% of each run, Pallas kernels for 0% -> 2%
where the time goes in v2:
time: 74.6 us; the launch traced here: 74.3 us
  blocking collectives  41.6 us (56%)
  Pallas kernels  19.9 us (27%)
  starting transfers between devices  7.9 us (11%)
  waiting for transfers between devices  2.9 us (4%)
    all_to_all x1, blocking collectives, on_device(): lax.all_to_all(slots.reshape(segs * owners, *shape[2:]), ('mic', 'mode'),...  26.5 us
    all_to_all x1, blocking collectives, on_device(): recv = lax.all_to_all(spectra, 'mode', 0, 0, tiled=True)  15.1 us
    pallas_call x1, Pallas kernels, solve_call(): pl.pallas_call(solve_kernel, in_specs=[SMEM, VMEM], out_specs=VMEM, out_s...  9.77 us
    ppermute x1, starting transfers between devices, on_device(): second = lax.ppermute(code, ('mic', 'mode'), pairs[1])  5.99 us
    pallas_call x1, Pallas kernels, spectra_call(): pl.pallas_call(spectra_kernel, grid=(steps,), in_specs=[VMEM, lo, hi, lo,...  4.97 us
    pallas_call x1, Pallas kernels, expand_call(): pl.pallas_call(expand_kernel, grid=(splits,), in_specs=[VMEM], out_specs=...  3.64 us
    ppermute x1, waiting for transfers between devices, on_device(): first = lax.ppermute(code, ('mic', 'mode'), pairs[0])  2.89 us
    ppermute x1, starting transfers between devices, on_device(): first = lax.ppermute(code, ('mic', 'mode'), pairs[0])  1.91 us
  transfers between devices with their start and end apart: 2, of which 1 were waited for; matrix products, arithmetic and copies ran while one was open for 0% of the time, Pallas kernels for 2%

profile of v2, /device:TPU:1, one launch (start us, length us, event | category | flops | bytes accessed | tf_op | source)
XLA Modules:
  0.0 74.3 jit_solution(15899660070184217281)
XLA Ops:
  0.6 0.7 multiply_add_fusion
  1.3 6.0 %collective-permute-start.1 = (s32[256]{0:T(256)S(1)}, s32[256]{0:T(256)S(1)}, u32[]{:S(2)}, u32[]{:S(2)}) collective-permute-start(s32[256]{0:T(256)S(1)} %multiply_add_fusion), channel_id=1, source_target_pairs={{0,64},{1,72},{2,80},{3,88},{4,96},{5,104},{6,112},{7,120},{8,0},{... | collective-permute-start | bytes 3080 | tf_op jit(solution)/shard_map/ppermute | solution.py:381
  7.3 1.9 %collective-permute-start = (s32[256]{0:T(256)S(1)}, s32[256]{0:T(256)S(1)}, u32[]{:S(2)}, u32[]{:S(2)}) collective-permute-start(s32[256]{0:T(256)S(1)} %multiply_add_fusion), channel_id=1, source_target_pairs={{0,0},{1,8},{2,16},{3,24},{4,32},{5,40},{6,48},{7,56},{8,64},{9,72... | collective-permute-start | bytes 3080 | tf_op jit(solution)/shard_map/ppermute | solution.py:380
  9.2 1.6 %analysis.1.analysis_ref = bf16[32,4096]{1,0:T(8,128)(2,1)} custom-call(s32[16]{0:T(128)} %freq_ref.3), custom_call_target="tpu_custom_call" | custom-call | flops 2097152 | bytes 262144 | tf_op jit(solution)/shard_map/analysis/pallas_call | solution.py:79
  10.8 0.0 collective-permute-done.1
  10.8 0.0 copy-start.1
  10.8 2.9 %collective-permute-done = s32[256]{0:T(256)S(1)} collective-permute-done((s32[256]{0:T(256)S(1)}, s32[256]{0:T(256)S(1)}, u32[]{:S(2)}, u32[]{:S(2)}) %collective-permute-start) | collective-permute-done | bytes 1056 | tf_op jit(solution)/shard_map/ppermute | solution.py:380
  13.7 0.0 copy-start.2
  13.7 0.0 copy-done.1
  13.7 0.6 copy-done.2
  14.3 0.0 copy-start
  14.3 5.0 %spectra.1 = f32[8,8,512]{2,1,0:T(8,128)} custom-call(bf16[32,4096]{1,0:T(8,128)(2,1)} %analysis.1.analysis_ref, s32[1,1024]{1,0:T(1,128)} %bitcast.12, s32[1,1024]{1,0:T(1,128)} %bitcast.13, s32[1,1024]{1,0:T(1,128)} %bitcast.14, s32[1,1024]{1,0:T(1,128)} %bitcast.15, s32[1,256]{1,0:T(1,128)} %bitcast.17, s32[1,256]{1,0:T(1,128)} %bitcast.16, ...), custom_call_target="tpu_custom_call" | custom-call | flops 134217728 | bytes 4194304 | tf_op jit(solution)/shard_map/spectra/pallas_call | solution.py:117
  19.2 15.1 %all_to_all.10.recv_ref = f32[8,8,512]{2,1,0:T(8,128)S(1)} all-to-all(f32[8,8,512]{2,1,0:T(8,128)} %spectra.1), channel_id=1, replica_groups=mesh['mic'=16,'mode'=8] {'mode'}, dimensions={0} | all-to-all | bytes 262144 | tf_op jit(solution)/shard_map/all_to_all | solution.py:384
  34.4 0.0 copy-done
  34.4 9.8 %solve.1 = bf16[16,8,40,128]{3,2,1,0:T(8,128)(2,1)S(1)} custom-call(s32[16]{0:T(128)S(1)} %copy-done, f32[8,8,512]{2,1,0:T(8,128)S(1)} %all_to_all.10.recv_ref), custom_call_target="tpu_custom_call" | custom-call | flops 1342177280 | bytes 8388608 | tf_op jit(solution)/shard_map/solve/pallas_call | solution.py:287
  44.1 26.5 %all_to_all.11 = bf16[128,40,128]{2,1,0:T(8,128)(2,1)} all-to-all(bf16[128,40,128]{2,1,0:T(8,128)(2,1)S(1)} %bitcast.9), channel_id=1, replica_groups=mesh['mic'=16,'mode'=8] {'mic','mode'}, dimensions={0} | all-to-all | bytes 2621440 | tf_op jit(solution)/shard_map/all_to_all | solution.py:387
  70.6 3.6 %expand.1 = (f32[32,16,1024]{2,1,0:T(8,128)}, f32[16,1024]{1,0:T(8,128)}, f32[4,16,256]{2,1,0:T(8,128)}) custom-call(bf16[16,8,40,128]{3,2,1,0:T(8,128)(2,1)} %bitcast.10), custom_call_target="tpu_custom_call" | custom-call | flops 2097152 | bytes 3145728 | tf_op jit(solution)/shard_map/expand/pallas_call | solution.py:348
Async XLA Ops:
  1.3 9.5 %collective-permute-start.1 = (s32[256]{0:T(256)S(1)}, s32[256]{0:T(256)S(1)}, u32[]{:S(2)}, u32[]{:S(2)}) collective-permute-start(s32[256]{0:T(256)S(1)} %multiply_add_fusion), channel_id=1, source_target_pairs={{0,64},{1,72},{2,80},{3,88},{4,96},{5,104},{6,112},{7,120},{8,0},{... | collective-permute-start | bytes 3080 | tf_op jit(solution)/shard_map/ppermute | solution.py:381
  7.3 6.4 %collective-permute-start = (s32[256]{0:T(256)S(1)}, s32[256]{0:T(256)S(1)}, u32[]{:S(2)}, u32[]{:S(2)}) collective-permute-start(s32[256]{0:T(256)S(1)} %multiply_add_fusion), channel_id=1, source_target_pairs={{0,0},{1,8},{2,16},{3,24},{4,32},{5,40},{6,48},{7,56},{8,64},{9,72... | collective-permute-start | bytes 3080 | tf_op jit(solution)/shard_map/ppermute | solution.py:380
  10.8 2.9 %copy-start.1 = (s32[256]{0:T(256)}, s32[256]{0:T(256)S(1)}, u32[]{:S(2)}) copy-start(s32[256]{0:T(256)S(1)} %collective-permute-done.1) | copy-start | bytes 3076
  13.7 0.6 copy-start.2
  14.3 20.1 %copy-start = (s32[16]{0:T(128)S(1)}, s32[16]{0:T(128)}, u32[]{:S(2)}) copy-start(s32[16]{0:T(128)} %freq_ref.3) | copy-start | bytes 196

commit v3 on v2

v3 whole, which is shorter than its diff:
```python
import jax
import jax.numpy as jnp
from jax import lax
from jax.experimental import pallas as pl
from jax.experimental.pallas import tpu as pltpu
from jax.sharding import PartitionSpec as P

ITERS = 2
AXIAL = 64
NRAD = 32
ORDERS = 256
HALF = ORDERS // 2
EPS = 1e-06
SIN_COEFS = (1.5707963200919937, -0.6459637612912833, 0.07968992686556589, -0.0046741574942986315, 0.0001516785309118288)
BF16 = jnp.bfloat16
F32 = jnp.float32
VMEM = pl.BlockSpec(memory_space=pltpu.VMEM)
SMEM = pl.BlockSpec(memory_space=pltpu.SMEM)


def cos_turns(turns):
    z = 1.0 - 4.0 * jnp.abs(turns - jnp.round(turns))
    square = z * z
    total = SIN_COEFS[-1] * square + SIN_COEFS[-2]
    for coef in SIN_COEFS[-3::-1]:
        total = total * square + coef
    return total * z


def sin_turns(turns):
    return cos_turns(turns - 0.25)


def turn_by(re, im, step_re, step_im):
    return re * step_re - im * step_im, re * step_im + im * step_re


def iota(shape, axis):
    return lax.broadcasted_iota(jnp.int32, shape, axis)


def nt_dot(a, b):
    return lax.dot_general(a, b, (((1,), (1,)), ((), ())), preferred_element_type=F32)


def groups(x):
    return x.reshape(x.shape[0] // 8, 8, x.shape[1])


def periodic(x):
    x = x + pltpu.roll(x, 4, 0)
    return x + pltpu.roll(x, 2, 0)


def codes_kernel(azimuth_ref, axial_ref, out_ref):
    code = azimuth_ref[...] * AXIAL + axial_ref[...]
    for copy in range(out_ref.shape[0]):
        out_ref[copy] = code


def codes_call(azimuth, axial, copies):
    mics = azimuth.shape[0]
    return pl.pallas_call(
        codes_kernel,
        in_specs=[VMEM] * 2,
        out_specs=VMEM,
        out_shape=jax.ShapeDtypeStruct((copies, 1, mics), jnp.int32),
        name="codes",
        cost_estimate=pl.CostEstimate(flops=1 << 10, bytes_accessed=1 << 14, transcendentals=0),
    )(azimuth.reshape(1, -1), axial.reshape(1, -1))


def spectra_kernel(freq_ref, m_ref, n_ref, signal_hbm, out_ref, analysis_ref, signal_ref, sems):
    pieces = sems.shape[0]
    tall = signal_ref.shape[0] // pieces
    copies = []
    for k in range(pieces):
        part = pl.ds(k * tall, tall)
        copies.append(pltpu.make_async_copy(signal_hbm.at[part], signal_ref.at[part], sems.at[k]))
        copies[-1].start()
    rows, seglen = analysis_ref.shape
    dests = out_ref.shape[0]
    freqs = rows // 2
    own = freqs // dests
    row = iota((freqs, 128), 0)
    freq = jnp.zeros((freqs, 128), jnp.int32)
    for f in range(freqs):
        freq = jnp.where(row == f, freq_ref[f], freq)
    freq = freq.astype(F32)
    lane = iota((freqs, 128), 1).astype(F32)
    start = freq * lane * (1.0 / seglen)
    step = freq * (128.0 / seglen)
    re, im = cos_turns(start), -sin_turns(start)
    step_re, step_im = cos_turns(step), -sin_turns(step)
    scale = (3.0 * seglen / 8.0) ** (-0.5)
    for block in range(seglen // 128):
        sample = iota((8, 128), 1).astype(F32) + block * 128.0
        window = (0.5 - 0.5 * cos_turns(sample * (1.0 / seglen)))[None] * scale
        at = slice(block * 128, (block + 1) * 128)
        analysis_ref[0:freqs, at] = (groups(re) * window).reshape(freqs, 128).astype(BF16)
        analysis_ref[freqs:, at] = (groups(im) * window).reshape(freqs, 128).astype(BF16)
        re, im = turn_by(re, im, step_re, step_im)

    mics = signal_ref.shape[0]
    m = m_ref[...]
    code = (jnp.where(m >= 0, m, HALF - 1 - m) * NRAD + n_ref[...]).astype(F32)
    tail = jnp.concatenate([code[:, :mics], code[:, mics:], jnp.zeros((2, mics), F32)], axis=0)
    for d in range(dests):
        out_ref[d, 2 * own :, :] = tail
    width = 128
    for block in range(mics // width):
        at = slice(block * width, (block + 1) * width)
        for k in range(block * width // tall, (block + 1) * width // tall):
            copies[k].wait()
        spectra = nt_dot(analysis_ref[...], signal_ref[at, :])
        for d in range(dests):
            out_ref[d, 0:own, at] = spectra[d * own : (d + 1) * own]
            out_ref[d, own : 2 * own, at] = spectra[freqs + d * own : freqs + (d + 1) * own]


def spectra_call(freq_bins, mode_m, mode_n, signal, dests):
    mics, seglen = signal.shape
    rows = 2 * freq_bins.shape[0]
    return pl.pallas_call(
        spectra_kernel,
        in_specs=[SMEM, VMEM, VMEM, pl.BlockSpec(memory_space=pltpu.HBM)],
        out_specs=VMEM,
        out_shape=jax.ShapeDtypeStruct((dests, 8, mics), F32),
        scratch_shapes=[
            pltpu.VMEM((rows, seglen), BF16),
            pltpu.VMEM((mics, seglen), BF16),
            pltpu.SemaphoreType.DMA((16,)),
        ],
        name="spectra",
        cost_estimate=pl.CostEstimate(flops=2 * rows * mics * seglen, bytes_accessed=mics * seglen * 2, transcendentals=0),
    )(freq_bins, mode_m.reshape(1, -1), mode_n.reshape(1, -1), signal)


def basis_kernel(freq_ref, code_ref, azim_ref, seed_ref):
    blocks, _, width = code_ref.shape
    chunks, _, per = azim_ref.shape
    base = 2 * lax.axis_index("mode")
    odd = (iota((8, width), 0) & 1) == 1
    freq = jnp.where(odd, freq_ref[base + 1], freq_ref[base]).astype(F32)
    row = iota((8, width), 0).astype(F32)
    radial = (iota((8, width), 0) >> 1).astype(F32)

    @pl.loop(0, chunks)
    def _(ch):
        for piece in range(per // width):
            at = slice(piece * width, (piece + 1) * width)
            code = jnp.broadcast_to(code_ref[ch * (per // width) + piece], (8, width))
            azimuth = (code >> 6).astype(F32)
            axial = (code & (AXIAL - 1)).astype(F32)
            turns = azimuth * (row + 0.5) * (1.0 / 512)
            re, im = cos_turns(turns), sin_turns(turns)
            turns = azimuth * (8.0 / 512)
            step_re, step_im = cos_turns(turns), sin_turns(turns)
            next_re, next_im = turn_by(re, im, step_re, step_im)
            step_re, step_im = turn_by(step_re, step_im, step_re, step_im)
            re = jnp.stack([re, next_re])
            im = jnp.stack([im, next_im])
            for a in range(HALF // 16):
                azim_ref[ch, 16 * a : 16 * a + 16, at] = re.reshape(16, width).astype(BF16)
                azim_ref[ch, HALF + 16 * a : HALF + 16 * a + 16, at] = im.reshape(16, width).astype(BF16)
                if a + 1 < HALF // 16:
                    re, im = turn_by(re, im, step_re[None], step_im[None])
            turns = (axial * freq * (2.0 * NRAD - radial) - azimuth * 32.0) * (1.0 / 32768)
            re, im = cos_turns(turns), sin_turns(turns)
            turns = axial * freq * (-4.0 / 32768)
            step_re, step_im = cos_turns(turns), sin_turns(turns)
            for k, value in enumerate((re, im, step_re, step_im)):
                seed_ref[ch, k, :, at] = value


def basis_call(freq_bins, codes, chunks):
    blocks, _, width = codes.shape
    per = blocks * width // chunks
    return pl.pallas_call(
        basis_kernel,
        in_specs=[SMEM, VMEM],
        out_specs=[VMEM] * 2,
        out_shape=[
            jax.ShapeDtypeStruct((chunks, ORDERS, per), BF16),
            jax.ShapeDtypeStruct((chunks, 4, 8, per), F32),
        ],
        compiler_params=pltpu.CompilerParams(vmem_limit_bytes=12 << 20),
        name="basis",
        cost_estimate=pl.CostEstimate(flops=40 * ORDERS * per * chunks, bytes_accessed=3 << 20, transcendentals=0),
    )(freq_bins, codes)


def solve_kernel(
    recv_ref, azim_ref, seed_ref, out_ref, rad_ref, res_ref, image_ref, field_ref, onehot_ref, dir_ref, grown_ref, rows_ref
):
    chunks, _, per = recv_ref.shape
    mics = chunks * per
    stack = 2 * NRAD
    odd = (iota((8, per), 0) & 1) == 1
    for ch in range(chunks):
        for c in range(2):
            res_ref[ch, c] = jnp.where(odd, recv_ref[ch, 2 * c + 1 : 2 * c + 2, :], recv_ref[ch, 2 * c : 2 * c + 1, :])

        re, im, step_re, step_im = (seed_ref[ch, k] for k in range(4))
        for a in range(stack // 8):
            rad_ref[ch, 0, 8 * a : 8 * a + 8] = re
            rad_ref[ch, 1, 8 * a : 8 * a + 8] = im
            if a + 1 < stack // 8:
                re, im = turn_by(re, im, step_re, step_im)

    order_rows = iota((ORDERS, 128), 0).astype(F32).astype(BF16)
    radial_rows = (iota((stack, 128), 0) >> 1).astype(F32).astype(BF16)
    one, zero = jnp.ones((), BF16), jnp.zeros((), BF16)
    counts = jnp.zeros((stack, ORDERS), F32)

    def modes_of(k):
        return jnp.concatenate([onehot_ref[k, q] for q in range(per // 128)], axis=1)

    for ch in range(chunks):
        for part in range(2):
            code = recv_ref[ch, 4 + part : 5 + part, :]
            order = jnp.floor(code * (1.0 / NRAD))
            radius = (code - order * NRAD).astype(BF16)
            order = order.astype(BF16)
            picks = []
            for q in range(per // 128):
                at = slice(q * 128, (q + 1) * 128)
                onehot_ref[2 * ch + part, q] = jnp.where(order_rows == order[:, at], one, zero)
                picks.append(jnp.where(radial_rows == radius[:, at], one, zero))
            counts = counts + nt_dot(jnp.concatenate(picks, axis=1), modes_of(2 * ch + part))

    weight = (mics ** (-0.5)) * lax.rsqrt(1.0 + (iota((stack, ORDERS), 0) >> 1).astype(F32))
    counts_weight = counts * weight

    def scaled(column, x):
        return (column[None] * groups(x)).reshape(x.shape)

    def row_sums(x):
        return periodic(jnp.sum(jnp.sum(groups(x), axis=0), axis=1, keepdims=True))

    def adjoint(advance):
        out = jnp.zeros((2 * stack, ORDERS), F32)
        for ch in range(chunks):
            re, im = advance(ch, 0)[None], advance(ch, 1)[None]
            ec, es = groups(rad_ref[ch, 0]), groups(rad_ref[ch, 1])
            field_ref[ch, 0:stack] = (re * ec + im * es).reshape(stack, per).astype(BF16)
            field_ref[ch, stack:] = (im * ec - re * es).reshape(stack, per).astype(BF16)
            out = out + nt_dot(field_ref[ch], azim_ref[ch])
        re, im = out[:stack], out[stack:]
        rc, rs, ic, ics = re[:, :HALF], re[:, HALF:], im[:, :HALF], im[:, HALF:]
        g_re = jnp.concatenate([rc + ics, rc - ics], axis=1) * weight
        g_im = jnp.concatenate([ic - rs, ic + rs], axis=1) * weight
        return g_re, g_im, row_sums(counts * (g_re * g_re + g_im * g_im))

    def forward():
        x_re, x_im = dir_ref[0] * counts_weight, dir_ref[1] * counts_weight
        p_re, m_re, p_im, m_im = x_re[:, :HALF], x_re[:, HALF:], x_im[:, :HALF], x_im[:, HALF:]
        rows_ref[0:stack] = jnp.concatenate([p_re + m_re, m_im - p_im], axis=1).astype(BF16)
        rows_ref[stack:] = jnp.concatenate([p_im + m_im, p_re - m_re], axis=1).astype(BF16)
        norm = jnp.zeros((8, per), F32)
        for ch in range(chunks):
            out = jnp.dot(rows_ref[...], azim_ref[ch], preferred_element_type=F32)
            t_re, t_im = out[:stack], out[stack:]
            ec, es = rad_ref[ch, 0], rad_ref[ch, 1]
            i_re = periodic(jnp.sum(groups(ec * t_re - es * t_im), axis=0))
            i_im = periodic(jnp.sum(groups(ec * t_im + es * t_re), axis=0))
            image_ref[ch, 0] = i_re
            image_ref[ch, 1] = i_im
            norm = norm + (i_re * i_re + i_im * i_im)
        return jnp.sum(norm, axis=1, keepdims=True)

    g_re, g_im, norm = adjoint(lambda ch, c: res_ref[ch, c])
    dir_ref[0] = g_re
    dir_ref[1] = g_im
    for sweep in range(ITERS):
        step = norm / (forward() + EPS)

        def advance(ch, c, step=step):
            value = res_ref[ch, c] - step * image_ref[ch, c]
            res_ref[ch, c] = value
            return value

        for c in range(2):
            grown = scaled(step, dir_ref[c])
            grown_ref[c] = grown if sweep == 0 else grown_ref[c] + grown
        if sweep + 1 < ITERS:
            g_re, g_im, next_norm = adjoint(advance)
            momentum = next_norm / (norm + EPS)
            dir_ref[0] = g_re + scaled(momentum, dir_ref[0])
            dir_ref[1] = g_im + scaled(momentum, dir_ref[1])
            norm = next_norm

    copies, _, lines, _ = out_ref.shape
    width = mics // copies
    upper = (iota((8, per), 0) & 2) == 0
    first = iota((8, 128), 0) < 4
    for ch in range(chunks):
        value = jnp.where(upper, advance(ch, 0), advance(ch, 1))
        for piece in range(per // width):
            left, right = value[:, piece * width : piece * width + 128], value[:, piece * width + 128 : (piece + 1) * width]
            packed = jnp.where(first, left, right).astype(BF16)
            for owner in range(chunks):
                out_ref[ch * (per // width) + piece, owner, lines - 8 :, :] = packed

    rows_ref[0:stack] = grown_ref[0].astype(BF16)
    rows_ref[stack:] = grown_ref[1].astype(BF16)
    radial_rows = (iota((stack, per), 0) >> 1).astype(F32)
    for ch in range(chunks):
        tiles = []
        for part in range(2):
            code = recv_ref[ch, 4 + part : 5 + part, :]
            radius = code - jnp.floor(code * (1.0 / NRAD)) * NRAD
            picked = jnp.dot(rows_ref[...], modes_of(2 * ch + part), preferred_element_type=F32)
            mask = radial_rows == radius
            re = periodic(jnp.sum(groups(jnp.where(mask, picked[:stack], 0.0)), axis=0))
            im = periodic(jnp.sum(groups(jnp.where(mask, picked[stack:], 0.0)), axis=0))
            value = jnp.where(upper, re, im)
            for q in range(0, per // 128, 2):
                tiles.append(jnp.where(first, value[:, q * 128 : (q + 1) * 128], value[:, (q + 1) * 128 : (q + 2) * 128]))
        packed = jnp.concatenate(tiles, axis=0).astype(BF16)
        for copy in range(copies):
            out_ref[copy, ch, 0 : lines - 8, :] = packed


def solve_call(recv, azim, seeds, copies):
    chunks, _, per = recv.shape
    modes, stack = 2 * chunks * per, 2 * NRAD
    return pl.pallas_call(
        solve_kernel,
        in_specs=[VMEM] * 3,
        out_specs=VMEM,
        out_shape=jax.ShapeDtypeStruct((copies, chunks, 4 * modes // chunks // 128 + 8, 128), BF16),
        scratch_shapes=[
            pltpu.VMEM((chunks, 2, stack, per), F32),
            pltpu.VMEM((chunks, 2, 8, per), F32),
            pltpu.VMEM((chunks, 2, 8, per), F32),
            pltpu.VMEM((chunks, 2 * stack, per), BF16),
            pltpu.VMEM((2 * chunks, per // 128, ORDERS, 128), BF16),
            pltpu.VMEM((2, stack, ORDERS), F32),
            pltpu.VMEM((2, stack, ORDERS), F32),
            pltpu.VMEM((2 * stack, ORDERS), BF16),
        ],
        compiler_params=pltpu.CompilerParams(vmem_limit_bytes=14 << 20),
        name="solve",
        cost_estimate=pl.CostEstimate(flops=10 * 256 * 4096 * 128, bytes_accessed=8 << 20, transcendentals=0),
    )(recv, azim, seeds)


def expand_kernel(in_ref, amp_ref, pow_ref, res_ref, wide_ref, ready_ref, sems):
    segs, dests, lines, _ = in_ref.shape
    rows = 4
    tiles = lines // 8
    copies = []
    for d in range(dests):
        for s in range(segs):
            for tile in range(tiles - 1):
                wide_ref[d % 2, tile, 8 * s : 8 * s + 8, :] = in_ref[s, d, 8 * tile : 8 * tile + 8, :].astype(F32)
        for kc in range(8 * (tiles - 1) // rows):
            at = slice(kc * 128, (kc + 1) * 128)
            for fl in range(rows // 2):
                power = jnp.zeros((segs, 128), F32)
                for c in range(2):
                    line = kc * rows + 2 * c + fl
                    value = wide_ref[d % 2, line // 8, pl.ds(line % 8, segs, stride=8), :]
                    ready_ref[d, 2 * fl + c, :, at] = value
                    power = power + value * value
                pow_ref[2 * d + fl : 2 * d + fl + 1, at] = jnp.sum(power, axis=0, keepdims=True) * (1.0 / segs)
        copies.append(pltpu.make_async_copy(ready_ref.at[d], amp_ref.at[pl.ds(d * rows, rows)], sems.at[d]))
        copies[-1].start()

    owner = lax.axis_index("mode")
    for s in range(segs):
        wide_ref[0, 0, 8 * s : 8 * s + 8, :] = in_ref[s, owner, 8 * (tiles - 1) :, :].astype(F32)
    for half in range(2):
        for fl in range(2):
            for c in range(2):
                line = half * rows + 2 * c + fl
                res_ref[2 * fl + c, :, half * 128 : (half + 1) * 128] = wide_ref[0, 0, pl.ds(line, segs, stride=8), :]
    for copy in copies:
        copy.wait()


def expand_call(recv):
    segs, dests, lines, _ = recv.shape
    rows = 4
    modes = (lines - 8) // rows * 128
    return pl.pallas_call(
        expand_kernel,
        in_specs=[VMEM],
        out_specs=[pl.BlockSpec(memory_space=pl.ANY), VMEM, VMEM],
        out_shape=[
            jax.ShapeDtypeStruct((dests * rows, segs, modes), F32),
            jax.ShapeDtypeStruct((dests * rows // 2, modes), F32),
            jax.ShapeDtypeStruct((rows, segs, 256), F32),
        ],
        scratch_shapes=[
            pltpu.VMEM((2, lines // 8 - 1, 8 * segs, 128), F32),
            pltpu.VMEM((dests, rows, segs, modes), F32),
            pltpu.SemaphoreType.DMA((dests,)),
        ],
        compiler_params=pltpu.CompilerParams(vmem_limit_bytes=12 << 20),
        name="expand",
        cost_estimate=pl.CostEstimate(flops=1 << 21, bytes_accessed=3 << 20, transcendentals=0),
    )(recv)


def on_device(signal, mic_axial, mic_azimuth, mode_m, mode_n, freq_bins):
    segs = lax.axis_size("mic")
    owners = lax.axis_size("mode")
    freqs = freq_bins.shape[0]
    own = freqs // owners
    codes = lax.all_to_all(codes_call(mic_azimuth, mic_axial, segs), "mic", 0, 0, tiled=True)
    spectra = spectra_call(freq_bins, mode_m, mode_n, signal[0], owners)
    recv = lax.all_to_all(spectra, "mode", 0, 0, tiled=True)
    azim, seeds = basis_call(freq_bins, codes, owners)
    slots = solve_call(recv, azim, seeds, segs)
    shape = slots.shape
    slots = lax.all_to_all(slots.reshape(segs * owners, *shape[2:]), ("mic", "mode"), 0, 0, tiled=True)
    amplitude, power, residual = expand_call(slots.reshape(shape))
    modes = mode_m.shape[0]
    return (
        amplitude.reshape(freqs, 2, segs, modes),
        power,
        residual.reshape(own, 2, segs, residual.shape[2]),
    )


def solution(mesh):
    in_specs = (P("mic", "mode", None), P("mic"), P("mic"), P("mode"), P("mode"), P())
    out_specs = (P(None, None, None, "mode"), P(None, "mode"), P("mode", None, None, "mic"))
    return jax.shard_map(
        on_device, mesh=mesh, in_specs=in_specs, out_specs=out_specs, check_vma=False
    )
```

time: 74.6 us -> 65.3 us (0.88)
  blocking collectives: 41.6 us -> 27.9 us
  starting transfers between devices: 7.9 us -> 15 us
  Pallas kernels: 19.9 us -> 16.9 us
  waiting for transfers between devices: 2.9 us -> 4.56 us
    all_to_all x1 -> x0, blocking collectives: 15.1 us -> none  [on_device(): recv = lax.all_to_all(spectra, 'mode', 0, 0, tiled=True)]
    all_to_all x0 -> x2, starting transfers between devices: none -> 15 us  [the longest x1 8.59 us: on_device(): lax.all_to_all(codes_call(mic_azimuth, mic_axial, segs), 'mic', 0, 0, til...]
    ppermute x2 -> x0, starting transfers between devices: 7.9 us -> none  [the longest x1 5.99 us: on_device(): second = lax.ppermute(code, ('mic', 'mode'), pairs[1])]
    all_to_all x0 -> x2, waiting for transfers between devices: none -> 4.56 us  [the longest x1 3.59 us: on_device(): recv = lax.all_to_all(spectra, 'mode', 0, 0, tiled=True)]
    pallas_call x4 -> x5, Pallas kernels: 19.9 us -> 16.9 us  [the longest x1 6.36 us: solve_call(): pl.pallas_call(solve_kernel, in_specs=[VMEM] * 3, out_specs=VMEM, out_sha...]
    ppermute x2 -> x0, waiting for transfers between devices: 2.9 us -> none  [the longest x1 2.89 us: on_device(): first = lax.ppermute(code, ('mic', 'mode'), pairs[0])]
    all_to_all x1, blocking collectives: 26.5 us -> 27.9 us  [on_device(): lax.all_to_all(slots.reshape(segs * owners, *shape[2:]), ('mic', 'mode'),...]
  transfers between devices with their start and end apart: 2 -> 2, of which waited for: 1 -> 2; matrix products, arithmetic and copies ran while one was open for 0% -> 0% of each run, Pallas kernels for 2% -> 11%
where the time goes in v3:
time: 65.3 us; the launch traced here: 65 us
  blocking collectives  27.9 us (43%)
  Pallas kernels  16.9 us (26%)
  starting transfers between devices  15 us (23%)
  waiting for transfers between devices  4.56 us (7%)
  between operations  0.67 us (1%)
    all_to_all x1, blocking collectives, on_device(): lax.all_to_all(slots.reshape(segs * owners, *shape[2:]), ('mic', 'mode'),...  27.9 us
    all_to_all x1, starting transfers between devices, on_device(): lax.all_to_all(codes_call(mic_azimuth, mic_axial, segs), 'mic', 0, 0, til...  8.59 us
    all_to_all x1, starting transfers between devices, on_device(): recv = lax.all_to_all(spectra, 'mode', 0, 0, tiled=True)  6.4 us
    pallas_call x1, Pallas kernels, solve_call(): pl.pallas_call(solve_kernel, in_specs=[VMEM] * 3, out_specs=VMEM, out_sha...  6.36 us
    pallas_call x1, Pallas kernels, spectra_call(): pl.pallas_call(spectra_kernel, in_specs=[SMEM, VMEM, VMEM, pl.BlockSpec(m...  5.45 us
    all_to_all x1, waiting for transfers between devices, on_device(): recv = lax.all_to_all(spectra, 'mode', 0, 0, tiled=True)  3.59 us
    pallas_call x1, Pallas kernels, expand_call(): pl.pallas_call(expand_kernel, in_specs=[VMEM], out_specs=[pl.BlockSpec(me...  2.1 us
    pallas_call x1, Pallas kernels, basis_call(): pl.pallas_call(basis_kernel, in_specs=[SMEM, VMEM], out_specs=[VMEM] * 2,...  1.64 us
  transfers between devices with their start and end apart: 2, of which 2 were waited for; matrix products, arithmetic and copies ran while one was open for 0% of the time, Pallas kernels for 11%

profile of v3, /device:TPU:1, one launch (start us, length us, event | category | flops | bytes accessed | tf_op | source)
XLA Modules:
  0.0 65.0 jit_solution(16779001037596749877)
XLA Ops:
  0.6 1.3 %codes.1 = s32[16,1,256]{2,1,0:T(1,128)} custom-call(s32[1,256]{1,0:T(1,128)} %bitcast.14, s32[1,256]{1,0:T(1,128)} %bitcast.15), custom_call_target="tpu_custom_call" | custom-call | flops 1024 | bytes 16384 | tf_op jit(solution)/shard_map/codes/pallas_call | solution.py:63
  1.9 8.6 %all-to-all-start.1 = ((s32[16,1,256]{2,1,0:T(1,128)}), s32[16,1,256]{2,1,0:T(1,128)S(1)}, u32[]{:S(2)}, u32[]{:S(2)}) async-start(s32[16,1,256]{2,1,0:T(1,128)} %codes.1), calls=%async_computation.1 | async-start | bytes 32768 | tf_op jit(solution)/shard_map/all_to_all | solution.py:412
  10.5 0.0 copy-start
  10.5 5.4 %spectra.1 = f32[8,8,512]{2,1,0:T(8,128)} custom-call(s32[16]{0:T(128)} %freq_ref.3, s32[1,1024]{1,0:T(1,128)} %bitcast.12, s32[1,1024]{1,0:T(1,128)} %bitcast.13, bf16[512,4096]{1,0:T(8,128)(2,1)} %bitcast.11), custom_call_target="tpu_custom_call" | custom-call | flops 134217728 | bytes 4194304 | tf_op jit(solution)/shard_map/spectra/pallas_call | solution.py:124
  16.0 1.0 %all-to-all-done.1.code_ref = s32[16,1,256]{2,1,0:T(1,128)S(1)} async-done(((s32[16,1,256]{2,1,0:T(1,128)}), s32[16,1,256]{2,1,0:T(1,128)S(1)}, u32[]{:S(2)}, u32[]{:S(2)}) %all-to-all-start.1) | async-done | bytes 16416 | tf_op jit(solution)/shard_map/all_to_all | solution.py:412
  17.0 6.4 %all-to-all-start = ((f32[8,8,512]{2,1,0:T(8,128)}), f32[8,8,512]{2,1,0:T(8,128)S(1)}, u32[]{:S(2)}, u32[]{:S(2)}) async-start(f32[8,8,512]{2,1,0:T(8,128)} %spectra.1), calls=%async_computation | async-start | bytes 262144 | tf_op jit(solution)/shard_map/all_to_all | solution.py:414
  23.4 0.0 copy-done
  23.4 1.6 %basis.1 = (bf16[8,256,512]{2,1,0:T(8,128)(2,1)S(1)}, f32[8,4,8,512]{3,2,1,0:T(8,128)S(1)}) custom-call(s32[16]{0:T(128)S(1)} %copy-done, s32[16,1,256]{2,1,0:T(1,128)S(1)} %all-to-all-done.1.code_ref), custom_call_target="tpu_custom_call" | custom-call | flops 41943040 | bytes 3145728 | tf_op jit(solution)/shard_map/basis/pallas_call | solution.py:179
  25.0 3.6 %all-to-all-done.recv_ref = f32[8,8,512]{2,1,0:T(8,128)S(1)} async-done(((f32[8,8,512]{2,1,0:T(8,128)}), f32[8,8,512]{2,1,0:T(8,128)S(1)}, u32[]{:S(2)}, u32[]{:S(2)}) %all-to-all-start) | async-done | bytes 131104 | tf_op jit(solution)/shard_map/all_to_all | solution.py:414
  28.6 6.4 %solve.1 = bf16[16,8,40,128]{3,2,1,0:T(8,128)(2,1)S(1)} custom-call(f32[8,8,512]{2,1,0:T(8,128)S(1)} %all-to-all-done.recv_ref, bf16[8,256,512]{2,1,0:T(8,128)(2,1)S(1)} %get-tuple-element.8.azim_ref, f32[8,4,8,512]{3,2,1,0:T(8,128)S(1)} %get-tuple-element.9.seed_ref), custom_call_target="tpu_custom_call" | custom-call | flops 1342177280 | bytes 8388608 | tf_op jit(solution)/shard_map/solve/pallas_call | solution.py:328
  35.0 27.9 %all_to_all.15 = bf16[128,40,128]{2,1,0:T(8,128)(2,1)S(1)} all-to-all(bf16[128,40,128]{2,1,0:T(8,128)(2,1)S(1)} %bitcast.10), channel_id=1, replica_groups=mesh['mic'=16,'mode'=8] {'mic','mode'}, dimensions={0} | all-to-all | bytes 2621440 | tf_op jit(solution)/shard_map/all_to_all | solution.py:418
  62.9 2.1 %expand.1 = (f32[32,16,1024]{2,1,0:T(8,128)}, f32[16,1024]{1,0:T(8,128)}, f32[4,16,256]{2,1,0:T(8,128)}) custom-call(bf16[16,8,40,128]{3,2,1,0:T(8,128)(2,1)S(1)} %bitcast.9), custom_call_target="tpu_custom_call" | custom-call | flops 2097152 | bytes 3145728 | tf_op jit(solution)/shard_map/expand/pallas_call | solution.py:387
Async XLA Ops:
  1.9 15.0 %all-to-all-start.1 = ((s32[16,1,256]{2,1,0:T(1,128)}), s32[16,1,256]{2,1,0:T(1,128)S(1)}, u32[]{:S(2)}, u32[]{:S(2)}) async-start(s32[16,1,256]{2,1,0:T(1,128)} %codes.1), calls=%async_computation.1 | async-start | bytes 32768 | tf_op jit(solution)/shard_map/all_to_all | solution.py:412
  10.5 12.8 %copy-start = (s32[16]{0:T(128)S(1)}, s32[16]{0:T(128)}, u32[]{:S(2)}) copy-start(s32[16]{0:T(128)} %freq_ref.3) | copy-start | bytes 196
  17.0 11.6 %all-to-all-start = ((f32[8,8,512]{2,1,0:T(8,128)}), f32[8,8,512]{2,1,0:T(8,128)S(1)}, u32[]{:S(2)}, u32[]{:S(2)}) async-start(f32[8,8,512]{2,1,0:T(8,128)} %spectra.1), calls=%async_computation | async-start | bytes 262144 | tf_op jit(solution)/shard_map/all_to_all | solution.py:414

commit v4 on v3

--- a/solution.py
+++ b/solution.py
@@ -16,6 +16,7 @@
 F32 = jnp.float32
 VMEM = pl.BlockSpec(memory_space=pltpu.VMEM)
 SMEM = pl.BlockSpec(memory_space=pltpu.SMEM)
+HBM = pl.BlockSpec(memory_space=pltpu.HBM)
 
 
 def cos_turns(turns):
@@ -52,32 +53,61 @@
     return x + pltpu.roll(x, 2, 0)
 
 
-def codes_kernel(azimuth_ref, axial_ref, out_ref):
+def codes_kernel(azimuth_hbm, axial_hbm, out_hbm, azimuth_ref, axial_ref, out_ref, sems):
+    loads = [
+        pltpu.make_async_copy(azimuth_hbm, azimuth_ref, sems.at[0]),
+        pltpu.make_async_copy(axial_hbm, axial_ref, sems.at[1]),
+    ]
+    for load in loads:
+        load.start()
+    for load in loads:
+        load.wait()
     code = azimuth_ref[...] * AXIAL + axial_ref[...]
     for copy in range(out_ref.shape[0]):
         out_ref[copy] = code
+    store = pltpu.make_async_copy(out_ref, out_hbm, sems.at[2])
+    store.start()
+    store.wait()
 
 
 def codes_call(azimuth, axial, copies):
     mics = azimuth.shape[0]
     return pl.pallas_call(
         codes_kernel,
-        in_specs=[VMEM] * 2,
-        out_specs=VMEM,
+        in_specs=[HBM] * 2,
+        out_specs=HBM,
         out_shape=jax.ShapeDtypeStruct((copies, 1, mics), jnp.int32),
+        scratch_shapes=[
+            pltpu.VMEM((1, mics), jnp.int32),
+            pltpu.VMEM((1, mics), jnp.int32),
+            pltpu.VMEM((copies, 1, mics), jnp.int32),
+            pltpu.SemaphoreType.DMA((3,)),
+        ],
         name="codes",
         cost_estimate=pl.CostEstimate(flops=1 << 10, bytes_accessed=1 << 14, transcendentals=0),
     )(azimuth.reshape(1, -1), axial.reshape(1, -1))
 
 
-def spectra_kernel(freq_ref, m_ref, n_ref, signal_hbm, out_ref, analysis_ref, signal_ref, sems):
+def spectra_kernel(
+    freq_hbm, m_hbm, n_hbm, signal_hbm, out_hbm, freq_ref, m_ref, n_ref, analysis_ref, signal_ref, out_ref, small_sems, sems, out_sems
+):
+    loads = [
+        pltpu.make_async_copy(freq_hbm, freq_ref, small_sems.at[0]),
+        pltpu.make_async_copy(m_hbm, m_ref, small_sems.at[1]),
+        pltpu.make_async_copy(n_hbm, n_ref, small_sems.at[2]),
+    ]
+    for load in loads:
+        load.start()
+    mics = signal_ref.shape[0]
     pieces = sems.shape[0]
-    tall = signal_ref.shape[0] // pieces
+    tall = mics // pieces
     copies = []
     for k in range(pieces):
         part = pl.ds(k * tall, tall)
         copies.append(pltpu.make_async_copy(signal_hbm.at[part], signal_ref.at[part], sems.at[k]))
         copies[-1].start()
+    for load in loads:
+        load.wait()
     rows, seglen = analysis_ref.shape
     dests = out_ref.shape[0]
     freqs = rows // 2
@@ -101,13 +131,13 @@
         analysis_ref[freqs:, at] = (groups(im) * window).reshape(freqs, 128).astype(BF16)
         re, im = turn_by(re, im, step_re, step_im)
 
-    mics = signal_ref.shape[0]
     m = m_ref[...]
     code = (jnp.where(m >= 0, m, HALF - 1 - m) * NRAD + n_ref[...]).astype(F32)
     tail = jnp.concatenate([code[:, :mics], code[:, mics:], jnp.zeros((2, mics), F32)], axis=0)
     for d in range(dests):
         out_ref[d, 2 * own :, :] = tail
     width = 128
+    stores = []
     for block in range(mics // width):
         at = slice(block * width, (block + 1) * width)
         for k in range(block * width // tall, (block + 1) * width // tall):
@@ -116,20 +146,32 @@
         for d in range(dests):
             out_ref[d, 0:own, at] = spectra[d * own : (d + 1) * own]
             out_ref[d, own : 2 * own, at] = spectra[freqs + d * own : freqs + (d + 1) * own]
+        part = pl.ds(block * width, width)
+        stores.append(pltpu.make_async_copy(out_ref.at[:, :, part], out_hbm.at[:, :, part], out_sems.at[block]))
+        stores[-1].start()
+    for store in stores:
+        store.wait()
 
 
 def spectra_call(freq_bins, mode_m, mode_n, signal, dests):
     mics, seglen = signal.shape
+    modes = mode_m.shape[0]
     rows = 2 * freq_bins.shape[0]
     return pl.pallas_call(
         spectra_kernel,
-        in_specs=[SMEM, VMEM, VMEM, pl.BlockSpec(memory_space=pltpu.HBM)],
-        out_specs=VMEM,
+        in_specs=[HBM] * 4,
+        out_specs=HBM,
         out_shape=jax.ShapeDtypeStruct((dests, 8, mics), F32),
         scratch_shapes=[
+            pltpu.SMEM(freq_bins.shape, jnp.int32),
+            pltpu.VMEM((1, modes), jnp.int32),
+            pltpu.VMEM((1, modes), jnp.int32),
             pltpu.VMEM((rows, seglen), BF16),
             pltpu.VMEM((mics, seglen), BF16),
-            pltpu.SemaphoreType.DMA((16,)),
+            pltpu.VMEM((dests, 8, mics), F32),
+            pltpu.SemaphoreType.DMA((3,)),
+            pltpu.SemaphoreType.DMA((mics // 32,)),
+            pltpu.SemaphoreType.DMA((mics // 128,)),
         ],
         name="spectra",
         cost_estimate=pl.CostEstimate(flops=2 * rows * mics * seglen, bytes_accessed=mics * seglen * 2, transcendentals=0),
@@ -346,11 +388,20 @@
     )(recv, azim, seeds)
 
 
-def expand_kernel(in_ref, amp_ref, pow_ref, res_ref, wide_ref, ready_ref, sems):
+def expand_kernel(in_ref, amp_hbm, pow_hbm, res_hbm, wide_ref, ready_ref, pow_ref, res_ref, sems):
     segs, dests, lines, _ = in_ref.shape
     rows = 4
     tiles = lines // 8
-    copies = []
+    owner = lax.axis_index("mode")
+    for s in range(segs):
+        wide_ref[1, 0, 8 * s : 8 * s + 8, :] = in_ref[s, owner, 8 * (tiles - 1) :, :].astype(F32)
+    for half in range(2):
+        for fl in range(2):
+            for c in range(2):
+                line = half * rows + 2 * c + fl
+                res_ref[2 * fl + c, :, half * 128 : (half + 1) * 128] = wide_ref[1, 0, pl.ds(line, segs, stride=8), :]
+    copies = [pltpu.make_async_copy(res_ref, res_hbm, sems.at[dests])]
+    copies[-1].start()
     for d in range(dests):
         for s in range(segs):
             for tile in range(tiles - 1):
@@ -365,17 +416,10 @@
                     ready_ref[d, 2 * fl + c, :, at] = value
                     power = power + value * value
                 pow_ref[2 * d + fl : 2 * d + fl + 1, at] = jnp.sum(power, axis=0, keepdims=True) * (1.0 / segs)
-        copies.append(pltpu.make_async_copy(ready_ref.at[d], amp_ref.at[pl.ds(d * rows, rows)], sems.at[d]))
+        copies.append(pltpu.make_async_copy(ready_ref.at[d], amp_hbm.at[pl.ds(d * rows, rows)], sems.at[d]))
         copies[-1].start()
-
-    owner = lax.axis_index("mode")
-    for s in range(segs):
-        wide_ref[0, 0, 8 * s : 8 * s + 8, :] = in_ref[s, owner, 8 * (tiles - 1) :, :].astype(F32)
-    for half in range(2):
-        for fl in range(2):
-            for c in range(2):
-                line = half * rows + 2 * c + fl
-                res_ref[2 * fl + c, :, half * 128 : (half + 1) * 128] = wide_ref[0, 0, pl.ds(line, segs, stride=8), :]
+    copies.append(pltpu.make_async_copy(pow_ref, pow_hbm, sems.at[dests + 1]))
+    copies[-1].start()
     for copy in copies:
         copy.wait()
 
@@ -387,7 +431,7 @@
     return pl.pallas_call(
         expand_kernel,
         in_specs=[VMEM],
-        out_specs=[pl.BlockSpec(memory_space=pl.ANY), VMEM, VMEM],
+        out_specs=[HBM] * 3,
         out_shape=[
             jax.ShapeDtypeStruct((dests * rows, segs, modes), F32),
             jax.ShapeDtypeStruct((dests * rows // 2, modes), F32),
@@ -396,7 +440,9 @@
         scratch_shapes=[
             pltpu.VMEM((2, lines // 8 - 1, 8 * segs, 128), F32),
             pltpu.VMEM((dests, rows, segs, modes), F32),
-            pltpu.SemaphoreType.DMA((dests,)),
+            pltpu.VMEM((dests * rows // 2, modes), F32),
+            pltpu.VMEM((rows, segs, 256), F32),
+            pltpu.SemaphoreType.DMA((dests + 2,)),
         ],
         compiler_params=pltpu.CompilerParams(vmem_limit_bytes=12 << 20),
         name="expand",

time: 65.3 us -> 64.9 us (level)
  no operation moved by 1% of the time
where the time goes in v4:
time: 64.9 us; the launch traced here: 64.6 us
  blocking collectives  28 us (43%)
  Pallas kernels  16.4 us (25%)
  starting transfers between devices  15 us (23%)
  waiting for transfers between devices  4.44 us (7%)
  between operations  0.68 us (1%)
    all_to_all x1, blocking collectives, on_device(): lax.all_to_all(slots.reshape(segs * owners, *shape[2:]), ('mic', 'mode'),...  28 us
    all_to_all x1, starting transfers between devices, on_device(): lax.all_to_all(codes_call(mic_azimuth, mic_axial, segs), 'mic', 0, 0, til...  8.6 us
    all_to_all x1, starting transfers between devices, on_device(): recv = lax.all_to_all(spectra, 'mode', 0, 0, tiled=True)  6.4 us
    pallas_call x1, Pallas kernels, solve_call(): pl.pallas_call(solve_kernel, in_specs=[VMEM] * 3, out_specs=VMEM, out_sha...  6.36 us
    pallas_call x1, Pallas kernels, spectra_call(): pl.pallas_call(spectra_kernel, in_specs=[HBM] * 4, out_specs=HBM, out_sha...  5.57 us
    all_to_all x1, waiting for transfers between devices, on_device(): recv = lax.all_to_all(spectra, 'mode', 0, 0, tiled=True)  3.59 us
    pallas_call x1, Pallas kernels, basis_call(): pl.pallas_call(basis_kernel, in_specs=[SMEM, VMEM], out_specs=[VMEM] * 2,...  1.64 us
    pallas_call x1, Pallas kernels, expand_call(): pl.pallas_call(expand_kernel, in_specs=[VMEM], out_specs=[HBM] * 3, out_s...  1.5 us
  transfers between devices with their start and end apart: 2, of which 2 were waited for; matrix products, arithmetic and copies ran while one was open for 0% of the time, Pallas kernels for 11%

profile of v4, /device:TPU:1, one launch (start us, length us, event | category | flops | bytes accessed | tf_op | source)
XLA Modules:
  0.0 64.6 jit_solution(1607498731606464339)
XLA Ops:
  0.6 1.3 %codes.1 = s32[16,1,256]{2,1,0:T(1,128)} custom-call(s32[1,256]{1,0:T(1,128)} %bitcast.14, s32[1,256]{1,0:T(1,128)} %bitcast.15), custom_call_target="tpu_custom_call" | custom-call | flops 1024 | bytes 16384 | tf_op jit(solution)/shard_map/codes/pallas_call | solution.py:75
  2.0 8.6 %all-to-all-start.1 = ((s32[16,1,256]{2,1,0:T(1,128)}), s32[16,1,256]{2,1,0:T(1,128)S(1)}, u32[]{:S(2)}, u32[]{:S(2)}) async-start(s32[16,1,256]{2,1,0:T(1,128)} %codes.1), calls=%async_computation.1 | async-start | bytes 32768 | tf_op jit(solution)/shard_map/all_to_all | solution.py:458
  10.6 0.0 copy-start
  10.6 5.6 %spectra.1 = f32[8,8,512]{2,1,0:T(8,128)} custom-call(s32[16]{0:T(128)} %freq_ref.1, s32[1,1024]{1,0:T(1,128)} %bitcast.12, s32[1,1024]{1,0:T(1,128)} %bitcast.13, bf16[512,4096]{1,0:T(8,128)(2,1)} %bitcast.11), custom_call_target="tpu_custom_call" | custom-call | flops 134217728 | bytes 4194304 | tf_op jit(solution)/shard_map/spectra/pallas_call | solution.py:160
  16.2 0.9 %all-to-all-done.1.code_ref = s32[16,1,256]{2,1,0:T(1,128)S(1)} async-done(((s32[16,1,256]{2,1,0:T(1,128)}), s32[16,1,256]{2,1,0:T(1,128)S(1)}, u32[]{:S(2)}, u32[]{:S(2)}) %all-to-all-start.1) | async-done | bytes 16416 | tf_op jit(solution)/shard_map/all_to_all | solution.py:458
  17.0 6.4 %all-to-all-start = ((f32[8,8,512]{2,1,0:T(8,128)}), f32[8,8,512]{2,1,0:T(8,128)S(1)}, u32[]{:S(2)}, u32[]{:S(2)}) async-start(f32[8,8,512]{2,1,0:T(8,128)} %spectra.1), calls=%async_computation | async-start | bytes 262144 | tf_op jit(solution)/shard_map/all_to_all | solution.py:460
  23.4 0.0 copy-done
  23.4 1.6 %basis.1 = (bf16[8,256,512]{2,1,0:T(8,128)(2,1)S(1)}, f32[8,4,8,512]{3,2,1,0:T(8,128)S(1)}) custom-call(s32[16]{0:T(128)S(1)} %copy-done, s32[16,1,256]{2,1,0:T(1,128)S(1)} %all-to-all-done.1.code_ref), custom_call_target="tpu_custom_call" | custom-call | flops 41943040 | bytes 3145728 | tf_op jit(solution)/shard_map/basis/pallas_call | solution.py:221
  25.1 3.6 %all-to-all-done.recv_ref = f32[8,8,512]{2,1,0:T(8,128)S(1)} async-done(((f32[8,8,512]{2,1,0:T(8,128)}), f32[8,8,512]{2,1,0:T(8,128)S(1)}, u32[]{:S(2)}, u32[]{:S(2)}) %all-to-all-start) | async-done | bytes 131104 | tf_op jit(solution)/shard_map/all_to_all | solution.py:460
  28.7 6.4 %solve.1 = bf16[16,8,40,128]{3,2,1,0:T(8,128)(2,1)S(1)} custom-call(f32[8,8,512]{2,1,0:T(8,128)S(1)} %all-to-all-done.recv_ref, bf16[8,256,512]{2,1,0:T(8,128)(2,1)S(1)} %get-tuple-element.8.azim_ref, f32[8,4,8,512]{3,2,1,0:T(8,128)S(1)} %get-tuple-element.9.seed_ref), custom_call_target="tpu_custom_call" | custom-call | flops 1342177280 | bytes 8388608 | tf_op jit(solution)/shard_map/solve/pallas_call | solution.py:370
  35.0 28.0 %all_to_all.15 = bf16[128,40,128]{2,1,0:T(8,128)(2,1)S(1)} all-to-all(bf16[128,40,128]{2,1,0:T(8,128)(2,1)S(1)} %bitcast.10), channel_id=1, replica_groups=mesh['mic'=16,'mode'=8] {'mic','mode'}, dimensions={0} | all-to-all | bytes 2621440 | tf_op jit(solution)/shard_map/all_to_all | solution.py:464
  63.1 1.5 %expand.1 = (f32[32,16,1024]{2,1,0:T(8,128)}, f32[16,1024]{1,0:T(8,128)}, f32[4,16,256]{2,1,0:T(8,128)}) custom-call(bf16[16,8,40,128]{3,2,1,0:T(8,128)(2,1)S(1)} %bitcast.9), custom_call_target="tpu_custom_call" | custom-call | flops 2097152 | bytes 3145728 | tf_op jit(solution)/shard_map/expand/pallas_call | solution.py:431
Async XLA Ops:
  2.0 15.0 %all-to-all-start.1 = ((s32[16,1,256]{2,1,0:T(1,128)}), s32[16,1,256]{2,1,0:T(1,128)S(1)}, u32[]{:S(2)}, u32[]{:S(2)}) async-start(s32[16,1,256]{2,1,0:T(1,128)} %codes.1), calls=%async_computation.1 | async-start | bytes 32768 | tf_op jit(solution)/shard_map/all_to_all | solution.py:458
  10.6 12.8 %copy-start = (s32[16]{0:T(128)S(1)}, s32[16]{0:T(128)}, u32[]{:S(2)}) copy-start(s32[16]{0:T(128)} %freq_ref.1) | copy-start | bytes 196
  17.0 11.6 %all-to-all-start = ((f32[8,8,512]{2,1,0:T(8,128)}), f32[8,8,512]{2,1,0:T(8,128)S(1)}, u32[]{:S(2)}, u32[]{:S(2)}) async-start(f32[8,8,512]{2,1,0:T(8,128)} %spectra.1), calls=%async_computation | async-start | bytes 262144 | tf_op jit(solution)/shard_map/all_to_all | solution.py:460

commit v5 on v4

--- a/solution.py
+++ b/solution.py
@@ -89,7 +89,7 @@
 
 
 def spectra_kernel(
-    freq_hbm, m_hbm, n_hbm, signal_hbm, out_hbm, freq_ref, m_ref, n_ref, analysis_ref, signal_ref, out_ref, small_sems, sems, out_sems
+    freq_hbm, m_hbm, n_hbm, signal_hbm, out_ref, freq_ref, m_ref, n_ref, analysis_ref, signal_ref, small_sems, sems
 ):
     loads = [
         pltpu.make_async_copy(freq_hbm, freq_ref, small_sems.at[0]),
@@ -98,13 +98,10 @@
     ]
     for load in loads:
         load.start()
-    mics = signal_ref.shape[0]
-    pieces = sems.shape[0]
-    tall = mics // pieces
+    pieces, mics, span = signal_ref.shape
     copies = []
     for k in range(pieces):
-        part = pl.ds(k * tall, tall)
-        copies.append(pltpu.make_async_copy(signal_hbm.at[part], signal_ref.at[part], sems.at[k]))
+        copies.append(pltpu.make_async_copy(signal_hbm.at[:, pl.ds(k * span, span)], signal_ref.at[k], sems.at[k]))
         copies[-1].start()
     for load in loads:
         load.wait()
@@ -136,21 +133,13 @@
     tail = jnp.concatenate([code[:, :mics], code[:, mics:], jnp.zeros((2, mics), F32)], axis=0)
     for d in range(dests):
         out_ref[d, 2 * own :, :] = tail
-    width = 128
-    stores = []
-    for block in range(mics // width):
-        at = slice(block * width, (block + 1) * width)
-        for k in range(block * width // tall, (block + 1) * width // tall):
-            copies[k].wait()
-        spectra = nt_dot(analysis_ref[...], signal_ref[at, :])
-        for d in range(dests):
-            out_ref[d, 0:own, at] = spectra[d * own : (d + 1) * own]
-            out_ref[d, own : 2 * own, at] = spectra[freqs + d * own : freqs + (d + 1) * own]
-        part = pl.ds(block * width, width)
-        stores.append(pltpu.make_async_copy(out_ref.at[:, :, part], out_hbm.at[:, :, part], out_sems.at[block]))
-        stores[-1].start()
-    for store in stores:
-        store.wait()
+    spectra = jnp.zeros((rows, mics), F32)
+    for k in range(pieces):
+        copies[k].wait()
+        spectra = spectra + nt_dot(analysis_ref[:, k * span : (k + 1) * span], signal_ref[k])
+    for d in range(dests):
+        out_ref[d, 0:own, :] = spectra[d * own : (d + 1) * own]
+        out_ref[d, own : 2 * own, :] = spectra[freqs + d * own : freqs + (d + 1) * own]
 
 
 def spectra_call(freq_bins, mode_m, mode_n, signal, dests):
@@ -160,18 +149,16 @@
     return pl.pallas_call(
         spectra_kernel,
         in_specs=[HBM] * 4,
-        out_specs=HBM,
+        out_specs=VMEM,
         out_shape=jax.ShapeDtypeStruct((dests, 8, mics), F32),
         scratch_shapes=[
             pltpu.SMEM(freq_bins.shape, jnp.int32),
             pltpu.VMEM((1, modes), jnp.int32),
             pltpu.VMEM((1, modes), jnp.int32),
             pltpu.VMEM((rows, seglen), BF16),
-            pltpu.VMEM((mics, seglen), BF16),
-            pltpu.VMEM((dests, 8, mics), F32),
+            pltpu.VMEM((8, mics, seglen // 8), BF16),
             pltpu.SemaphoreType.DMA((3,)),
-            pltpu.SemaphoreType.DMA((mics // 32,)),
-            pltpu.SemaphoreType.DMA((mics // 128,)),
+            pltpu.SemaphoreType.DMA((8,)),
         ],
         name="spectra",
         cost_estimate=pl.CostEstimate(flops=2 * rows * mics * seglen, bytes_accessed=mics * seglen * 2, transcendentals=0),
@@ -233,7 +220,7 @@
 
 
 def solve_kernel(
-    recv_ref, azim_ref, seed_ref, out_ref, rad_ref, res_ref, image_ref, field_ref, onehot_ref, dir_ref, grown_ref, rows_ref
+    recv_ref, azim_ref, seed_ref, out_ref, rad_ref, res_ref, image_ref, field_ref, onehot_ref, dir_ref, grown_ref, rows_ref, pick_ref
 ):
     chunks, _, per = recv_ref.shape
     mics = chunks * per
@@ -250,26 +237,32 @@
             if a + 1 < stack // 8:
                 re, im = turn_by(re, im, step_re, step_im)
 
-    order_rows = iota((ORDERS, 128), 0).astype(F32).astype(BF16)
-    radial_rows = (iota((stack, 128), 0) >> 1).astype(F32).astype(BF16)
+    low_rows = iota((HALF, 128), 0).astype(F32).astype(BF16)
+    high_rows = (iota((2 * stack, 128), 0) >> 1).astype(F32).astype(BF16)
     one, zero = jnp.ones((), BF16), jnp.zeros((), BF16)
-    counts = jnp.zeros((stack, ORDERS), F32)
+    counts = jnp.zeros((2 * stack, HALF), F32)
+
+    def split_code(ch, part):
+        code = recv_ref[ch, 4 + part : 5 + part, :]
+        order = jnp.floor(code * (1.0 / NRAD))
+        upper = order >= HALF
+        return code - order * NRAD, jnp.where(upper, order - HALF, order), upper
 
     def modes_of(k):
         return jnp.concatenate([onehot_ref[k, q] for q in range(per // 128)], axis=1)
 
     for ch in range(chunks):
         for part in range(2):
-            code = recv_ref[ch, 4 + part : 5 + part, :]
-            order = jnp.floor(code * (1.0 / NRAD))
-            radius = (code - order * NRAD).astype(BF16)
-            order = order.astype(BF16)
+            radius, low, upper = split_code(ch, part)
+            high = jnp.where(upper, radius + NRAD, radius).astype(BF16)
+            low = low.astype(BF16)
             picks = []
             for q in range(per // 128):
                 at = slice(q * 128, (q + 1) * 128)
-                onehot_ref[2 * ch + part, q] = jnp.where(order_rows == order[:, at], one, zero)
-                picks.append(jnp.where(radial_rows == radius[:, at], one, zero))
+                onehot_ref[2 * ch + part, q] = jnp.where(low_rows == low[:, at], one, zero)
+                picks.append(jnp.where(high_rows == high[:, at], one, zero))
             counts = counts + nt_dot(jnp.concatenate(picks, axis=1), modes_of(2 * ch + part))
+    counts = jnp.concatenate([counts[:stack], counts[stack:]], axis=1)
 
     weight = (mics ** (-0.5)) * lax.rsqrt(1.0 + (iota((stack, ORDERS), 0) >> 1).astype(F32))
     counts_weight = counts * weight
@@ -344,18 +337,24 @@
             for owner in range(chunks):
                 out_ref[ch * (per // width) + piece, owner, lines - 8 :, :] = packed
 
-    rows_ref[0:stack] = grown_ref[0].astype(BF16)
-    rows_ref[stack:] = grown_ref[1].astype(BF16)
+    for c in range(2):
+        for half in range(2):
+            begin = (2 * c + half) * stack
+            pick_ref[begin : begin + stack] = grown_ref[c, :, half * HALF : (half + 1) * HALF].astype(BF16)
     radial_rows = (iota((stack, per), 0) >> 1).astype(F32)
     for ch in range(chunks):
         tiles = []
         for part in range(2):
-            code = recv_ref[ch, 4 + part : 5 + part, :]
-            radius = code - jnp.floor(code * (1.0 / NRAD)) * NRAD
-            picked = jnp.dot(rows_ref[...], modes_of(2 * ch + part), preferred_element_type=F32)
+            radius, _, minus = split_code(ch, part)
+            picked = jnp.dot(pick_ref[...], modes_of(2 * ch + part), preferred_element_type=F32)
             mask = radial_rows == radius
-            re = periodic(jnp.sum(groups(jnp.where(mask, picked[:stack], 0.0)), axis=0))
-            im = periodic(jnp.sum(groups(jnp.where(mask, picked[stack:], 0.0)), axis=0))
+            sides = []
+            for c in range(2):
+                plus_rows = picked[2 * c * stack : (2 * c + 1) * stack]
+                minus_rows = picked[(2 * c + 1) * stack : (2 * c + 2) * stack]
+                side = jnp.where(mask, jnp.where(minus, minus_rows, plus_rows), 0.0)
+                sides.append(periodic(jnp.sum(groups(side), axis=0)))
+            re, im = sides
             value = jnp.where(upper, re, im)
             for q in range(0, per // 128, 2):
                 tiles.append(jnp.where(first, value[:, q * 128 : (q + 1) * 128], value[:, (q + 1) * 128 : (q + 2) * 128]))
@@ -377,10 +376,11 @@
             pltpu.VMEM((chunks, 2, 8, per), F32),
             pltpu.VMEM((chunks, 2, 8, per), F32),
             pltpu.VMEM((chunks, 2 * stack, per), BF16),
-            pltpu.VMEM((2 * chunks, per // 128, ORDERS, 128), BF16),
+            pltpu.VMEM((2 * chunks, per // 128, HALF, 128), BF16),
             pltpu.VMEM((2, stack, ORDERS), F32),
             pltpu.VMEM((2, stack, ORDERS), F32),
             pltpu.VMEM((2 * stack, ORDERS), BF16),
+            pltpu.VMEM((4 * stack, HALF), BF16),
         ],
         compiler_params=pltpu.CompilerParams(vmem_limit_bytes=14 << 20),
         name="solve",

time: 64.9 us -> 63.2 us (0.974)
  Pallas kernels: 16.4 us -> 14.7 us
  waiting for transfers between devices: 4.44 us -> 5.76 us
  blocking collectives: 28 us -> 26.7 us
    pallas_call x1, Pallas kernels: 5.57 us -> 4.25 us  [spectra_call(): pl.pallas_call(spectra_kernel, in_specs=[HBM] * 4, out_specs=VMEM, out_sh...]
    all_to_all x1, waiting for transfers between devices: 0.85 us -> 2.17 us  [on_device(): lax.all_to_all(codes_call(mic_azimuth, mic_axial, segs), 'mic', 0, 0, til...]
    all_to_all x1, blocking collectives: 28 us -> 26.7 us  [on_device(): lax.all_to_all(slots.reshape(segs * owners, *shape[2:]), ('mic', 'mode'),...]
  transfers between devices with their start and end apart: 2 -> 2, of which waited for: 2 -> 2; matrix products, arithmetic and copies ran while one was open for 0% -> 0% of each run, Pallas kernels for 11% -> 9%
where the time goes in v5:
time: 63.2 us; the launch traced here: 62.9 us
  blocking collectives  26.7 us (42%)
  starting transfers between devices  15 us (24%)
  Pallas kernels  14.7 us (23%)
  waiting for transfers between devices  5.76 us (9%)
  between operations  0.68 us (1%)
    all_to_all x1, blocking collectives, on_device(): lax.all_to_all(slots.reshape(segs * owners, *shape[2:]), ('mic', 'mode'),...  26.7 us
    all_to_all x1, starting transfers between devices, on_device(): lax.all_to_all(codes_call(mic_azimuth, mic_axial, segs), 'mic', 0, 0, til...  8.6 us
    all_to_all x1, starting transfers between devices, on_device(): recv = lax.all_to_all(spectra, 'mode', 0, 0, tiled=True)  6.4 us
    pallas_call x1, Pallas kernels, solve_call(): pl.pallas_call(solve_kernel, in_specs=[VMEM] * 3, out_specs=VMEM, out_sha...  6 us
    pallas_call x1, Pallas kernels, spectra_call(): pl.pallas_call(spectra_kernel, in_specs=[HBM] * 4, out_specs=VMEM, out_sh...  4.25 us
    all_to_all x1, waiting for transfers between devices, on_device(): recv = lax.all_to_all(spectra, 'mode', 0, 0, tiled=True)  3.59 us
    all_to_all x1, waiting for transfers between devices, on_device(): lax.all_to_all(codes_call(mic_azimuth, mic_axial, segs), 'mic', 0, 0, til...  2.17 us
    pallas_call x1, Pallas kernels, basis_call(): pl.pallas_call(basis_kernel, in_specs=[SMEM, VMEM], out_specs=[VMEM] * 2,...  1.64 us
  transfers between devices with their start and end apart: 2, of which 2 were waited for; matrix products, arithmetic and copies ran while one was open for 0% of the time, Pallas kernels for 9%

profile of v5, /device:TPU:1, one launch (start us, length us, event | category | flops | bytes accessed | tf_op | source)
XLA Modules:
  0.0 62.9 jit_solution(3977225955089869498)
XLA Ops:
  0.6 1.3 %codes.1 = s32[16,1,256]{2,1,0:T(1,128)} custom-call(s32[1,256]{1,0:T(1,128)} %bitcast.14, s32[1,256]{1,0:T(1,128)} %bitcast.15), custom_call_target="tpu_custom_call" | custom-call | flops 1024 | bytes 16384 | tf_op jit(solution)/shard_map/codes/pallas_call | solution.py:75
  2.0 8.6 %all-to-all-start.1 = ((s32[16,1,256]{2,1,0:T(1,128)}), s32[16,1,256]{2,1,0:T(1,128)S(1)}, u32[]{:S(2)}, u32[]{:S(2)}) async-start(s32[16,1,256]{2,1,0:T(1,128)} %codes.1), calls=%async_computation.1 | async-start | bytes 32768 | tf_op jit(solution)/shard_map/all_to_all | solution.py:458
  10.6 0.0 copy-start
  10.6 4.3 %spectra.1 = f32[8,8,512]{2,1,0:T(8,128)} custom-call(s32[16]{0:T(128)} %freq_ref.1, s32[1,1024]{1,0:T(1,128)} %bitcast.12, s32[1,1024]{1,0:T(1,128)} %bitcast.13, bf16[512,4096]{1,0:T(8,128)(2,1)} %bitcast.11), custom_call_target="tpu_custom_call" | custom-call | flops 134217728 | bytes 4194304 | tf_op jit(solution)/shard_map/spectra/pallas_call | solution.py:149
  14.8 2.2 %all-to-all-done.1.code_ref = s32[16,1,256]{2,1,0:T(1,128)S(1)} async-done(((s32[16,1,256]{2,1,0:T(1,128)}), s32[16,1,256]{2,1,0:T(1,128)S(1)}, u32[]{:S(2)}, u32[]{:S(2)}) %all-to-all-start.1) | async-done | bytes 16416 | tf_op jit(solution)/shard_map/all_to_all | solution.py:458
  17.0 6.4 %all-to-all-start = ((f32[8,8,512]{2,1,0:T(8,128)}), f32[8,8,512]{2,1,0:T(8,128)S(1)}, u32[]{:S(2)}, u32[]{:S(2)}) async-start(f32[8,8,512]{2,1,0:T(8,128)} %spectra.1), calls=%async_computation | async-start | bytes 262144 | tf_op jit(solution)/shard_map/all_to_all | solution.py:460
  23.4 0.0 copy-done
  23.4 1.6 %basis.1 = (bf16[8,256,512]{2,1,0:T(8,128)(2,1)S(1)}, f32[8,4,8,512]{3,2,1,0:T(8,128)S(1)}) custom-call(s32[16]{0:T(128)S(1)} %copy-done, s32[16,1,256]{2,1,0:T(1,128)S(1)} %all-to-all-done.1.code_ref), custom_call_target="tpu_custom_call" | custom-call | flops 41943040 | bytes 3145728 | tf_op jit(solution)/shard_map/basis/pallas_call | solution.py:208
  25.1 3.6 %all-to-all-done.recv_ref = f32[8,8,512]{2,1,0:T(8,128)S(1)} async-done(((f32[8,8,512]{2,1,0:T(8,128)}), f32[8,8,512]{2,1,0:T(8,128)S(1)}, u32[]{:S(2)}, u32[]{:S(2)}) %all-to-all-start) | async-done | bytes 131104 | tf_op jit(solution)/shard_map/all_to_all | solution.py:460
  28.7 6.0 %solve.1 = bf16[16,8,40,128]{3,2,1,0:T(8,128)(2,1)S(1)} custom-call(f32[8,8,512]{2,1,0:T(8,128)S(1)} %all-to-all-done.recv_ref, bf16[8,256,512]{2,1,0:T(8,128)(2,1)S(1)} %get-tuple-element.8.azim_ref, f32[8,4,8,512]{3,2,1,0:T(8,128)S(1)} %get-tuple-element.9.seed_ref), custom_call_target="tpu_custom_call" | custom-call | flops 1342177280 | bytes 8388608 | tf_op jit(solution)/shard_map/solve/pallas_call | solution.py:369
  34.7 26.7 %all_to_all.15 = bf16[128,40,128]{2,1,0:T(8,128)(2,1)S(1)} all-to-all(bf16[128,40,128]{2,1,0:T(8,128)(2,1)S(1)} %bitcast.10), channel_id=1, replica_groups=mesh['mic'=16,'mode'=8] {'mic','mode'}, dimensions={0} | all-to-all | bytes 2621440 | tf_op jit(solution)/shard_map/all_to_all | solution.py:464
  61.4 1.5 %expand.1 = (f32[32,16,1024]{2,1,0:T(8,128)}, f32[16,1024]{1,0:T(8,128)}, f32[4,16,256]{2,1,0:T(8,128)}) custom-call(bf16[16,8,40,128]{3,2,1,0:T(8,128)(2,1)S(1)} %bitcast.9), custom_call_target="tpu_custom_call" | custom-call | flops 2097152 | bytes 3145728 | tf_op jit(solution)/shard_map/expand/pallas_call | solution.py:431
Async XLA Ops:
  2.0 15.0 %all-to-all-start.1 = ((s32[16,1,256]{2,1,0:T(1,128)}), s32[16,1,256]{2,1,0:T(1,128)S(1)}, u32[]{:S(2)}, u32[]{:S(2)}) async-start(s32[16,1,256]{2,1,0:T(1,128)} %codes.1), calls=%async_computation.1 | async-start | bytes 32768 | tf_op jit(solution)/shard_map/all_to_all | solution.py:458
  10.6 12.8 %copy-start = (s32[16]{0:T(128)S(1)}, s32[16]{0:T(128)}, u32[]{:S(2)}) copy-start(s32[16]{0:T(128)} %freq_ref.1) | copy-start | bytes 196
  17.0 11.6 %all-to-all-start = ((f32[8,8,512]{2,1,0:T(8,128)}), f32[8,8,512]{2,1,0:T(8,128)S(1)}, u32[]{:S(2)}, u32[]{:S(2)}) async-start(f32[8,8,512]{2,1,0:T(8,128)} %spectra.1), calls=%async_computation | async-start | bytes 262144 | tf_op jit(solution)/shard_map/all_to_all | solution.py:460

commit v6 on v5

--- a/solution.py
+++ b/solution.py
@@ -5,12 +5,14 @@
 from jax.experimental.pallas import tpu as pltpu
 from jax.sharding import PartitionSpec as P
 
+
 ITERS = 2
 AXIAL = 64
 NRAD = 32
 ORDERS = 256
 HALF = ORDERS // 2
 EPS = 1e-06
+SIDE = 4
 SIN_COEFS = (1.5707963200919937, -0.6459637612912833, 0.07968992686556589, -0.0046741574942986315, 0.0001516785309118288)
 BF16 = jnp.bfloat16
 F32 = jnp.float32
@@ -166,7 +168,7 @@
 
 
 def basis_kernel(freq_ref, code_ref, azim_ref, seed_ref):
-    blocks, _, width = code_ref.shape
+    _, _, width = code_ref.shape
     chunks, _, per = azim_ref.shape
     base = 2 * lax.axis_index("mode")
     odd = (iota((8, width), 0) & 1) == 1
@@ -220,8 +222,9 @@
 
 
 def solve_kernel(
-    recv_ref, azim_ref, seed_ref, out_ref, rad_ref, res_ref, image_ref, field_ref, onehot_ref, dir_ref, grown_ref, rows_ref, pick_ref
+    recv_ref, azim_ref, seed_ref, out_hbm, *refs
 ):
+    pack_refs, (rad_ref, res_ref, image_ref, field_ref, onehot_ref, dir_ref, grown_ref, rows_ref, pick_ref, out_ref, sems) = refs[:SIDE], refs[SIDE:]
     chunks, _, per = recv_ref.shape
     mics = chunks * per
     stack = 2 * NRAD
@@ -325,23 +328,28 @@
             dir_ref[1] = g_im + scaled(momentum, dir_ref[1])
             norm = next_norm
 
-    copies, _, lines, _ = out_ref.shape
+    copies = out_hbm.shape[0]
     width = mics // copies
     upper = (iota((8, per), 0) & 2) == 0
     first = iota((8, 128), 0) < 4
+    here = lax.axis_index("mic") // SIDE
     for ch in range(chunks):
-        value = jnp.where(upper, advance(ch, 0), advance(ch, 1))
-        for piece in range(per // width):
-            left, right = value[:, piece * width : piece * width + 128], value[:, piece * width + 128 : (piece + 1) * width]
-            packed = jnp.where(first, left, right).astype(BF16)
-            for owner in range(chunks):
-                out_ref[ch * (per // width) + piece, owner, lines - 8 :, :] = packed
+        advance(ch, 0)
+        advance(ch, 1)
+    for distance in range(SIDE):
+        there = lax.rem(here + distance, SIDE)
+        for y in range(SIDE):
+            ch = (there * SIDE * width + (y * width // per) * per) // per
+            at = slice(y * width % per, y * width % per + width)
+            value = jnp.where(upper[:, at], res_ref[ch, 0, :, at], res_ref[ch, 1, :, at])
+            pack_refs[distance][y] = value[0:4]
 
     for c in range(2):
         for half in range(2):
             begin = (2 * c + half) * stack
             pick_ref[begin : begin + stack] = grown_ref[c, :, half * HALF : (half + 1) * HALF].astype(BF16)
     radial_rows = (iota((stack, per), 0) >> 1).astype(F32)
+    stores = []
     for ch in range(chunks):
         tiles = []
         for part in range(2):
@@ -358,9 +366,12 @@
             value = jnp.where(upper, re, im)
             for q in range(0, per // 128, 2):
                 tiles.append(jnp.where(first, value[:, q * 128 : (q + 1) * 128], value[:, (q + 1) * 128 : (q + 2) * 128]))
-        packed = jnp.concatenate(tiles, axis=0).astype(BF16)
+        out_ref[ch] = jnp.concatenate(tiles, axis=0).astype(BF16)
         for copy in range(copies):
-            out_ref[copy, ch, 0 : lines - 8, :] = packed
+            stores.append(pltpu.make_async_copy(out_ref.at[ch], out_hbm.at[copy, ch], sems.at[ch, copy]))
+            stores[-1].start()
+    for store in stores:
+        store.wait()
 
 
 def solve_call(recv, azim, seeds, copies):
@@ -369,8 +380,9 @@
     return pl.pallas_call(
         solve_kernel,
         in_specs=[VMEM] * 3,
-        out_specs=VMEM,
-        out_shape=jax.ShapeDtypeStruct((copies, chunks, 4 * modes // chunks // 128 + 8, 128), BF16),
+        out_specs=[HBM] + [VMEM] * SIDE,
+        out_shape=[jax.ShapeDtypeStruct((copies, chunks, 4 * modes // chunks // 128, 128), BF16)]
+        + [jax.ShapeDtypeStruct((SIDE, 4, chunks * per // copies), F32)] * SIDE,
         scratch_shapes=[
             pltpu.VMEM((chunks, 2, stack, per), F32),
             pltpu.VMEM((chunks, 2, 8, per), F32),
@@ -381,6 +393,8 @@
             pltpu.VMEM((2, stack, ORDERS), F32),
             pltpu.VMEM((2 * stack, ORDERS), BF16),
             pltpu.VMEM((4 * stack, HALF), BF16),
+            pltpu.VMEM((chunks, 4 * modes // chunks // 128, 128), BF16),
+            pltpu.SemaphoreType.DMA((chunks, copies)),
         ],
         compiler_params=pltpu.CompilerParams(vmem_limit_bytes=14 << 20),
         name="solve",
@@ -388,25 +402,16 @@
     )(recv, azim, seeds)
 
 
-def expand_kernel(in_ref, amp_hbm, pow_hbm, res_hbm, wide_ref, ready_ref, pow_ref, res_ref, sems):
+def expand_kernel(in_ref, amp_hbm, pow_hbm, wide_ref, ready_ref, pow_ref, sems):
     segs, dests, lines, _ = in_ref.shape
     rows = 4
     tiles = lines // 8
-    owner = lax.axis_index("mode")
-    for s in range(segs):
-        wide_ref[1, 0, 8 * s : 8 * s + 8, :] = in_ref[s, owner, 8 * (tiles - 1) :, :].astype(F32)
-    for half in range(2):
-        for fl in range(2):
-            for c in range(2):
-                line = half * rows + 2 * c + fl
-                res_ref[2 * fl + c, :, half * 128 : (half + 1) * 128] = wide_ref[1, 0, pl.ds(line, segs, stride=8), :]
-    copies = [pltpu.make_async_copy(res_ref, res_hbm, sems.at[dests])]
-    copies[-1].start()
+    copies = []
     for d in range(dests):
         for s in range(segs):
-            for tile in range(tiles - 1):
+            for tile in range(tiles):
                 wide_ref[d % 2, tile, 8 * s : 8 * s + 8, :] = in_ref[s, d, 8 * tile : 8 * tile + 8, :].astype(F32)
-        for kc in range(8 * (tiles - 1) // rows):
+        for kc in range(lines // rows):
             at = slice(kc * 128, (kc + 1) * 128)
             for fl in range(rows // 2):
                 power = jnp.zeros((segs, 128), F32)
@@ -418,7 +423,7 @@
                 pow_ref[2 * d + fl : 2 * d + fl + 1, at] = jnp.sum(power, axis=0, keepdims=True) * (1.0 / segs)
         copies.append(pltpu.make_async_copy(ready_ref.at[d], amp_hbm.at[pl.ds(d * rows, rows)], sems.at[d]))
         copies[-1].start()
-    copies.append(pltpu.make_async_copy(pow_ref, pow_hbm, sems.at[dests + 1]))
+    copies.append(pltpu.make_async_copy(pow_ref, pow_hbm, sems.at[dests]))
     copies[-1].start()
     for copy in copies:
         copy.wait()
@@ -427,27 +432,76 @@
 def expand_call(recv):
     segs, dests, lines, _ = recv.shape
     rows = 4
-    modes = (lines - 8) // rows * 128
+    modes = lines // rows * 128
     return pl.pallas_call(
         expand_kernel,
         in_specs=[VMEM],
-        out_specs=[HBM] * 3,
+        out_specs=[HBM] * 2,
         out_shape=[
             jax.ShapeDtypeStruct((dests * rows, segs, modes), F32),
             jax.ShapeDtypeStruct((dests * rows // 2, modes), F32),
-            jax.ShapeDtypeStruct((rows, segs, 256), F32),
         ],
         scratch_shapes=[
-            pltpu.VMEM((2, lines // 8 - 1, 8 * segs, 128), F32),
+            pltpu.VMEM((2, lines // 8, 8 * segs, 128), F32),
             pltpu.VMEM((dests, rows, segs, modes), F32),
             pltpu.VMEM((dests * rows // 2, modes), F32),
-            pltpu.VMEM((rows, segs, 256), F32),
-            pltpu.SemaphoreType.DMA((dests + 2,)),
+            pltpu.SemaphoreType.DMA((dests + 1,)),
         ],
         compiler_params=pltpu.CompilerParams(vmem_limit_bytes=12 << 20),
         name="expand",
         cost_estimate=pl.CostEstimate(flops=1 << 21, bytes_accessed=3 << 20, transcendentals=0),
     )(recv)
+
+
+def repack_kernel(*refs):
+    here = lax.rem(lax.axis_index("mic"), SIDE)
+    for distance in range(SIDE):
+        there = lax.rem(here + distance, SIDE)
+        for k in range(SIDE):
+            refs[SIDE + distance][k] = refs[k][there]
+
+
+def repack_call(parts):
+    return pl.pallas_call(
+        repack_kernel,
+        in_specs=[VMEM] * SIDE,
+        out_specs=[VMEM] * SIDE,
+        out_shape=[jax.ShapeDtypeStruct(parts[0].shape, F32)] * SIDE,
+        compiler_params=pltpu.CompilerParams(vmem_limit_bytes=4 << 20),
+        name="repack",
+        cost_estimate=pl.CostEstimate(flops=0, bytes_accessed=1 << 17, transcendentals=0),
+    )(*parts)
+
+
+def turn_kernel(*refs):
+    out_ref = refs[SIDE]
+    rows, segs, width = out_ref.shape
+    mic = lax.axis_index("mic")
+    z, y = mic // SIDE, lax.rem(mic, SIDE)
+    seg = iota((segs, width), 0)
+    totals = [jnp.zeros((segs, width), F32)] * rows
+    for dy in range(SIDE):
+        for dz in range(SIDE):
+            source = lax.rem(z + SIDE - dz, SIDE) * SIDE + lax.rem(y + SIDE - dy, SIDE)
+            mask = seg == source
+            value = refs[dy][dz]
+            totals = [jnp.where(mask, value[k : k + 1], totals[k]) for k in range(rows)]
+    for fl in range(2):
+        for c in range(2):
+            out_ref[2 * fl + c] = totals[2 * c + fl]
+
+
+def turn_call(parts, segs):
+    _, rows, width = parts[0].shape
+    return pl.pallas_call(
+        turn_kernel,
+        in_specs=[VMEM] * SIDE,
+        out_specs=VMEM,
+        out_shape=jax.ShapeDtypeStruct((rows, segs, width), F32),
+        compiler_params=pltpu.CompilerParams(vmem_limit_bytes=4 << 20),
+        name="turn",
+        cost_estimate=pl.CostEstimate(flops=0, bytes_accessed=1 << 17, transcendentals=0),
+    )(*parts)
 
 
 def on_device(signal, mic_axial, mic_azimuth, mode_m, mode_n, freq_bins):
@@ -459,10 +513,22 @@
     spectra = spectra_call(freq_bins, mode_m, mode_n, signal[0], owners)
     recv = lax.all_to_all(spectra, "mode", 0, 0, tiled=True)
     azim, seeds = basis_call(freq_bins, codes, owners)
-    slots = solve_call(recv, azim, seeds, segs)
+    slots, *parts = solve_call(recv, azim, seeds, segs)
     shape = slots.shape
+
+    def along(distance, stride):
+        pairs = []
+        for source in range(segs):
+            step = (source // stride + distance) % SIDE - source // stride % SIDE
+            pairs.append((source, source + step * stride))
+        return pairs
+
     slots = lax.all_to_all(slots.reshape(segs * owners, *shape[2:]), ("mic", "mode"), 0, 0, tiled=True)
-    amplitude, power, residual = expand_call(slots.reshape(shape))
+    parts = [parts[0]] + [lax.ppermute(parts[d], "mic", along(d, SIDE)) for d in range(1, SIDE)]
+    parts = repack_call(parts)
+    parts = [parts[0]] + [lax.ppermute(parts[d], "mic", along(d, 1)) for d in range(1, SIDE)]
+    residual = turn_call(parts, segs)
+    amplitude, power = expand_call(slots.reshape(shape))
     modes = mode_m.shape[0]
     return (
         amplitude.reshape(freqs, 2, segs, modes),

time: 63.2 us -> 66.4 us (1.051)
  the two profiles are of different devices: /device:TPU:1 before, /device:TPU:4 now
where the time goes in v6:
time: 66.4 us; the launch traced here: 66 us
  starting transfers between devices  33.5 us (50%)
  Pallas kernels  17.1 us (26%)
  waiting for transfers between devices  14.7 us (22%)
  between operations  0.7 us (1%)
    all_to_all x1, starting transfers between devices, on_device(): lax.all_to_all(codes_call(mic_azimuth, mic_axial, segs), 'mic', 0, 0, til...  8.06 us
    ppermute x3, starting transfers between devices, on_device(): lax.ppermute(parts[d], 'mic', along(d, 1))  7.85 us
    pallas_call x1, Pallas kernels, solve_call(): pl.pallas_call(solve_kernel, in_specs=[VMEM] * 3, out_specs=[HBM] + [VMEM...  7.67 us
    ppermute x3, waiting for transfers between devices, on_device(): lax.ppermute(parts[d], 'mic', along(d, SIDE))  7.48 us
    all_to_all x1, starting transfers between devices, on_device(): lax.all_to_all(slots.reshape(segs * owners, *shape[2:]), ('mic', 'mode'),...  6.73 us
    ppermute x3, starting transfers between devices, on_device(): lax.ppermute(parts[d], 'mic', along(d, SIDE))  6.09 us
    all_to_all x1, starting transfers between devices, on_device(): recv = lax.all_to_all(spectra, 'mode', 0, 0, tiled=True)  4.8 us
    pallas_call x1, Pallas kernels, spectra_call(): pl.pallas_call(spectra_kernel, in_specs=[HBM] * 4, out_specs=VMEM, out_sh...  4.25 us
  transfers between devices with their start and end apart: 9, of which 7 were waited for; matrix products, arithmetic and copies ran while one was open for 0% of the time, Pallas kernels for 10%

profile of v6, /device:TPU:4, one launch (start us, length us, event | category | flops | bytes accessed | tf_op | source)
XLA Modules:
  0.0 66.0 jit_solution(7539909629055184007)
XLA Ops:
  0.6 1.3 %codes.1 = s32[16,1,256]{2,1,0:T(1,128)} custom-call(s32[1,256]{1,0:T(1,128)} %bitcast.14, s32[1,256]{1,0:T(1,128)} %bitcast.15), custom_call_target="tpu_custom_call" | custom-call | flops 1024 | bytes 16384 | tf_op jit(solution)/shard_map/codes/pallas_call | solution.py:77
  2.0 8.1 %all-to-all-start.1 = ((s32[16,1,256]{2,1,0:T(1,128)}), s32[16,1,256]{2,1,0:T(1,128)S(1)}, u32[]{:S(2)}, u32[]{:S(2)}) async-start(s32[16,1,256]{2,1,0:T(1,128)} %codes.1), calls=%async_computation.1 | async-start | bytes 32768 | tf_op jit(solution)/shard_map/all_to_all | solution.py:512
  10.0 0.0 copy-start
  10.1 4.3 %spectra.1 = f32[8,8,512]{2,1,0:T(8,128)} custom-call(s32[16]{0:T(128)} %freq_ref.1, s32[1,1024]{1,0:T(1,128)} %bitcast.12, s32[1,1024]{1,0:T(1,128)} %bitcast.13, bf16[512,4096]{1,0:T(8,128)(2,1)} %bitcast.10), custom_call_target="tpu_custom_call" | custom-call | flops 134217728 | bytes 4194304 | tf_op jit(solution)/shard_map/spectra/pallas_call | solution.py:151
  14.3 3.3 %all-to-all-done.1.code_ref = s32[16,1,256]{2,1,0:T(1,128)S(1)} async-done(((s32[16,1,256]{2,1,0:T(1,128)}), s32[16,1,256]{2,1,0:T(1,128)S(1)}, u32[]{:S(2)}, u32[]{:S(2)}) %all-to-all-start.1) | async-done | bytes 16416 | tf_op jit(solution)/shard_map/all_to_all | solution.py:512
  17.6 4.8 %all-to-all-start = ((f32[8,8,512]{2,1,0:T(8,128)}), f32[8,8,512]{2,1,0:T(8,128)S(1)}, u32[]{:S(2)}, u32[]{:S(2)}) async-start(f32[8,8,512]{2,1,0:T(8,128)} %spectra.1), calls=%async_computation | async-start | bytes 262144 | tf_op jit(solution)/shard_map/all_to_all | solution.py:514
  22.4 0.0 copy-done
  22.4 1.6 %basis.1 = (bf16[8,256,512]{2,1,0:T(8,128)(2,1)S(1)}, f32[8,4,8,512]{3,2,1,0:T(8,128)S(1)}) custom-call(s32[16]{0:T(128)S(1)} %copy-done, s32[16,1,256]{2,1,0:T(1,128)S(1)} %all-to-all-done.1.code_ref), custom_call_target="tpu_custom_call" | custom-call | flops 41943040 | bytes 3145728 | tf_op jit(solution)/shard_map/basis/pallas_call | solution.py:210
  24.1 1.7 %all-to-all-done.recv_ref = f32[8,8,512]{2,1,0:T(8,128)S(1)} async-done(((f32[8,8,512]{2,1,0:T(8,128)}), f32[8,8,512]{2,1,0:T(8,128)S(1)}, u32[]{:S(2)}, u32[]{:S(2)}) %all-to-all-start) | async-done | bytes 131104 | tf_op jit(solution)/shard_map/all_to_all | solution.py:514
  25.8 7.7 %solve.1 = (bf16[16,8,32,128]{3,2,1,0:T(8,128)(2,1)}, f32[4,4,256]{2,1,0:T(4,128)S(1)}, f32[4,4,256]{2,1,0:T(4,128)S(1)}, f32[4,4,256]{2,1,0:T(4,128)S(1)}, f32[4,4,256]{2,1,0:T(4,128)S(1)}) custom-call(f32[8,8,512]{2,1,0:T(8,128)S(1)} %all-to-all-done.recv_ref, bf16[8,256,512]{2,1,0:T(8,128)(2,1)S(1)} %get-tuple-element.16.azim_ref, ...), custom_call_target="tpu_custom_call" | custom-call | flops 1342177280 | bytes 8388608 | tf_op jit(solution)/shard_map/solve/pallas_call | solution.py:380
  33.5 6.7 %all-to-all-start.2 = ((bf16[128,32,128]{2,1,0:T(8,128)(2,1)}), bf16[128,32,128]{2,1,0:T(8,128)(2,1)S(1)}, u32[]{:S(2)}, u32[]{:S(2)}) async-start(bf16[128,32,128]{2,1,0:T(8,128)(2,1)} %bitcast.5), calls=%async_computation.2 | async-start | bytes 2097152 | tf_op jit(solution)/shard_map/all_to_all | solution.py:526
  40.2 1.7 %collective-permute-start = (f32[4,4,256]{2,1,0:T(4,128)S(1)}, f32[4,4,256]{2,1,0:T(4,128)S(1)}, u32[]{:S(2)}, u32[]{:S(2)}) collective-permute-start(f32[4,4,256]{2,1,0:T(4,128)S(1)} %get-tuple-element.22), channel_id=1, source_target_pairs={{0,32},{8,40},{16,48},{24,56},{32,64},{40,72},{48,80},{56,88},{64,... | collective-permute-start | bytes 49160 | tf_op jit(solution)/shard_map/ppermute | solution.py:527
  41.9 3.2 %collective-permute-start.1 = (f32[4,4,256]{2,1,0:T(4,128)S(1)}, f32[4,4,256]{2,1,0:T(4,128)S(1)}, u32[]{:S(2)}, u32[]{:S(2)}) collective-permute-start(f32[4,4,256]{2,1,0:T(4,128)S(1)} %get-tuple-element.23), channel_id=1, source_target_pairs={{0,64},{8,72},{16,80},{24,88},{32,96},{40,104},{48,112},{56,120},{... | collective-permute-start | bytes 49160 | tf_op jit(solution)/shard_map/ppermute | solution.py:527
  45.1 1.2 %collective-permute-start.2 = (f32[4,4,256]{2,1,0:T(4,128)S(1)}, f32[4,4,256]{2,1,0:T(4,128)S(1)}, u32[]{:S(2)}, u32[]{:S(2)}) collective-permute-start(f32[4,4,256]{2,1,0:T(4,128)S(1)} %get-tuple-element.24), channel_id=1, source_target_pairs={{0,96},{8,104},{16,112},{24,120},{32,0},{40,8},{48,16},{56,24},{64... | collective-permute-start | bytes 49160 | tf_op jit(solution)/shard_map/ppermute | solution.py:527
  46.3 0.3 collective-permute-done.refs_1_
  46.6 6.2 %collective-permute-done.1.refs_2_ = f32[4,4,256]{2,1,0:T(4,128)S(1)} collective-permute-done((f32[4,4,256]{2,1,0:T(4,128)S(1)}, f32[4,4,256]{2,1,0:T(4,128)S(1)}, u32[]{:S(2)}, u32[]{:S(2)}) %collective-permute-start.1) | collective-permute-done | bytes 16416 | tf_op jit(solution)/shard_map/ppermute | solution.py:527
  52.8 1.0 %collective-permute-done.2.refs_3_ = f32[4,4,256]{2,1,0:T(4,128)S(1)} collective-permute-done((f32[4,4,256]{2,1,0:T(4,128)S(1)}, f32[4,4,256]{2,1,0:T(4,128)S(1)}, u32[]{:S(2)}, u32[]{:S(2)}) %collective-permute-start.2) | collective-permute-done | bytes 16416 | tf_op jit(solution)/shard_map/ppermute | solution.py:527
  53.8 3.4 %collective-permute-start.3 = (f32[4,4,256]{2,1,0:T(4,128)S(1)}, f32[4,4,256]{2,1,0:T(4,128)S(1)}, u32[]{:S(2)}, u32[]{:S(2)}) collective-permute-start(f32[4,4,256]{2,1,0:T(4,128)S(1)} %get-tuple-element.26), channel_id=1, source_target_pairs={{0,8},{8,16},{16,24},{24,0},{32,40},{40,48},{48,56},{56,32},{64,72... | collective-permute-start | bytes 49160 | tf_op jit(solution)/shard_map/ppermute | solution.py:529
  57.2 2.9 %collective-permute-start.4 = (f32[4,4,256]{2,1,0:T(4,128)S(1)}, f32[4,4,256]{2,1,0:T(4,128)S(1)}, u32[]{:S(2)}, u32[]{:S(2)}) collective-permute-start(f32[4,4,256]{2,1,0:T(4,128)S(1)} %get-tuple-element.27), channel_id=1, source_target_pairs={{0,16},{8,24},{16,0},{24,8},{32,48},{40,56},{48,32},{56,40},{64,80... | collective-permute-start | bytes 49160 | tf_op jit(solution)/shard_map/ppermute | solution.py:529
  60.1 1.6 %collective-permute-start.5 = (f32[4,4,256]{2,1,0:T(4,128)S(1)}, f32[4,4,256]{2,1,0:T(4,128)S(1)}, u32[]{:S(2)}, u32[]{:S(2)}) collective-permute-start(f32[4,4,256]{2,1,0:T(4,128)S(1)} %get-tuple-element.28), channel_id=1, source_target_pairs={{0,24},{8,0},{16,8},{24,16},{32,56},{40,32},{48,40},{56,48},{64,88... | collective-permute-start | bytes 49160 | tf_op jit(solution)/shard_map/ppermute | solution.py:529
  61.7 0.0 collective-permute-done.3.refs_1_
  61.7 0.8 %collective-permute-done.4.refs_2_ = f32[4,4,256]{2,1,0:T(4,128)S(1)} collective-permute-done((f32[4,4,256]{2,1,0:T(4,128)S(1)}, f32[4,4,256]{2,1,0:T(4,128)S(1)}, u32[]{:S(2)}, u32[]{:S(2)}) %collective-permute-start.4) | collective-permute-done | bytes 16416 | tf_op jit(solution)/shard_map/ppermute | solution.py:529
  62.5 1.4 %collective-permute-done.5.refs_3_ = f32[4,4,256]{2,1,0:T(4,128)S(1)} collective-permute-done((f32[4,4,256]{2,1,0:T(4,128)S(1)}, f32[4,4,256]{2,1,0:T(4,128)S(1)}, u32[]{:S(2)}, u32[]{:S(2)}) %collective-permute-start.5) | collective-permute-done | bytes 16416 | tf_op jit(solution)/shard_map/ppermute | solution.py:529
  63.8 0.7 %turn.1 = f32[4,16,256]{2,1,0:T(8,128)} custom-call(f32[4,4,256]{2,1,0:T(4,128)S(1)} %get-tuple-element.25.refs_0_, f32[4,4,256]{2,1,0:T(4,128)S(1)} %collective-permute-done.3.refs_1_, f32[4,4,256]{2,1,0:T(4,128)S(1)} %collective-permute-done.4.refs_2_, f32[4,4,256]{2,1,0:T(4,128)S(1)} %collective-permute-done.5.refs_3_), custom_call_target="tpu_custom_call" | custom-call | bytes 131072 | tf_op jit(solution)/shard_map/turn/pallas_call | solution.py:496
  64.5 0.0 all-to-all-done.2
  64.5 1.5 %expand.1 = (f32[32,16,1024]{2,1,0:T(8,128)}, f32[16,1024]{1,0:T(8,128)}) custom-call(bf16[16,8,32,128]{3,2,1,0:T(8,128)(2,1)S(1)} %bitcast.9), custom_call_target="tpu_custom_call" | custom-call | flops 2097152 | bytes 3145728 | tf_op jit(solution)/shard_map/expand/pallas_call | solution.py:436
  (1 shorter events, 0.0 us)
Async XLA Ops:
  2.0 15.7 %all-to-all-start.1 = ((s32[16,1,256]{2,1,0:T(1,128)}), s32[16,1,256]{2,1,0:T(1,128)S(1)}, u32[]{:S(2)}, u32[]{:S(2)}) async-start(s32[16,1,256]{2,1,0:T(1,128)} %codes.1), calls=%async_computation.1 | async-start | bytes 32768 | tf_op jit(solution)/shard_map/all_to_all | solution.py:512
  10.0 12.4 %copy-start = (s32[16]{0:T(128)S(1)}, s32[16]{0:T(128)}, u32[]{:S(2)}) copy-start(s32[16]{0:T(128)} %freq_ref.1) | copy-start | bytes 196
  17.6 8.2 %all-to-all-start = ((f32[8,8,512]{2,1,0:T(8,128)}), f32[8,8,512]{2,1,0:T(8,128)S(1)}, u32[]{:S(2)}, u32[]{:S(2)}) async-start(f32[8,8,512]{2,1,0:T(8,128)} %spectra.1), calls=%async_computation | async-start | bytes 262144 | tf_op jit(solution)/shard_map/all_to_all | solution.py:514
  33.5 31.0 %all-to-all-start.2 = ((bf16[128,32,128]{2,1,0:T(8,128)(2,1)}), bf16[128,32,128]{2,1,0:T(8,128)(2,1)S(1)}, u32[]{:S(2)}, u32[]{:S(2)}) async-start(bf16[128,32,128]{2,1,0:T(8,128)(2,1)} %bitcast.5), calls=%async_computation.2 | async-start | bytes 2097152 | tf_op jit(solution)/shard_map/all_to_all | solution.py:526
  40.2 6.4 %collective-permute-start = (f32[4,4,256]{2,1,0:T(4,128)S(1)}, f32[4,4,256]{2,1,0:T(4,128)S(1)}, u32[]{:S(2)}, u32[]{:S(2)}) collective-permute-start(f32[4,4,256]{2,1,0:T(4,128)S(1)} %get-tuple-element.22), channel_id=1, source_target_pairs={{0,32},{8,40},{16,48},{24,56},{32,64},{40,72},{48,80},{56,88},{64,... | collective-permute-start | bytes 49160 | tf_op jit(solution)/shard_map/ppermute | solution.py:527
  41.9 10.9 %collective-permute-start.1 = (f32[4,4,256]{2,1,0:T(4,128)S(1)}, f32[4,4,256]{2,1,0:T(4,128)S(1)}, u32[]{:S(2)}, u32[]{:S(2)}) collective-permute-start(f32[4,4,256]{2,1,0:T(4,128)S(1)} %get-tuple-element.23), channel_id=1, source_target_pairs={{0,64},{8,72},{16,80},{24,88},{32,96},{40,104},{48,112},{56,120},{... | collective-permute-start | bytes 49160 | tf_op jit(solution)/shard_map/ppermute | solution.py:527
  45.1 8.7 %collective-permute-start.2 = (f32[4,4,256]{2,1,0:T(4,128)S(1)}, f32[4,4,256]{2,1,0:T(4,128)S(1)}, u32[]{:S(2)}, u32[]{:S(2)}) collective-permute-start(f32[4,4,256]{2,1,0:T(4,128)S(1)} %get-tuple-element.24), channel_id=1, source_target_pairs={{0,96},{8,104},{16,112},{24,120},{32,0},{40,8},{48,16},{56,24},{64... | collective-permute-start | bytes 49160 | tf_op jit(solution)/shard_map/ppermute | solution.py:527
  53.8 7.8 %collective-permute-start.3 = (f32[4,4,256]{2,1,0:T(4,128)S(1)}, f32[4,4,256]{2,1,0:T(4,128)S(1)}, u32[]{:S(2)}, u32[]{:S(2)}) collective-permute-start(f32[4,4,256]{2,1,0:T(4,128)S(1)} %get-tuple-element.26), channel_id=1, source_target_pairs={{0,8},{8,16},{16,24},{24,0},{32,40},{40,48},{48,56},{56,32},{64,72... | collective-permute-start | bytes 49160 | tf_op jit(solution)/shard_map/ppermute | solution.py:529
  57.2 5.2 %collective-permute-start.4 = (f32[4,4,256]{2,1,0:T(4,128)S(1)}, f32[4,4,256]{2,1,0:T(4,128)S(1)}, u32[]{:S(2)}, u32[]{:S(2)}) collective-permute-start(f32[4,4,256]{2,1,0:T(4,128)S(1)} %get-tuple-element.27), channel_id=1, source_target_pairs={{0,16},{8,24},{16,0},{24,8},{32,48},{40,56},{48,32},{56,40},{64,80... | collective-permute-start | bytes 49160 | tf_op jit(solution)/shard_map/ppermute | solution.py:529
  60.1 3.7 %collective-permute-start.5 = (f32[4,4,256]{2,1,0:T(4,128)S(1)}, f32[4,4,256]{2,1,0:T(4,128)S(1)}, u32[]{:S(2)}, u32[]{:S(2)}) collective-permute-start(f32[4,4,256]{2,1,0:T(4,128)S(1)} %get-tuple-element.28), channel_id=1, source_target_pairs={{0,24},{8,0},{16,8},{24,16},{32,56},{40,32},{48,40},{56,48},{64,88... | collective-permute-start | bytes 49160 | tf_op jit(solution)/shard_map/ppermute | solution.py:529

commit v7 on v5

--- a/solution.py
+++ b/solution.py
@@ -138,8 +138,8 @@
         copies[k].wait()
         spectra = spectra + nt_dot(analysis_ref[:, k * span : (k + 1) * span], signal_ref[k])
     for d in range(dests):
-        out_ref[d, 0:own, :] = spectra[d * own : (d + 1) * own]
-        out_ref[d, own : 2 * own, :] = spectra[freqs + d * own : freqs + (d + 1) * own]
+        for k in range(2 * own):
+            out_ref[d, k : k + 1, :] = spectra[k * dests + d : k * dests + d + 1]
 
 
 def spectra_call(freq_bins, mode_m, mode_n, signal, dests):
@@ -168,9 +168,9 @@
 def basis_kernel(freq_ref, code_ref, azim_ref, seed_ref):
     blocks, _, width = code_ref.shape
     chunks, _, per = azim_ref.shape
-    base = 2 * lax.axis_index("mode")
+    base = lax.axis_index("mode")
     odd = (iota((8, width), 0) & 1) == 1
-    freq = jnp.where(odd, freq_ref[base + 1], freq_ref[base]).astype(F32)
+    freq = jnp.where(odd, freq_ref[base + chunks], freq_ref[base]).astype(F32)
     row = iota((8, width), 0).astype(F32)
     radial = (iota((8, width), 0) >> 1).astype(F32)
 
@@ -325,23 +325,28 @@
             dir_ref[1] = g_im + scaled(momentum, dir_ref[1])
             norm = next_norm
 
-    copies, _, lines, _ = out_ref.shape
+    copies, _, lines, _, _ = out_ref.shape
     width = mics // copies
+    even = (iota((8, per), 0) & 1) == 0
     upper = (iota((8, per), 0) & 2) == 0
-    first = iota((8, 128), 0) < 4
+    first = iota((8, 128), 0) < 2
     for ch in range(chunks):
-        value = jnp.where(upper, advance(ch, 0), advance(ch, 1))
+        re, im = advance(ch, 0), advance(ch, 1)
+        sides = [jnp.where(even, re, pltpu.roll(im, 1, 0)), jnp.where(even, pltpu.roll(re, 7, 0), im)]
         for piece in range(per // width):
-            left, right = value[:, piece * width : piece * width + 128], value[:, piece * width + 128 : (piece + 1) * width]
-            packed = jnp.where(first, left, right).astype(BF16)
-            for owner in range(chunks):
-                out_ref[ch * (per // width) + piece, owner, lines - 8 :, :] = packed
+            for fl in range(2):
+                left = sides[fl][:, piece * width : piece * width + 128]
+                right = sides[fl][:, piece * width + 128 : (piece + 1) * width]
+                packed = jnp.where(first, left, right)[0:4].astype(BF16)
+                for owner in range(fl * chunks // 2, (fl + 1) * chunks // 2):
+                    out_ref[ch * (per // width) + piece, owner, lines - 1] = packed
 
     for c in range(2):
         for half in range(2):
             begin = (2 * c + half) * stack
             pick_ref[begin : begin + stack] = grown_ref[c, :, half * HALF : (half + 1) * HALF].astype(BF16)
     radial_rows = (iota((stack, per), 0) >> 1).astype(F32)
+    first = iota((8, 128), 0) < 4
     for ch in range(chunks):
         tiles = []
         for part in range(2):
@@ -358,9 +363,11 @@
             value = jnp.where(upper, re, im)
             for q in range(0, per // 128, 2):
                 tiles.append(jnp.where(first, value[:, q * 128 : (q + 1) * 128], value[:, (q + 1) * 128 : (q + 2) * 128]))
-        packed = jnp.concatenate(tiles, axis=0).astype(BF16)
-        for copy in range(copies):
-            out_ref[copy, ch, 0 : lines - 8, :] = packed
+        for k, tile in enumerate(tiles):
+            for half in range(2):
+                packed = tile[4 * half : 4 * half + 4].astype(BF16)
+                for copy in range(copies):
+                    out_ref[copy, ch, 2 * k + half] = packed
 
 
 def solve_call(recv, azim, seeds, copies):
@@ -370,7 +377,7 @@
         solve_kernel,
         in_specs=[VMEM] * 3,
         out_specs=VMEM,
-        out_shape=jax.ShapeDtypeStruct((copies, chunks, 4 * modes // chunks // 128 + 8, 128), BF16),
+        out_shape=jax.ShapeDtypeStruct((copies, chunks, modes // chunks // 128 + 1, 4, 128), BF16),
         scratch_shapes=[
             pltpu.VMEM((chunks, 2, stack, per), F32),
             pltpu.VMEM((chunks, 2, 8, per), F32),
@@ -389,45 +396,46 @@
 
 
 def expand_kernel(in_ref, amp_hbm, pow_hbm, res_hbm, wide_ref, ready_ref, pow_ref, res_ref, sems):
-    segs, dests, lines, _ = in_ref.shape
-    rows = 4
-    tiles = lines // 8
-    owner = lax.axis_index("mode")
-    for s in range(segs):
-        wide_ref[1, 0, 8 * s : 8 * s + 8, :] = in_ref[s, owner, 8 * (tiles - 1) :, :].astype(F32)
-    for half in range(2):
-        for fl in range(2):
+    segs, dests, lines, rows, _ = in_ref.shape
+    lines = lines - 1
+    owner = lax.rem(2 * lax.axis_index("mode"), dests)
+    for f in range(2):
+        for s in range(segs):
+            wide_ref[1, f, 8 * s : 8 * s + rows, :] = in_ref[s, owner + f, lines].astype(F32)
+        for half in range(2):
             for c in range(2):
-                line = half * rows + 2 * c + fl
-                res_ref[2 * fl + c, :, half * 128 : (half + 1) * 128] = wide_ref[1, 0, pl.ds(line, segs, stride=8), :]
-    copies = [pltpu.make_async_copy(res_ref, res_hbm, sems.at[dests])]
+                value = wide_ref[1, f, pl.ds(2 * half + c, segs, stride=8), :]
+                res_ref[2 * f + c, :, half * 128 : (half + 1) * 128] = value
+    copies = [pltpu.make_async_copy(res_ref, res_hbm, sems.at[2 * dests])]
     copies[-1].start()
     for d in range(dests):
         for s in range(segs):
-            for tile in range(tiles - 1):
-                wide_ref[d % 2, tile, 8 * s : 8 * s + 8, :] = in_ref[s, d, 8 * tile : 8 * tile + 8, :].astype(F32)
-        for kc in range(8 * (tiles - 1) // rows):
+            for kc in range(lines):
+                begin = 8 * s + rows * (kc % 2)
+                wide_ref[d % 2, kc // 2, begin : begin + rows, :] = in_ref[s, d, kc].astype(F32)
+        for kc in range(lines):
             at = slice(kc * 128, (kc + 1) * 128)
             for fl in range(rows // 2):
                 power = jnp.zeros((segs, 128), F32)
                 for c in range(2):
-                    line = kc * rows + 2 * c + fl
-                    value = wide_ref[d % 2, line // 8, pl.ds(line % 8, segs, stride=8), :]
-                    ready_ref[d, 2 * fl + c, :, at] = value
+                    value = wide_ref[d % 2, kc // 2, pl.ds(rows * (kc % 2) + 2 * c + fl, segs, stride=8), :]
+                    ready_ref[d, fl, c, :, at] = value
                     power = power + value * value
-                pow_ref[2 * d + fl : 2 * d + fl + 1, at] = jnp.sum(power, axis=0, keepdims=True) * (1.0 / segs)
-        copies.append(pltpu.make_async_copy(ready_ref.at[d], amp_hbm.at[pl.ds(d * rows, rows)], sems.at[d]))
-        copies[-1].start()
-    copies.append(pltpu.make_async_copy(pow_ref, pow_hbm, sems.at[dests + 1]))
+                f = d + fl * dests
+                pow_ref[f : f + 1, at] = jnp.sum(power, axis=0, keepdims=True) * (1.0 / segs)
+        for fl in range(rows // 2):
+            f = d + fl * dests
+            copies.append(pltpu.make_async_copy(ready_ref.at[d, fl], amp_hbm.at[pl.ds(2 * f, 2)], sems.at[2 * d + fl]))
+            copies[-1].start()
+    copies.append(pltpu.make_async_copy(pow_ref, pow_hbm, sems.at[2 * dests + 1]))
     copies[-1].start()
     for copy in copies:
         copy.wait()
 
 
 def expand_call(recv):
-    segs, dests, lines, _ = recv.shape
-    rows = 4
-    modes = (lines - 8) // rows * 128
+    segs, dests, lines, rows, _ = recv.shape
+    modes = (lines - 1) * 128
     return pl.pallas_call(
         expand_kernel,
         in_specs=[VMEM],
@@ -438,11 +446,11 @@
             jax.ShapeDtypeStruct((rows, segs, 256), F32),
         ],
         scratch_shapes=[
-            pltpu.VMEM((2, lines // 8 - 1, 8 * segs, 128), F32),
-            pltpu.VMEM((dests, rows, segs, modes), F32),
+            pltpu.VMEM((2, (lines - 1) // 2, 8 * segs, 128), F32),
+            pltpu.VMEM((dests, rows // 2, 2, segs, modes), F32),
             pltpu.VMEM((dests * rows // 2, modes), F32),
             pltpu.VMEM((rows, segs, 256), F32),
-            pltpu.SemaphoreType.DMA((dests + 2,)),
+            pltpu.SemaphoreType.DMA((2 * dests + 2,)),
         ],
         compiler_params=pltpu.CompilerParams(vmem_limit_bytes=12 << 20),
         name="expand",

time: 63.2 us -> 61.9 us (0.979)
  blocking collectives: 26.7 us -> 25.3 us
    all_to_all x1, blocking collectives: 26.7 us -> 25.3 us  [on_device(): lax.all_to_all(slots.reshape(segs * owners, *shape[2:]), ('mic', 'mode'),...]
  transfers between devices with their start and end apart: 2 -> 2, of which waited for: 2 -> 2; matrix products, arithmetic and copies ran while one was open for 0% -> 0% of each run, Pallas kernels for 9% -> 10%
where the time goes in v7:
time: 61.9 us; the launch traced here: 61.6 us
  blocking collectives  25.3 us (41%)
  starting transfers between devices  15 us (24%)
  Pallas kernels  14.8 us (24%)
  waiting for transfers between devices  5.76 us (9%)
  between operations  0.68 us (1%)
    all_to_all x1, blocking collectives, on_device(): lax.all_to_all(slots.reshape(segs * owners, *shape[2:]), ('mic', 'mode'),...  25.3 us
    all_to_all x1, starting transfers between devices, on_device(): lax.all_to_all(codes_call(mic_azimuth, mic_axial, segs), 'mic', 0, 0, til...  8.6 us
    all_to_all x1, starting transfers between devices, on_device(): recv = lax.all_to_all(spectra, 'mode', 0, 0, tiled=True)  6.4 us
    pallas_call x1, Pallas kernels, solve_call(): pl.pallas_call(solve_kernel, in_specs=[VMEM] * 3, out_specs=VMEM, out_sha...  6.02 us
    pallas_call x1, Pallas kernels, spectra_call(): pl.pallas_call(spectra_kernel, in_specs=[HBM] * 4, out_specs=VMEM, out_sh...  4.25 us
    all_to_all x1, waiting for transfers between devices, on_device(): recv = lax.all_to_all(spectra, 'mode', 0, 0, tiled=True)  3.59 us
    all_to_all x1, waiting for transfers between devices, on_device(): lax.all_to_all(codes_call(mic_azimuth, mic_axial, segs), 'mic', 0, 0, til...  2.17 us
    pallas_call x1, Pallas kernels, basis_call(): pl.pallas_call(basis_kernel, in_specs=[SMEM, VMEM], out_specs=[VMEM] * 2,...  1.64 us
  transfers between devices with their start and end apart: 2, of which 2 were waited for; matrix products, arithmetic and copies ran while one was open for 0% of the time, Pallas kernels for 10%

profile of v7, /device:TPU:1, one launch (start us, length us, event | category | flops | bytes accessed | tf_op | source)
XLA Modules:
  0.0 61.6 jit_solution(721569418251663470)
XLA Ops:
  0.6 1.3 %codes.1 = s32[16,1,256]{2,1,0:T(1,128)} custom-call(s32[1,256]{1,0:T(1,128)} %bitcast.14, s32[1,256]{1,0:T(1,128)} %bitcast.15), custom_call_target="tpu_custom_call" | custom-call | flops 1024 | bytes 16384 | tf_op jit(solution)/shard_map/codes/pallas_call | solution.py:75
  2.0 8.6 %all-to-all-start.1 = ((s32[16,1,256]{2,1,0:T(1,128)}), s32[16,1,256]{2,1,0:T(1,128)S(1)}, u32[]{:S(2)}, u32[]{:S(2)}) async-start(s32[16,1,256]{2,1,0:T(1,128)} %codes.1), calls=%async_computation.1 | async-start | bytes 32768 | tf_op jit(solution)/shard_map/all_to_all | solution.py:466
  10.6 0.0 copy-start
  10.6 4.3 %spectra.1 = f32[8,8,512]{2,1,0:T(8,128)} custom-call(s32[16]{0:T(128)} %freq_ref.1, s32[1,1024]{1,0:T(1,128)} %bitcast.12, s32[1,1024]{1,0:T(1,128)} %bitcast.13, bf16[512,4096]{1,0:T(8,128)(2,1)} %bitcast.11), custom_call_target="tpu_custom_call" | custom-call | flops 134217728 | bytes 4194304 | tf_op jit(solution)/shard_map/spectra/pallas_call | solution.py:149
  14.8 2.2 %all-to-all-done.1.code_ref = s32[16,1,256]{2,1,0:T(1,128)S(1)} async-done(((s32[16,1,256]{2,1,0:T(1,128)}), s32[16,1,256]{2,1,0:T(1,128)S(1)}, u32[]{:S(2)}, u32[]{:S(2)}) %all-to-all-start.1) | async-done | bytes 16416 | tf_op jit(solution)/shard_map/all_to_all | solution.py:466
  17.0 6.4 %all-to-all-start = ((f32[8,8,512]{2,1,0:T(8,128)}), f32[8,8,512]{2,1,0:T(8,128)S(1)}, u32[]{:S(2)}, u32[]{:S(2)}) async-start(f32[8,8,512]{2,1,0:T(8,128)} %spectra.1), calls=%async_computation | async-start | bytes 262144 | tf_op jit(solution)/shard_map/all_to_all | solution.py:468
  23.4 0.0 copy-done
  23.4 1.6 %basis.1 = (bf16[8,256,512]{2,1,0:T(8,128)(2,1)S(1)}, f32[8,4,8,512]{3,2,1,0:T(8,128)S(1)}) custom-call(s32[16]{0:T(128)S(1)} %copy-done, s32[16,1,256]{2,1,0:T(1,128)S(1)} %all-to-all-done.1.code_ref), custom_call_target="tpu_custom_call" | custom-call | flops 41943040 | bytes 3145728 | tf_op jit(solution)/shard_map/basis/pallas_call | solution.py:208
  25.1 3.6 %all-to-all-done.recv_ref = f32[8,8,512]{2,1,0:T(8,128)S(1)} async-done(((f32[8,8,512]{2,1,0:T(8,128)}), f32[8,8,512]{2,1,0:T(8,128)S(1)}, u32[]{:S(2)}, u32[]{:S(2)}) %all-to-all-start) | async-done | bytes 131104 | tf_op jit(solution)/shard_map/all_to_all | solution.py:468
  28.7 6.0 %solve.1 = bf16[16,8,9,4,128]{4,3,2,1,0:T(4,128)(2,1)S(1)} custom-call(f32[8,8,512]{2,1,0:T(8,128)S(1)} %all-to-all-done.recv_ref, bf16[8,256,512]{2,1,0:T(8,128)(2,1)S(1)} %get-tuple-element.8.azim_ref, f32[8,4,8,512]{3,2,1,0:T(8,128)S(1)} %get-tuple-element.9.seed_ref), custom_call_target="tpu_custom_call" | custom-call | flops 1342177280 | bytes 8388608 | tf_op jit(solution)/shard_map/solve/pallas_call | solution.py:376
  34.7 25.3 %all_to_all.15 = bf16[128,9,4,128]{3,2,1,0:T(4,128)(2,1)S(1)} all-to-all(bf16[128,9,4,128]{3,2,1,0:T(4,128)(2,1)S(1)} %bitcast.10), channel_id=1, replica_groups=mesh['mic'=16,'mode'=8] {'mic','mode'}, dimensions={0} | all-to-all | bytes 2359296 | tf_op jit(solution)/shard_map/all_to_all | solution.py:472
  60.0 1.6 %expand.1 = (f32[32,16,1024]{2,1,0:T(8,128)}, f32[16,1024]{1,0:T(8,128)}, f32[4,16,256]{2,1,0:T(8,128)}) custom-call(bf16[16,8,9,4,128]{4,3,2,1,0:T(4,128)(2,1)S(1)} %bitcast.9), custom_call_target="tpu_custom_call" | custom-call | flops 2097152 | bytes 3145728 | tf_op jit(solution)/shard_map/expand/pallas_call | solution.py:439
Async XLA Ops:
  2.0 15.0 %all-to-all-start.1 = ((s32[16,1,256]{2,1,0:T(1,128)}), s32[16,1,256]{2,1,0:T(1,128)S(1)}, u32[]{:S(2)}, u32[]{:S(2)}) async-start(s32[16,1,256]{2,1,0:T(1,128)} %codes.1), calls=%async_computation.1 | async-start | bytes 32768 | tf_op jit(solution)/shard_map/all_to_all | solution.py:466
  10.6 12.8 %copy-start = (s32[16]{0:T(128)S(1)}, s32[16]{0:T(128)}, u32[]{:S(2)}) copy-start(s32[16]{0:T(128)} %freq_ref.1) | copy-start | bytes 196
  17.0 11.6 %all-to-all-start = ((f32[8,8,512]{2,1,0:T(8,128)}), f32[8,8,512]{2,1,0:T(8,128)S(1)}, u32[]{:S(2)}, u32[]{:S(2)}) async-start(f32[8,8,512]{2,1,0:T(8,128)} %spectra.1), calls=%async_computation | async-start | bytes 262144 | tf_op jit(solution)/shard_map/all_to_all | solution.py:468

commit v8 on v7

--- a/solution.py
+++ b/solution.py
@@ -6,7 +6,6 @@
 from jax.sharding import PartitionSpec as P
 
 ITERS = 2
-AXIAL = 64
 NRAD = 32
 ORDERS = 256
 HALF = ORDERS // 2
@@ -53,21 +52,14 @@
     return x + pltpu.roll(x, 2, 0)
 
 
-def codes_kernel(azimuth_hbm, axial_hbm, out_hbm, azimuth_ref, axial_ref, out_ref, sems):
-    loads = [
-        pltpu.make_async_copy(azimuth_hbm, azimuth_ref, sems.at[0]),
-        pltpu.make_async_copy(axial_hbm, axial_ref, sems.at[1]),
-    ]
-    for load in loads:
-        load.start()
-    for load in loads:
-        load.wait()
-    code = azimuth_ref[...] * AXIAL + axial_ref[...]
-    for copy in range(out_ref.shape[0]):
-        out_ref[copy] = code
-    store = pltpu.make_async_copy(out_ref, out_hbm, sems.at[2])
-    store.start()
-    store.wait()
+def codes_kernel(azimuth_hbm, axial_hbm, out_hbm, sems):
+    stores = []
+    for copy in range(out_hbm.shape[0]):
+        for k, source in enumerate((azimuth_hbm, axial_hbm)):
+            stores.append(pltpu.make_async_copy(source, out_hbm.at[copy, k], sems.at[copy, k]))
+            stores[-1].start()
+    for store in stores:
+        store.wait()
 
 
 def codes_call(azimuth, axial, copies):
@@ -76,13 +68,8 @@
         codes_kernel,
         in_specs=[HBM] * 2,
         out_specs=HBM,
-        out_shape=jax.ShapeDtypeStruct((copies, 1, mics), jnp.int32),
-        scratch_shapes=[
-            pltpu.VMEM((1, mics), jnp.int32),
-            pltpu.VMEM((1, mics), jnp.int32),
-            pltpu.VMEM((copies, 1, mics), jnp.int32),
-            pltpu.SemaphoreType.DMA((3,)),
-        ],
+        out_shape=jax.ShapeDtypeStruct((copies, 2, 1, mics), jnp.int32),
+        scratch_shapes=[pltpu.SemaphoreType.DMA((copies, 2))],
         name="codes",
         cost_estimate=pl.CostEstimate(flops=1 << 10, bytes_accessed=1 << 14, transcendentals=0),
     )(azimuth.reshape(1, -1), axial.reshape(1, -1))
@@ -166,7 +153,7 @@
 
 
 def basis_kernel(freq_ref, code_ref, azim_ref, seed_ref):
-    blocks, _, width = code_ref.shape
+    blocks, _, _, width = code_ref.shape
     chunks, _, per = azim_ref.shape
     base = lax.axis_index("mode")
     odd = (iota((8, width), 0) & 1) == 1
@@ -178,9 +165,9 @@
     def _(ch):
         for piece in range(per // width):
             at = slice(piece * width, (piece + 1) * width)
-            code = jnp.broadcast_to(code_ref[ch * (per // width) + piece], (8, width))
-            azimuth = (code >> 6).astype(F32)
-            axial = (code & (AXIAL - 1)).astype(F32)
+            block = ch * (per // width) + piece
+            azimuth = jnp.broadcast_to(code_ref[block, 0], (8, width)).astype(F32)
+            axial = jnp.broadcast_to(code_ref[block, 1], (8, width)).astype(F32)
             turns = azimuth * (row + 0.5) * (1.0 / 512)
             re, im = cos_turns(turns), sin_turns(turns)
             turns = azimuth * (8.0 / 512)
@@ -203,7 +190,7 @@
 
 
 def basis_call(freq_bins, codes, chunks):
-    blocks, _, width = codes.shape
+    blocks, _, _, width = codes.shape
     per = blocks * width // chunks
     return pl.pallas_call(
         basis_kernel,

time: 61.9 us -> 62.9 us (1.016)
  Pallas kernels: 14.8 us -> 15.9 us
    pallas_call x1, Pallas kernels: 1.33 us -> 2.39 us  [codes_call(): pl.pallas_call(codes_kernel, in_specs=[HBM] * 2, out_specs=HBM, out_shape...]
  transfers between devices with their start and end apart: 2 -> 2, of which waited for: 2 -> 2; matrix products, arithmetic and copies ran while one was open for 0% -> 0% of each run, Pallas kernels for 10% -> 9%
where the time goes in v8:
time: 62.9 us; the launch traced here: 62.6 us
  blocking collectives  25.3 us (40%)
  Pallas kernels  15.9 us (25%)
  starting transfers between devices  15 us (24%)
  waiting for transfers between devices  5.79 us (9%)
  between operations  0.68 us (1%)
    all_to_all x1, blocking collectives, on_device(): lax.all_to_all(slots.reshape(segs * owners, *shape[2:]), ('mic', 'mode'),...  25.3 us
    all_to_all x1, starting transfers between devices, on_device(): lax.all_to_all(codes_call(mic_azimuth, mic_axial, segs), 'mic', 0, 0, til...  8.6 us
    all_to_all x1, starting transfers between devices, on_device(): recv = lax.all_to_all(spectra, 'mode', 0, 0, tiled=True)  6.38 us
    pallas_call x1, Pallas kernels, solve_call(): pl.pallas_call(solve_kernel, in_specs=[VMEM] * 3, out_specs=VMEM, out_sha...  6.03 us
    pallas_call x1, Pallas kernels, spectra_call(): pl.pallas_call(spectra_kernel, in_specs=[HBM] * 4, out_specs=VMEM, out_sh...  4.25 us
    all_to_all x1, waiting for transfers between devices, on_device(): recv = lax.all_to_all(spectra, 'mode', 0, 0, tiled=True)  3.59 us
    pallas_call x1, Pallas kernels, codes_call(): pl.pallas_call(codes_kernel, in_specs=[HBM] * 2, out_specs=HBM, out_shape...  2.39 us
    all_to_all x1, waiting for transfers between devices, on_device(): lax.all_to_all(codes_call(mic_azimuth, mic_axial, segs), 'mic', 0, 0, til...  2.2 us
  transfers between devices with their start and end apart: 2, of which 2 were waited for; matrix products, arithmetic and copies ran while one was open for 0% of the time, Pallas kernels for 9%

profile of v8, /device:TPU:1, one launch (start us, length us, event | category | flops | bytes accessed | tf_op | source)
XLA Modules:
  0.0 62.6 jit_solution(18223380421641779110)
XLA Ops:
  0.6 2.4 %codes.1 = s32[16,2,1,256]{3,2,1,0:T(1,128)} custom-call(s32[1,256]{1,0:T(1,128)} %bitcast.14, s32[1,256]{1,0:T(1,128)} %bitcast.15), custom_call_target="tpu_custom_call" | custom-call | flops 1024 | bytes 16384 | tf_op jit(solution)/shard_map/codes/pallas_call | solution.py:67
  3.0 8.6 %all-to-all-start.1 = ((s32[16,2,1,256]{3,2,1,0:T(1,128)}), s32[16,2,1,256]{3,2,1,0:T(1,128)S(1)}, u32[]{:S(2)}, u32[]{:S(2)}) async-start(s32[16,2,1,256]{3,2,1,0:T(1,128)} %codes.1), calls=%async_computation.1 | async-start | bytes 65536 | tf_op jit(solution)/shard_map/all_to_all | solution.py:453
  11.6 0.0 copy-start
  11.6 4.3 %spectra.1 = f32[8,8,512]{2,1,0:T(8,128)} custom-call(s32[16]{0:T(128)} %freq_ref.1, s32[1,1024]{1,0:T(1,128)} %bitcast.12, s32[1,1024]{1,0:T(1,128)} %bitcast.13, bf16[512,4096]{1,0:T(8,128)(2,1)} %bitcast.11), custom_call_target="tpu_custom_call" | custom-call | flops 134217728 | bytes 4194304 | tf_op jit(solution)/shard_map/spectra/pallas_call | solution.py:136
  15.9 2.2 %all-to-all-done.1.code_ref = s32[16,2,1,256]{3,2,1,0:T(1,128)S(1)} async-done(((s32[16,2,1,256]{3,2,1,0:T(1,128)}), s32[16,2,1,256]{3,2,1,0:T(1,128)S(1)}, u32[]{:S(2)}, u32[]{:S(2)}) %all-to-all-start.1) | async-done | bytes 32800 | tf_op jit(solution)/shard_map/all_to_all | solution.py:453
  18.1 6.4 %all-to-all-start = ((f32[8,8,512]{2,1,0:T(8,128)}), f32[8,8,512]{2,1,0:T(8,128)S(1)}, u32[]{:S(2)}, u32[]{:S(2)}) async-start(f32[8,8,512]{2,1,0:T(8,128)} %spectra.1), calls=%async_computation | async-start | bytes 262144 | tf_op jit(solution)/shard_map/all_to_all | solution.py:455
  24.5 0.0 copy-done
  24.5 1.6 %basis.1 = (bf16[8,256,512]{2,1,0:T(8,128)(2,1)S(1)}, f32[8,4,8,512]{3,2,1,0:T(8,128)S(1)}) custom-call(s32[16]{0:T(128)S(1)} %copy-done, s32[16,2,1,256]{3,2,1,0:T(1,128)S(1)} %all-to-all-done.1.code_ref), custom_call_target="tpu_custom_call" | custom-call | flops 41943040 | bytes 3145728 | tf_op jit(solution)/shard_map/basis/pallas_call | solution.py:195
  26.1 3.6 %all-to-all-done.recv_ref = f32[8,8,512]{2,1,0:T(8,128)S(1)} async-done(((f32[8,8,512]{2,1,0:T(8,128)}), f32[8,8,512]{2,1,0:T(8,128)S(1)}, u32[]{:S(2)}, u32[]{:S(2)}) %all-to-all-start) | async-done | bytes 131104 | tf_op jit(solution)/shard_map/all_to_all | solution.py:455
  29.7 6.0 %solve.1 = bf16[16,8,9,4,128]{4,3,2,1,0:T(4,128)(2,1)S(1)} custom-call(f32[8,8,512]{2,1,0:T(8,128)S(1)} %all-to-all-done.recv_ref, bf16[8,256,512]{2,1,0:T(8,128)(2,1)S(1)} %get-tuple-element.8.azim_ref, f32[8,4,8,512]{3,2,1,0:T(8,128)S(1)} %get-tuple-element.9.seed_ref), custom_call_target="tpu_custom_call" | custom-call | flops 1342177280 | bytes 8388608 | tf_op jit(solution)/shard_map/solve/pallas_call | solution.py:363
  35.8 25.3 %all_to_all.15 = bf16[128,9,4,128]{3,2,1,0:T(4,128)(2,1)S(1)} all-to-all(bf16[128,9,4,128]{3,2,1,0:T(4,128)(2,1)S(1)} %bitcast.10), channel_id=1, replica_groups=mesh['mic'=16,'mode'=8] {'mic','mode'}, dimensions={0} | all-to-all | bytes 2359296 | tf_op jit(solution)/shard_map/all_to_all | solution.py:459
  61.1 1.6 %expand.1 = (f32[32,16,1024]{2,1,0:T(8,128)}, f32[16,1024]{1,0:T(8,128)}, f32[4,16,256]{2,1,0:T(8,128)}) custom-call(bf16[16,8,9,4,128]{4,3,2,1,0:T(4,128)(2,1)S(1)} %bitcast.9), custom_call_target="tpu_custom_call" | custom-call | flops 2097152 | bytes 3145728 | tf_op jit(solution)/shard_map/expand/pallas_call | solution.py:426
Async XLA Ops:
  3.0 15.1 %all-to-all-start.1 = ((s32[16,2,1,256]{3,2,1,0:T(1,128)}), s32[16,2,1,256]{3,2,1,0:T(1,128)S(1)}, u32[]{:S(2)}, u32[]{:S(2)}) async-start(s32[16,2,1,256]{3,2,1,0:T(1,128)} %codes.1), calls=%async_computation.1 | async-start | bytes 65536 | tf_op jit(solution)/shard_map/all_to_all | solution.py:453
  11.6 12.9 %copy-start = (s32[16]{0:T(128)S(1)}, s32[16]{0:T(128)}, u32[]{:S(2)}) copy-start(s32[16]{0:T(128)} %freq_ref.1) | copy-start | bytes 196
  18.1 11.6 %all-to-all-start = ((f32[8,8,512]{2,1,0:T(8,128)}), f32[8,8,512]{2,1,0:T(8,128)S(1)}, u32[]{:S(2)}, u32[]{:S(2)}) async-start(f32[8,8,512]{2,1,0:T(8,128)} %spectra.1), calls=%async_computation | async-start | bytes 262144 | tf_op jit(solution)/shard_map/all_to_all | solution.py:455

commit v9 on v7

--- a/solution.py
+++ b/solution.py
@@ -165,7 +165,7 @@
     )(freq_bins, mode_m.reshape(1, -1), mode_n.reshape(1, -1), signal)
 
 
-def basis_kernel(freq_ref, code_ref, azim_ref, seed_ref):
+def basis_kernel(freq_ref, code_ref, azim_ref, early_ref, seed_ref):
     blocks, _, width = code_ref.shape
     chunks, _, per = azim_ref.shape
     base = lax.axis_index("mode")
@@ -174,8 +174,9 @@
     row = iota((8, width), 0).astype(F32)
     radial = (iota((8, width), 0) >> 1).astype(F32)
 
-    @pl.loop(0, chunks)
-    def _(ch):
+    early = early_ref.shape[0]
+
+    def make(ch, whole):
         for piece in range(per // width):
             at = slice(piece * width, (piece + 1) * width)
             code = jnp.broadcast_to(code_ref[ch * (per // width) + piece], (8, width))
@@ -198,8 +199,23 @@
             re, im = cos_turns(turns), sin_turns(turns)
             turns = axial * freq * (-4.0 / 32768)
             step_re, step_im = cos_turns(turns), sin_turns(turns)
-            for k, value in enumerate((re, im, step_re, step_im)):
-                seed_ref[ch, k, :, at] = value
+            if whole:
+                for a in range(2 * NRAD // 8):
+                    early_ref[ch, 0, 8 * a : 8 * a + 8, at] = re
+                    early_ref[ch, 1, 8 * a : 8 * a + 8, at] = im
+                    if a + 1 < 2 * NRAD // 8:
+                        re, im = turn_by(re, im, step_re, step_im)
+            else:
+                for k, value in enumerate((re, im, step_re, step_im)):
+                    seed_ref[ch - early, k, :, at] = value
+
+    @pl.loop(0, early)
+    def _(ch):
+        make(ch, True)
+
+    @pl.loop(early, chunks)
+    def _(ch):
+        make(ch, False)
 
 
 def basis_call(freq_bins, codes, chunks):
@@ -208,10 +224,11 @@
     return pl.pallas_call(
         basis_kernel,
         in_specs=[SMEM, VMEM],
-        out_specs=[VMEM] * 2,
+        out_specs=[VMEM] * 3,
         out_shape=[
             jax.ShapeDtypeStruct((chunks, ORDERS, per), BF16),
-            jax.ShapeDtypeStruct((chunks, 4, 8, per), F32),
+            jax.ShapeDtypeStruct((3 * chunks // 8, 2, 2 * NRAD, per), F32),
+            jax.ShapeDtypeStruct((chunks - 3 * chunks // 8, 4, 8, per), F32),
         ],
         compiler_params=pltpu.CompilerParams(vmem_limit_bytes=12 << 20),
         name="basis",
@@ -220,20 +237,27 @@
 
 
 def solve_kernel(
-    recv_ref, azim_ref, seed_ref, out_ref, rad_ref, res_ref, image_ref, field_ref, onehot_ref, dir_ref, grown_ref, rows_ref, pick_ref
+    recv_ref, azim_ref, early_ref, seed_ref, out_ref, late_ref, res_ref, image_ref, field_ref, onehot_ref, dir_ref, grown_ref, rows_ref, pick_ref
 ):
     chunks, _, per = recv_ref.shape
     mics = chunks * per
     stack = 2 * NRAD
     odd = (iota((8, per), 0) & 1) == 1
+    early = early_ref.shape[0]
+
+    def rad(ch, c):
+        return early_ref[ch, c] if ch < early else late_ref[ch - early, c]
+
     for ch in range(chunks):
         for c in range(2):
             res_ref[ch, c] = jnp.where(odd, recv_ref[ch, 2 * c + 1 : 2 * c + 2, :], recv_ref[ch, 2 * c : 2 * c + 1, :])
 
-        re, im, step_re, step_im = (seed_ref[ch, k] for k in range(4))
+        if ch < early:
+            continue
+        re, im, step_re, step_im = (seed_ref[ch - early, k] for k in range(4))
         for a in range(stack // 8):
-            rad_ref[ch, 0, 8 * a : 8 * a + 8] = re
-            rad_ref[ch, 1, 8 * a : 8 * a + 8] = im
+            late_ref[ch - early, 0, 8 * a : 8 * a + 8] = re
+            late_ref[ch - early, 1, 8 * a : 8 * a + 8] = im
             if a + 1 < stack // 8:
                 re, im = turn_by(re, im, step_re, step_im)
 
@@ -277,7 +301,7 @@
         out = jnp.zeros((2 * stack, ORDERS), F32)
         for ch in range(chunks):
             re, im = advance(ch, 0)[None], advance(ch, 1)[None]
-            ec, es = groups(rad_ref[ch, 0]), groups(rad_ref[ch, 1])
+            ec, es = groups(rad(ch, 0)), groups(rad(ch, 1))
             field_ref[ch, 0:stack] = (re * ec + im * es).reshape(stack, per).astype(BF16)
             field_ref[ch, stack:] = (im * ec - re * es).reshape(stack, per).astype(BF16)
             out = out + nt_dot(field_ref[ch], azim_ref[ch])
@@ -296,7 +320,7 @@
         for ch in range(chunks):
             out = jnp.dot(rows_ref[...], azim_ref[ch], preferred_element_type=F32)
             t_re, t_im = out[:stack], out[stack:]
-            ec, es = rad_ref[ch, 0], rad_ref[ch, 1]
+            ec, es = rad(ch, 0), rad(ch, 1)
             i_re = periodic(jnp.sum(groups(ec * t_re - es * t_im), axis=0))
             i_im = periodic(jnp.sum(groups(ec * t_im + es * t_re), axis=0))
             image_ref[ch, 0] = i_re
@@ -370,16 +394,16 @@
                     out_ref[copy, ch, 2 * k + half] = packed
 
 
-def solve_call(recv, azim, seeds, copies):
+def solve_call(recv, azim, early, seeds, copies):
     chunks, _, per = recv.shape
     modes, stack = 2 * chunks * per, 2 * NRAD
     return pl.pallas_call(
         solve_kernel,
-        in_specs=[VMEM] * 3,
+        in_specs=[VMEM] * 4,
         out_specs=VMEM,
         out_shape=jax.ShapeDtypeStruct((copies, chunks, modes // chunks // 128 + 1, 4, 128), BF16),
         scratch_shapes=[
-            pltpu.VMEM((chunks, 2, stack, per), F32),
+            pltpu.VMEM((chunks - 3 * chunks // 8, 2, stack, per), F32),
             pltpu.VMEM((chunks, 2, 8, per), F32),
             pltpu.VMEM((chunks, 2, 8, per), F32),
             pltpu.VMEM((chunks, 2 * stack, per), BF16),
@@ -392,7 +416,7 @@
         compiler_params=pltpu.CompilerParams(vmem_limit_bytes=14 << 20),
         name="solve",
         cost_estimate=pl.CostEstimate(flops=10 * 256 * 4096 * 128, bytes_accessed=8 << 20, transcendentals=0),
-    )(recv, azim, seeds)
+    )(recv, azim, early, seeds)
 
 
 def expand_kernel(in_ref, amp_hbm, pow_hbm, res_hbm, wide_ref, ready_ref, pow_ref, res_ref, sems):
@@ -466,8 +490,8 @@
     codes = lax.all_to_all(codes_call(mic_azimuth, mic_axial, segs), "mic", 0, 0, tiled=True)
     spectra = spectra_call(freq_bins, mode_m, mode_n, signal[0], owners)
     recv = lax.all_to_all(spectra, "mode", 0, 0, tiled=True)
-    azim, seeds = basis_call(freq_bins, codes, owners)
-    slots = solve_call(recv, azim, seeds, segs)
+    azim, early, seeds = basis_call(freq_bins, codes, owners)
+    slots = solve_call(recv, azim, early, seeds, segs)
     shape = slots.shape
     slots = lax.all_to_all(slots.reshape(segs * owners, *shape[2:]), ("mic", "mode"), 0, 0, tiled=True)
     amplitude, power, residual = expand_call(slots.reshape(shape))

time: 61.9 us -> 61.7 us (level)
  no operation moved by 1% of the time
where the time goes in v9:
time: 61.7 us; the launch traced here: 61.4 us
  blocking collectives  25.3 us (41%)
  starting transfers between devices  15 us (24%)
  Pallas kernels  14.8 us (24%)
  waiting for transfers between devices  5.66 us (9%)
  between operations  0.68 us (1%)
    all_to_all x1, blocking collectives, on_device(): lax.all_to_all(slots.reshape(segs * owners, *shape[2:]), ('mic', 'mode'),...  25.3 us
    all_to_all x1, starting transfers between devices, on_device(): lax.all_to_all(codes_call(mic_azimuth, mic_axial, segs), 'mic', 0, 0, til...  8.6 us
    all_to_all x1, starting transfers between devices, on_device(): recv = lax.all_to_all(spectra, 'mode', 0, 0, tiled=True)  6.4 us
    pallas_call x1, Pallas kernels, solve_call(): pl.pallas_call(solve_kernel, in_specs=[VMEM] * 4, out_specs=VMEM, out_sha...  5.88 us
    pallas_call x1, Pallas kernels, spectra_call(): pl.pallas_call(spectra_kernel, in_specs=[HBM] * 4, out_specs=VMEM, out_sh...  4.25 us
    all_to_all x1, waiting for transfers between devices, on_device(): recv = lax.all_to_all(spectra, 'mode', 0, 0, tiled=True)  3.49 us
    all_to_all x1, waiting for transfers between devices, on_device(): lax.all_to_all(codes_call(mic_azimuth, mic_axial, segs), 'mic', 0, 0, til...  2.17 us
    pallas_call x1, Pallas kernels, basis_call(): pl.pallas_call(basis_kernel, in_specs=[SMEM, VMEM], out_specs=[VMEM] * 3,...  1.74 us
  transfers between devices with their start and end apart: 2, of which 2 were waited for; matrix products, arithmetic and copies ran while one was open for 0% of the time, Pallas kernels for 10%

profile of v9, /device:TPU:1, one launch (start us, length us, event | category | flops | bytes accessed | tf_op | source)
XLA Modules:
  0.0 61.4 jit_solution(11137139162454747945)
XLA Ops:
  0.6 1.3 %codes.1 = s32[16,1,256]{2,1,0:T(1,128)} custom-call(s32[1,256]{1,0:T(1,128)} %bitcast.14, s32[1,256]{1,0:T(1,128)} %bitcast.15), custom_call_target="tpu_custom_call" | custom-call | flops 1024 | bytes 16384 | tf_op jit(solution)/shard_map/codes/pallas_call | solution.py:75
  2.0 8.6 %all-to-all-start.1 = ((s32[16,1,256]{2,1,0:T(1,128)}), s32[16,1,256]{2,1,0:T(1,128)S(1)}, u32[]{:S(2)}, u32[]{:S(2)}) async-start(s32[16,1,256]{2,1,0:T(1,128)} %codes.1), calls=%async_computation.1 | async-start | bytes 32768 | tf_op jit(solution)/shard_map/all_to_all | solution.py:490
  10.6 0.0 copy-start
  10.6 4.3 %spectra.1 = f32[8,8,512]{2,1,0:T(8,128)} custom-call(s32[16]{0:T(128)} %freq_ref.1, s32[1,1024]{1,0:T(1,128)} %bitcast.12, s32[1,1024]{1,0:T(1,128)} %bitcast.13, bf16[512,4096]{1,0:T(8,128)(2,1)} %bitcast.11), custom_call_target="tpu_custom_call" | custom-call | flops 134217728 | bytes 4194304 | tf_op jit(solution)/shard_map/spectra/pallas_call | solution.py:149
  14.8 2.2 %all-to-all-done.1.code_ref = s32[16,1,256]{2,1,0:T(1,128)S(1)} async-done(((s32[16,1,256]{2,1,0:T(1,128)}), s32[16,1,256]{2,1,0:T(1,128)S(1)}, u32[]{:S(2)}, u32[]{:S(2)}) %all-to-all-start.1) | async-done | bytes 16416 | tf_op jit(solution)/shard_map/all_to_all | solution.py:490
  17.0 6.4 %all-to-all-start = ((f32[8,8,512]{2,1,0:T(8,128)}), f32[8,8,512]{2,1,0:T(8,128)S(1)}, u32[]{:S(2)}, u32[]{:S(2)}) async-start(f32[8,8,512]{2,1,0:T(8,128)} %spectra.1), calls=%async_computation | async-start | bytes 262144 | tf_op jit(solution)/shard_map/all_to_all | solution.py:492
  23.4 0.0 copy-done
  23.4 1.7 %basis.1 = (bf16[8,256,512]{2,1,0:T(8,128)(2,1)S(1)}, f32[3,2,64,512]{3,2,1,0:T(8,128)S(1)}, f32[5,4,8,512]{3,2,1,0:T(8,128)S(1)}) custom-call(s32[16]{0:T(128)S(1)} %copy-done, s32[16,1,256]{2,1,0:T(1,128)S(1)} %all-to-all-done.1.code_ref), custom_call_target="tpu_custom_call" | custom-call | flops 41943040 | bytes 3145728 | tf_op jit(solution)/shard_map/basis/pallas_call | solution.py:224
  25.2 3.5 %all-to-all-done.recv_ref = f32[8,8,512]{2,1,0:T(8,128)S(1)} async-done(((f32[8,8,512]{2,1,0:T(8,128)}), f32[8,8,512]{2,1,0:T(8,128)S(1)}, u32[]{:S(2)}, u32[]{:S(2)}) %all-to-all-start) | async-done | bytes 131104 | tf_op jit(solution)/shard_map/all_to_all | solution.py:492
  28.7 5.9 %solve.1 = bf16[16,8,9,4,128]{4,3,2,1,0:T(4,128)(2,1)S(1)} custom-call(f32[8,8,512]{2,1,0:T(8,128)S(1)} %all-to-all-done.recv_ref, bf16[8,256,512]{2,1,0:T(8,128)(2,1)S(1)} %get-tuple-element.9.azim_ref, f32[3,2,64,512]{3,2,1,0:T(8,128)S(1)} %get-tuple-element.10.early_ref, f32[5,4,8,512]{3,2,1,0:T(8,128)S(1)} %get-tuple-element.11.seed_ref), custom_call_target="tpu_custom_call" | custom-call | flops 1342177280 | bytes 8388608 | tf_op jit(solution)/shard_map/solve/pallas_call | solution.py:400
  34.5 25.3 %all_to_all.15 = bf16[128,9,4,128]{3,2,1,0:T(4,128)(2,1)S(1)} all-to-all(bf16[128,9,4,128]{3,2,1,0:T(4,128)(2,1)S(1)} %bitcast.10), channel_id=1, replica_groups=mesh['mic'=16,'mode'=8] {'mic','mode'}, dimensions={0} | all-to-all | bytes 2359296 | tf_op jit(solution)/shard_map/all_to_all | solution.py:496
  59.9 1.6 %expand.1 = (f32[32,16,1024]{2,1,0:T(8,128)}, f32[16,1024]{1,0:T(8,128)}, f32[4,16,256]{2,1,0:T(8,128)}) custom-call(bf16[16,8,9,4,128]{4,3,2,1,0:T(4,128)(2,1)S(1)} %bitcast.9), custom_call_target="tpu_custom_call" | custom-call | flops 2097152 | bytes 3145728 | tf_op jit(solution)/shard_map/expand/pallas_call | solution.py:463
Async XLA Ops:
  2.0 15.0 %all-to-all-start.1 = ((s32[16,1,256]{2,1,0:T(1,128)}), s32[16,1,256]{2,1,0:T(1,128)S(1)}, u32[]{:S(2)}, u32[]{:S(2)}) async-start(s32[16,1,256]{2,1,0:T(1,128)} %codes.1), calls=%async_computation.1 | async-start | bytes 32768 | tf_op jit(solution)/shard_map/all_to_all | solution.py:490
  10.6 12.8 %copy-start = (s32[16]{0:T(128)S(1)}, s32[16]{0:T(128)}, u32[]{:S(2)}) copy-start(s32[16]{0:T(128)} %freq_ref.1) | copy-start | bytes 196
  17.0 11.6 %all-to-all-start = ((f32[8,8,512]{2,1,0:T(8,128)}), f32[8,8,512]{2,1,0:T(8,128)S(1)}, u32[]{:S(2)}, u32[]{:S(2)}) async-start(f32[8,8,512]{2,1,0:T(8,128)} %spectra.1), calls=%async_computation | async-start | bytes 262144 | tf_op jit(solution)/shard_map/all_to_all | solution.py:492

commit v10 on v9

--- a/solution.py
+++ b/solution.py
@@ -425,10 +425,10 @@
     owner = lax.rem(2 * lax.axis_index("mode"), dests)
     for f in range(2):
         for s in range(segs):
-            wide_ref[1, f, 8 * s : 8 * s + rows, :] = in_ref[s, owner + f, lines].astype(F32)
+            wide_ref[3, f, 8 * s : 8 * s + rows, :] = in_ref[s, owner + f, lines].astype(F32)
         for half in range(2):
             for c in range(2):
-                value = wide_ref[1, f, pl.ds(2 * half + c, segs, stride=8), :]
+                value = wide_ref[3, f, pl.ds(2 * half + c, segs, stride=8), :]
                 res_ref[2 * f + c, :, half * 128 : (half + 1) * 128] = value
     copies = [pltpu.make_async_copy(res_ref, res_hbm, sems.at[2 * dests])]
     copies[-1].start()
@@ -436,13 +436,13 @@
         for s in range(segs):
             for kc in range(lines):
                 begin = 8 * s + rows * (kc % 2)
-                wide_ref[d % 2, kc // 2, begin : begin + rows, :] = in_ref[s, d, kc].astype(F32)
+                wide_ref[d % 4, kc // 2, begin : begin + rows, :] = in_ref[s, d, kc].astype(F32)
         for kc in range(lines):
             at = slice(kc * 128, (kc + 1) * 128)
             for fl in range(rows // 2):
                 power = jnp.zeros((segs, 128), F32)
                 for c in range(2):
-                    value = wide_ref[d % 2, kc // 2, pl.ds(rows * (kc % 2) + 2 * c + fl, segs, stride=8), :]
+                    value = wide_ref[d % 4, kc // 2, pl.ds(rows * (kc % 2) + 2 * c + fl, segs, stride=8), :]
                     ready_ref[d, fl, c, :, at] = value
                     power = power + value * value
                 f = d + fl * dests
@@ -470,7 +470,7 @@
             jax.ShapeDtypeStruct((rows, segs, 256), F32),
         ],
         scratch_shapes=[
-            pltpu.VMEM((2, (lines - 1) // 2, 8 * segs, 128), F32),
+            pltpu.VMEM((4, (lines - 1) // 2, 8 * segs, 128), F32),
             pltpu.VMEM((dests, rows // 2, 2, segs, modes), F32),
             pltpu.VMEM((dests * rows // 2, modes), F32),
             pltpu.VMEM((rows, segs, 256), F32),

time: 61.7 us -> 61.7 us (level)
  no operation moved by 1% of the time
where the time goes in v10:
time: 61.7 us; the launch traced here: 61.4 us
  blocking collectives  25.3 us (41%)
  starting transfers between devices  15 us (24%)
  Pallas kernels  14.8 us (24%)
  waiting for transfers between devices  5.66 us (9%)
  between operations  0.68 us (1%)
    all_to_all x1, blocking collectives, on_device(): lax.all_to_all(slots.reshape(segs * owners, *shape[2:]), ('mic', 'mode'),...  25.3 us
    all_to_all x1, starting transfers between devices, on_device(): lax.all_to_all(codes_call(mic_azimuth, mic_axial, segs), 'mic', 0, 0, til...  8.6 us
    all_to_all x1, starting transfers between devices, on_device(): recv = lax.all_to_all(spectra, 'mode', 0, 0, tiled=True)  6.4 us
    pallas_call x1, Pallas kernels, solve_call(): pl.pallas_call(solve_kernel, in_specs=[VMEM] * 4, out_specs=VMEM, out_sha...  5.88 us
    pallas_call x1, Pallas kernels, spectra_call(): pl.pallas_call(spectra_kernel, in_specs=[HBM] * 4, out_specs=VMEM, out_sh...  4.25 us
    all_to_all x1, waiting for transfers between devices, on_device(): recv = lax.all_to_all(spectra, 'mode', 0, 0, tiled=True)  3.49 us
    all_to_all x1, waiting for transfers between devices, on_device(): lax.all_to_all(codes_call(mic_azimuth, mic_axial, segs), 'mic', 0, 0, til...  2.17 us
    pallas_call x1, Pallas kernels, basis_call(): pl.pallas_call(basis_kernel, in_specs=[SMEM, VMEM], out_specs=[VMEM] * 3,...  1.74 us
  transfers between devices with their start and end apart: 2, of which 2 were waited for; matrix products, arithmetic and copies ran while one was open for 0% of the time, Pallas kernels for 10%

profile of v10, /device:TPU:1, one launch (start us, length us, event | category | flops | bytes accessed | tf_op | source)
XLA Modules:
  0.0 61.4 jit_solution(5830077713638256518)
XLA Ops:
  0.6 1.3 %codes.1 = s32[16,1,256]{2,1,0:T(1,128)} custom-call(s32[1,256]{1,0:T(1,128)} %bitcast.14, s32[1,256]{1,0:T(1,128)} %bitcast.15), custom_call_target="tpu_custom_call" | custom-call | flops 1024 | bytes 16384 | tf_op jit(solution)/shard_map/codes/pallas_call | solution.py:75
  2.0 8.6 %all-to-all-start.1 = ((s32[16,1,256]{2,1,0:T(1,128)}), s32[16,1,256]{2,1,0:T(1,128)S(1)}, u32[]{:S(2)}, u32[]{:S(2)}) async-start(s32[16,1,256]{2,1,0:T(1,128)} %codes.1), calls=%async_computation.1 | async-start | bytes 32768 | tf_op jit(solution)/shard_map/all_to_all | solution.py:490
  10.6 0.0 copy-start
  10.6 4.3 %spectra.1 = f32[8,8,512]{2,1,0:T(8,128)} custom-call(s32[16]{0:T(128)} %freq_ref.1, s32[1,1024]{1,0:T(1,128)} %bitcast.12, s32[1,1024]{1,0:T(1,128)} %bitcast.13, bf16[512,4096]{1,0:T(8,128)(2,1)} %bitcast.11), custom_call_target="tpu_custom_call" | custom-call | flops 134217728 | bytes 4194304 | tf_op jit(solution)/shard_map/spectra/pallas_call | solution.py:149
  14.8 2.2 %all-to-all-done.1.code_ref = s32[16,1,256]{2,1,0:T(1,128)S(1)} async-done(((s32[16,1,256]{2,1,0:T(1,128)}), s32[16,1,256]{2,1,0:T(1,128)S(1)}, u32[]{:S(2)}, u32[]{:S(2)}) %all-to-all-start.1) | async-done | bytes 16416 | tf_op jit(solution)/shard_map/all_to_all | solution.py:490
  17.0 6.4 %all-to-all-start = ((f32[8,8,512]{2,1,0:T(8,128)}), f32[8,8,512]{2,1,0:T(8,128)S(1)}, u32[]{:S(2)}, u32[]{:S(2)}) async-start(f32[8,8,512]{2,1,0:T(8,128)} %spectra.1), calls=%async_computation | async-start | bytes 262144 | tf_op jit(solution)/shard_map/all_to_all | solution.py:492
  23.4 0.0 copy-done
  23.4 1.7 %basis.1 = (bf16[8,256,512]{2,1,0:T(8,128)(2,1)S(1)}, f32[3,2,64,512]{3,2,1,0:T(8,128)S(1)}, f32[5,4,8,512]{3,2,1,0:T(8,128)S(1)}) custom-call(s32[16]{0:T(128)S(1)} %copy-done, s32[16,1,256]{2,1,0:T(1,128)S(1)} %all-to-all-done.1.code_ref), custom_call_target="tpu_custom_call" | custom-call | flops 41943040 | bytes 3145728 | tf_op jit(solution)/shard_map/basis/pallas_call | solution.py:224
  25.2 3.5 %all-to-all-done.recv_ref = f32[8,8,512]{2,1,0:T(8,128)S(1)} async-done(((f32[8,8,512]{2,1,0:T(8,128)}), f32[8,8,512]{2,1,0:T(8,128)S(1)}, u32[]{:S(2)}, u32[]{:S(2)}) %all-to-all-start) | async-done | bytes 131104 | tf_op jit(solution)/shard_map/all_to_all | solution.py:492
  28.7 5.9 %solve.1 = bf16[16,8,9,4,128]{4,3,2,1,0:T(4,128)(2,1)S(1)} custom-call(f32[8,8,512]{2,1,0:T(8,128)S(1)} %all-to-all-done.recv_ref, bf16[8,256,512]{2,1,0:T(8,128)(2,1)S(1)} %get-tuple-element.9.azim_ref, f32[3,2,64,512]{3,2,1,0:T(8,128)S(1)} %get-tuple-element.10.early_ref, f32[5,4,8,512]{3,2,1,0:T(8,128)S(1)} %get-tuple-element.11.seed_ref), custom_call_target="tpu_custom_call" | custom-call | flops 1342177280 | bytes 8388608 | tf_op jit(solution)/shard_map/solve/pallas_call | solution.py:400
  34.5 25.3 %all_to_all.15 = bf16[128,9,4,128]{3,2,1,0:T(4,128)(2,1)S(1)} all-to-all(bf16[128,9,4,128]{3,2,1,0:T(4,128)(2,1)S(1)} %bitcast.10), channel_id=1, replica_groups=mesh['mic'=16,'mode'=8] {'mic','mode'}, dimensions={0} | all-to-all | bytes 2359296 | tf_op jit(solution)/shard_map/all_to_all | solution.py:496
  59.9 1.6 %expand.1 = (f32[32,16,1024]{2,1,0:T(8,128)}, f32[16,1024]{1,0:T(8,128)}, f32[4,16,256]{2,1,0:T(8,128)}) custom-call(bf16[16,8,9,4,128]{4,3,2,1,0:T(4,128)(2,1)S(1)} %bitcast.9), custom_call_target="tpu_custom_call" | custom-call | flops 2097152 | bytes 3145728 | tf_op jit(solution)/shard_map/expand/pallas_call | solution.py:463
Async XLA Ops:
  2.0 15.0 %all-to-all-start.1 = ((s32[16,1,256]{2,1,0:T(1,128)}), s32[16,1,256]{2,1,0:T(1,128)S(1)}, u32[]{:S(2)}, u32[]{:S(2)}) async-start(s32[16,1,256]{2,1,0:T(1,128)} %codes.1), calls=%async_computation.1 | async-start | bytes 32768 | tf_op jit(solution)/shard_map/all_to_all | solution.py:490
  10.6 12.8 %copy-start = (s32[16]{0:T(128)S(1)}, s32[16]{0:T(128)}, u32[]{:S(2)}) copy-start(s32[16]{0:T(128)} %freq_ref.1) | copy-start | bytes 196
  17.0 11.6 %all-to-all-start = ((f32[8,8,512]{2,1,0:T(8,128)}), f32[8,8,512]{2,1,0:T(8,128)S(1)}, u32[]{:S(2)}, u32[]{:S(2)}) async-start(f32[8,8,512]{2,1,0:T(8,128)} %spectra.1), calls=%async_computation | async-start | bytes 262144 | tf_op jit(solution)/shard_map/all_to_all | solution.py:492
